TPU v7x, 256 devices: a whole 4x4x8 slice. The times are simulated.
256 devices in a mesh: pole: 16 (over z, core), row: 4 (over y), col: 4 (over x).
Axes of the slice: x: 4, y: 4, z: 8, core: 2. Of those that a mesh axis runs over, the one named last changes fastest.
Arguments:
- inverse_trail: bfloat16 [16, 1024, 2, 1024], P('pole', 'row', None, 'col'), may hold values from -6 to 6
- lower_t: bfloat16 [16, 2048, 2, 1024], P('pole', 'col', None, 'row'), may hold values from -0.125 to 0.125
- diag_inverse: bfloat16 [16, 2048, 2, 2048], P('pole', 'row', None, 'col'), may hold values from -6 to 6
- pole_weight: float32 [256, 2], replicated, may hold values from -4 to 4
- pole_slot: int32 [16], P('pole'), may hold values from 0 to 255
- pair_row: int32 [8192], replicated, may hold values from 0 to 383, as said below
- pair_col: int32 [8192], replicated, may hold values from 0 to 255, as said below
- projector: bfloat16 [8192, 64], P('pole'), may hold values from -6 to 6
Outputs:
- diag_block: bfloat16 [16, 2048, 2, 2048], P('pole', 'row', None, 'col')
- pair_density: float32 [8192, 128], P('pole')
Inputs may be any that keep to these rules, and one draw needn't show every extreme that they name: `pair_row`: pairs come in aligned blocks of 512, one block for each index of pole. A pair's grid cell is (a // (256 // size of row), b // (256 // size of col)) for a supernode row atom a and column atom b, and (b // (256 // size of row), (a - 256) // (128 // size of col)) otherwise. In every block at most 64 pairs share one grid cell, and some cell holds exactly 64. `pair_col`: drawn together with pair_row.
All inputs are finite; a program needn't handle non-finite values.
Results may differ from a plain program's by a relative error of at most 0.0038.
Values may be sent and summed in bfloat16 or wider, within the bound.
No kernel may reach another device: no remote copies, remote signals or barrier semaphores. Data moves between devices by JAX's collectives and lax.ppermute only.
A program may use at most 64 MiB of HBM per device.

v0:
```python
import jax
import jax.numpy as jnp
from jax import lax
from jax.sharding import Mesh
from jax.sharding import PartitionSpec as P

K = 2048
M = 1024
B = 8
KA = 256
POLE = ("pole_0", "pole_1")


def from_everyone(shard, axis):
    peers = lax.axis_size(axis)
    return lax.all_to_all(
        jnp.broadcast_to(shard[None], (peers, *shard.shape)), axis, 0, 0, tiled=True
    )


def in_order(parts, dim):
    parts = jnp.moveaxis(parts, 0, dim)
    dims = parts.shape
    return parts.reshape(*dims[:dim], dims[dim] * dims[dim + 1], *dims[dim + 2 :])


def gather_directly(shard, axis, dim):
    parts = from_everyone(shard, axis)
    return in_order(parts, dim)


def in_blocks(shard, dim, peers):
    dims = shard.shape
    parts = shard.reshape(*dims[:dim], peers, dims[dim] // peers, *dims[dim + 1 :])
    return jnp.moveaxis(parts, dim, 0)


def summed_on_arrival(shard, axis, dim):
    peers = lax.axis_size(axis)
    parts = lax.all_to_all(in_blocks(shard, dim, peers), axis, 0, 0, tiled=True)
    return jnp.sum(parts, axis=0)


def scatter_axes(shard, axes, dim):
    for axis in axes:
        shard = lax.psum_scatter(shard, axis, scatter_dimension=dim, tiled=True)
    return shard


def over_copies(shard, axis):
    everything = from_everyone(shard, axis)
    return jnp.sum(everything, axis=0)


def local(
    inverse_trail, lower_t, diag_inverse, pole_weight, pole_slot, pair_row, pair_col, projector
):
    trail = inverse_trail[0]
    lower = lower_t[0]
    inverse = diag_inverse[0]
    trail_rows = trail.shape[0]
    trail_cols = trail.shape[2]
    upper_half = trail.reshape(trail_rows, 2 * trail_cols)
    lower_half = jnp.concatenate([-trail[:, 1, :], trail[:, 0, :]], axis=1)
    trail_real = jnp.concatenate([upper_half, lower_half], axis=0)
    gathered = gather_directly(lower, "col", 0)
    flat_lower = gathered.reshape(gathered.shape[0], 2 * trail_rows)
    local_super = K // lax.axis_size("row")
    chosen = flat_lower
    coupling = summed_on_arrival(
        -jnp.dot(chosen, trail_real, preferred_element_type=jnp.float32), "row", 0
    )
    coupling = coupling.astype(jnp.bfloat16).reshape(local_super, 2, trail_cols)
    coupling_all = lax.all_gather(coupling, "col", axis=2, tiled=True)
    lower_all = lax.all_gather(lower, "row", axis=2, tiled=True)
    real_side = jnp.concatenate([lower_all[:, 0, :], -lower_all[:, 1, :]], axis=1)
    imag_side = jnp.concatenate([lower_all[:, 1, :], lower_all[:, 0, :]], axis=1)
    stacked = jnp.concatenate([real_side, imag_side], axis=0)
    coupling_flat = coupling_all.reshape(local_super, 2 * M)
    product = lax.dot_general(
        coupling_flat, stacked, (((1,), (1,)), ((), ())), preferred_element_type=jnp.float32
    )
    super_cols = lower.shape[0]
    product = product.reshape(local_super, 2, super_cols)
    block = (inverse.astype(jnp.float32) - product).astype(jnp.bfloat16)
    row_atoms = local_super // B
    col_atoms = super_cols // B
    trail_atoms = trail_cols // B
    table_super = (
        block.reshape(row_atoms, B, 2, col_atoms, B)
        .transpose(0, 3, 2, 1, 4)
        .reshape(row_atoms * col_atoms, 2 * B * B)
    )
    table_trail = (
        coupling.reshape(row_atoms, B, 2, trail_atoms, B)
        .transpose(3, 0, 2, 4, 1)
        .reshape(trail_atoms * row_atoms, 2 * B * B)
    )
    my_row = lax.axis_index("row")
    my_col = lax.axis_index("col")
    in_super = pair_row < KA
    super_here = in_super & (pair_row // row_atoms == my_row) & (pair_col // col_atoms == my_col)
    super_index = jnp.clip(
        (pair_row - my_row * row_atoms) * col_atoms + pair_col - my_col * col_atoms,
        0,
        row_atoms * col_atoms - 1,
    )
    trail_atom = pair_row - KA
    trail_here = (
        jnp.logical_not(in_super)
        & (pair_col // row_atoms == my_row)
        & (trail_atom // trail_atoms == my_col)
    )
    trail_index = jnp.clip(
        (trail_atom - my_col * trail_atoms) * row_atoms + pair_col - my_row * row_atoms,
        0,
        trail_atoms * row_atoms - 1,
    )
    from_super = jnp.take(table_super, super_index, axis=0).astype(jnp.float32)
    from_trail = jnp.take(table_trail, trail_index, axis=0).astype(jnp.float32)
    chosen = jnp.where(super_here[:, None], from_super, 0.0) + jnp.where(
        trail_here[:, None], from_trail, 0.0
    )
    pair_total = chosen.shape[0]
    chosen = chosen.reshape(pair_total, 2, B * B)
    weight_slot = pole_slot[0]
    selector = (jnp.arange(pole_weight.shape[0], dtype=jnp.int32) == weight_slot).astype(
        jnp.float32
    )
    weight = jnp.sum(selector[:, None] * pole_weight, axis=0)
    real_part = weight[0] * chosen[:, 0] - weight[1] * chosen[:, 1]
    imag_part = weight[0] * chosen[:, 1] + weight[1] * chosen[:, 0]
    pair_term = jnp.stack([real_part, imag_part], axis=1).reshape(pair_total, 2 * B * B)
    owner_part = scatter_axes(pair_term, POLE, 0)
    at_owner = over_copies(owner_part, ("row", "col"))
    owner_pairs = at_owner.shape[0]
    density = at_owner.reshape(owner_pairs, 2, B * B) * projector.astype(jnp.float32)[:, None, :]
    return (block[None], density.reshape(owner_pairs, 2 * B * B))


def solution(mesh):
    split = Mesh(
        mesh.devices.reshape(8, 2, mesh.shape["row"], mesh.shape["col"]),
        ("pole_0", "pole_1", "row", "col"),
    )
    in_specs = (
        P(POLE, "row", None, "col"),
        P(POLE, "col", None, "row"),
        P(POLE, "row", None, "col"),
        P(),
        P(POLE),
        P(),
        P(),
        P(POLE, None),
    )
    out_specs = (P(POLE, "row", None, "col"), P(POLE, None))
    return jax.shard_map(local, mesh=split, in_specs=in_specs, out_specs=out_specs, check_vma=False)
```

profile of v0, /device:TPU:1, one launch (start us, length us, event | category | flops | bytes accessed | tf_op | source)
XLA Modules:
  0.0 426.1 jit_solution(14345049404709254025)
XLA Ops:
  7.2 3.5 broadcast_in_dim.61
  10.6 5.0 %all-to-all-start = ((bf16[4,512,2,256]{3,2,1,0:T(2,128)(2,1)}), bf16[4,512,2,256]{3,2,1,0:T(2,128)(2,1)S(1)}, u32[]{:S(2)}, u32[]{:S(2)}) async-start(bf16[4,512,2,256]{3,2,1,0:T(2,128)(2,1)} %broadcast_in_dim.61), calls=%async_computation | async-start | bytes 4194304 | tf_op jit(solution)/shard_map/all_to_all | solution.py:16
  15.6 0.0 copy-done.4
  15.7 24.3 %all-to-all-done = bf16[4,512,2,256]{3,2,1,0:T(2,128)(2,1)S(1)} async-done(((bf16[4,512,2,256]{3,2,1,0:T(2,128)(2,1)}), bf16[4,512,2,256]{3,2,1,0:T(2,128)(2,1)S(1)}, u32[]{:S(2)}, u32[]{:S(2)}) %all-to-all-start) | async-done | bytes 2097184 | tf_op jit(solution)/shard_map/all_to_all | solution.py:16
  40.0 0.4 copy.63
  40.4 1.3 convolution_negate_fusion
  41.8 2.6 copy.67
  44.3 5.4 %all-to-all-start.1 = ((f32[4,512,512]{1,2,0:T(8,128)}), f32[4,512,512]{1,2,0:T(8,128)}, u32[]{:S(2)}, u32[]{:S(2)}) async-start(f32[4,512,512]{1,2,0:T(8,128)} %bitcast.57), calls=%async_computation.1 | async-start | bytes 8388608 | tf_op jit(solution)/shard_map/all_to_all | solution.py:40
  49.7 0.0 all-gather.6.cloned.1.call-start
  49.7 0.0 copy-done.3
  49.7 0.9 copy.49
  50.6 0.0 all-gather.6.cloned.1.call-update
  50.6 0.0 copy-start.8
  50.6 0.0 copy-start.5
  50.6 0.0 copy-start.6
  50.6 0.0 all-gather.4.cloned.1.call-start
  50.7 60.6 %all-to-all-done.1 = f32[4,512,512]{1,2,0:T(8,128)} async-done(((f32[4,512,512]{1,2,0:T(8,128)}), f32[4,512,512]{1,2,0:T(8,128)}, u32[]{:S(2)}, u32[]{:S(2)}) %all-to-all-start.1) | async-done | bytes 4194336 | tf_op jit(solution)/shard_map/all_to_all | solution.py:40
  111.3 2.7 reduce_sum.27
  114.0 1.1 copy.48
  115.1 0.0 all-gather.4.cloned.1.call-update
  115.2 0.0 reduce-scatter.3.cloned.1.call-start
  115.9 0.0 copy-done.8
  115.9 0.1 multiply_reduce_fusion
  116.0 0.7 fusion.17
  116.7 0.0 copy-done.5
  116.7 0.1 compare_and_fusion.2
  116.9 0.0 all-gather.6.cloned.1.call-done
  116.9 1.4 fusion.16
  118.3 0.5 copy-done
  118.8 0.2 slice_bitcast_fusion
  119.0 19.2 %maximum_maximum_fusion = bf16[1024,2048]{1,0:T(8,128)(2,1)} fusion(bf16[512,1024]{1,0:T(8,128)(2,1)S(1)} %get-tuple-element.13, bf16[512,1024]{1,0:T(8,128)(2,1)S(1)} %get-tuple-element.12, bf16[512,1024]{1,0:T(8,128)(2,1)S(1)} %fusion.16), kind=kLoop, calls=%fused_computation.3 | loop fusion | flops 16777216 | bytes 7340032 | tf_op jit(solution)/shard_map/concatenate | solution.py:78
  138.1 0.2 copy.53
  138.4 10.9 %convert_element_type.45 = bf16[64,8,2,32,8]{4,3,2,1,0:T(8,128)(2,1)} reshape(bf16[512,512]{1,0:T(8,128)(2,1)S(1)} %copy.53) | data formatting | bytes 1048576 | tf_op jit(solution)/shard_map/convert_element_type | solution.py:73
  149.2 11.8 %copy.54 = bf16[32,64,2,8,8]{1,0,4,3,2:T(8,128)(2,1)S(1)} copy(bf16[32,64,2,8,8]{3,0,2,4,1:T(8,128)(2,1)} %bitcast.56) | data formatting | bytes 1048576 | tf_op jit(solution)/shard_map/transpose | solution.py:96
  161.0 0.8 reshape.81
  161.8 0.3 copy.55
  162.1 24.0 %gather_fusion.1 = bf16[8192,128]{1,0:T(8,128)(2,1)S(1)} fusion(bf16[2048,128]{1,0:T(8,128)(2,1)S(1)} %copy.55, s32[8192]{0:T(1024)S(1)} %get-tuple-element.21), kind=kCustom, calls=%fused_computation.1 | custom fusion | bytes 4227072 | tf_op jit(solution)/shard_map/jit(_take)/gather | solution.py:120
  186.1 3.0 copy.56
  189.1 3.3 reshape.103
  192.4 4.9 %fusion = bf16[512,2,512]{2,0,1:T(8,128)(2,1)S(1)} fusion(bf16[512,2048,1]{1,0,2:T(8,128)(2,1)S(1)} %reshape.103, bf16[2,512,2048]{2,1,0:T(8,128)(2,1)} %bitcast.67, bf16[1,512,2,512]{3,2,1,0:T(2,128)(2,1)} %param.10), kind=kOutput, calls=%fused_computation.8 | convolution fusion | flops 2149056512 | bytes 8388608 | tf_op jit(solution)/shard_map/dot_general | solution.py:80
  197.3 0.0 copy-start.1
  197.3 20.7 %reshape.79 = bf16[64,8,2,64,8]{4,3,1,0,2:T(8,128)(2,1)} reshape(bf16[512,2,512]{2,0,1:T(8,128)(2,1)S(1)} %fusion) | data formatting | bytes 2097152 | tf_op jit(solution)/shard_map/reshape | solution.py:90
  217.9 14.0 %copy.50 = bf16[64,64,2,8,8]{1,0,4,3,2:T(8,128)(2,1)S(1)} copy(bf16[64,64,2,8,8]{4,1,3,0,2:T(8,128)(2,1)} %bitcast.55) | data formatting | bytes 2097152 | tf_op jit(solution)/shard_map/transpose | solution.py:91
  231.9 1.7 reshape.80
  233.6 0.7 copy.51
  234.3 24.0 %gather_fusion = bf16[8192,128]{1,0:T(8,128)(2,1)S(1)} fusion(bf16[4096,128]{1,0:T(8,128)(2,1)S(1)} %copy.51, s32[8192]{0:T(1024)S(1)} %get-tuple-element.20), kind=kCustom, calls=%fused_computation | custom fusion | bytes 4227072 | tf_op jit(solution)/shard_map/jit(_take)/gather | solution.py:119
  258.4 3.0 copy.52
  261.3 3.3 select_add_fusion
  264.6 1.9 multiply_subtract_fusion
  266.5 2.3 pad_maximum_fusion
  268.8 0.0 reduce-scatter.3.cloned.1.call-update
  268.9 0.0 reduce-scatter.5.cloned.1.call-start
  268.9 59.6 %reduce-scatter.3.cloned.1.call-done = f32[1024,128]{0,1:T(8,128)} async-done(((f32[8192,128]{0,1:T(8,128)}), f32[1024,128]{0,1:T(8,128)}) %reduce-scatter.3.cloned.1.call-update) | async-done | bytes 524304 | tf_op jit(solution)/shard_map/reduce_scatter | solution.py:46
  328.5 0.0 reduce-scatter.5.cloned.1.call-update
  328.5 15.0 %reduce-scatter.5.cloned.1.call-done = f32[512,128]{0,1:T(8,128)} async-done(((f32[1024,128]{0,1:T(8,128)}), f32[512,128]{0,1:T(8,128)}) %reduce-scatter.5.cloned.1.call-update) | async-done | bytes 262160 | tf_op jit(solution)/shard_map/reduce_scatter | solution.py:46
  343.5 1.1 copy.57
  344.6 2.4 broadcast_in_dim.71
  347.0 6.4 %all-to-all-start.2 = ((f32[16,512,128]{2,1,0:T(8,128)}), f32[16,512,128]{2,1,0:T(8,128)}, u32[]{:S(2)}, u32[]{:S(2)}) async-start(f32[16,512,128]{2,1,0:T(8,128)} %broadcast_in_dim.71), calls=%async_computation.4 | async-start | bytes 8388608 | tf_op jit(solution)/shard_map/all_to_all | solution.py:16
  353.4 0.0 copy-done.7
  353.5 0.1 copy.58
  353.6 2.0 copy.59
  355.6 60.8 %all-to-all-done.2 = f32[16,512,128]{2,1,0:T(8,128)} async-done(((f32[16,512,128]{2,1,0:T(8,128)}), f32[16,512,128]{2,1,0:T(8,128)}, u32[]{:S(2)}, u32[]{:S(2)}) %all-to-all-start.2) | async-done | bytes 4194336 | tf_op jit(solution)/shard_map/all_to_all | solution.py:16
  416.4 2.4 reduce_sum.29
  418.8 0.7 mul.74
  (15 shorter events, 0.2 us)
Async XLA Ops:
  10.6 5.0 %copy-start.4 = (bf16[1,256,2,256]{3,2,1,0:T(2,128)(2,1)S(1)}, bf16[1,256,2,256]{3,2,1,0:T(2,128)(2,1)}, u32[]{:S(2)}) copy-start(bf16[1,256,2,256]{3,2,1,0:T(2,128)(2,1)} %param.8) | copy-start | bytes 786436
  10.6 29.4 %all-to-all-start = ((bf16[4,512,2,256]{3,2,1,0:T(2,128)(2,1)}), bf16[4,512,2,256]{3,2,1,0:T(2,128)(2,1)S(1)}, u32[]{:S(2)}, u32[]{:S(2)}) async-start(bf16[4,512,2,256]{3,2,1,0:T(2,128)(2,1)} %broadcast_in_dim.61), calls=%async_computation | async-start | bytes 4194304 | tf_op jit(solution)/shard_map/all_to_all | solution.py:16
  44.3 5.4 %copy-start.3 = (bf16[1,512,2,256]{3,2,1,0:T(2,128)(2,1)S(1)}, bf16[1,512,2,256]{3,2,1,0:T(2,128)(2,1)}, u32[]{:S(2)}) copy-start(bf16[1,512,2,256]{3,2,1,0:T(2,128)(2,1)} %param.9) | copy-start | bytes 1572868
  44.3 67.0 %all-to-all-start.1 = ((f32[4,512,512]{1,2,0:T(8,128)}), f32[4,512,512]{1,2,0:T(8,128)}, u32[]{:S(2)}, u32[]{:S(2)}) async-start(f32[4,512,512]{1,2,0:T(8,128)} %bitcast.57), calls=%async_computation.1 | async-start | bytes 8388608 | tf_op jit(solution)/shard_map/all_to_all | solution.py:40
  49.7 67.2 %all-gather.6.cloned.1.call-start = ((), (), s32[]{:S(2)}) async-start(), calls=%async_computation.8 | async-start | bytes 2621440 | tf_op jit(solution)/shard_map/all_gather | solution.py:75
  50.6 65.3 %copy-start.8 = (f32[256,2]{0,1:T(2,128)S(1)}, f32[256,2]{0,1:T(2,128)}, u32[]{:S(2)}) copy-start(f32[256,2]{0,1:T(2,128)} %param.11) | copy-start | bytes 6148
  50.6 66.1 %copy-start.5 = (s32[8192]{0:T(1024)S(1)}, s32[8192]{0:T(1024)}, u32[]{:S(2)}) copy-start(s32[8192]{0:T(1024)} %param.14) | copy-start | bytes 98308
  50.6 66.1 %copy-start.6 = (s32[8192]{0:T(1024)S(1)}, s32[8192]{0:T(1024)}, u32[]{:S(2)}) copy-start(s32[8192]{0:T(1024)} %param.13) | copy-start | bytes 98308
  50.6 138.5 %all-gather.4.cloned.1.call-start = ((), (), s32[]{:S(2)}) async-start(), calls=%async_computation.5 | async-start | bytes 2621440 | tf_op jit(solution)/shard_map/all_gather | solution.py:74
  115.2 213.3 %reduce-scatter.3.cloned.1.call-start = ((), (), s32[]{:S(2)}) async-start(), calls=%async_computation.6 | async-start | bytes 4718592 | tf_op jit(solution)/shard_map/reduce_scatter | solution.py:46
  116.9 1.9 copy-start
  197.3 20.7 %copy-start.1 = (bf16[512,2,512]{2,0,1:T(8,128)(2,1)}, bf16[512,2,512]{2,0,1:T(8,128)(2,1)S(1)}, u32[]{:S(2)}) copy-start(bf16[512,2,512]{2,0,1:T(8,128)(2,1)S(1)} %fusion) | copy-start | bytes 3145732
  268.9 74.6 %reduce-scatter.5.cloned.1.call-start = ((), (), s32[]{:S(2)}) async-start(), calls=%async_computation.7 | async-start | bytes 786432 | tf_op jit(solution)/shard_map/reduce_scatter | solution.py:46
  347.0 6.5 %copy-start.7 = (bf16[512,64]{0,1:T(8,128)(2,1)S(1)}, bf16[512,64]{0,1:T(8,128)(2,1)}, u32[]{:S(2)}) copy-start(bf16[512,64]{0,1:T(8,128)(2,1)} %param.15) | copy-start | bytes 196612
  347.0 6.6 %copy-start.2 = (bf16[512,2,512]{2,0,1:T(8,128)(2,1)S(1)}, bf16[512,2,512]{2,0,1:T(8,128)(2,1)}, u32[]{:S(2)}) copy-start(bf16[512,2,512]{2,0,1:T(8,128)(2,1)} %copy-done.1) | copy-start | bytes 3145732
  347.0 69.5 %all-to-all-start.2 = ((f32[16,512,128]{2,1,0:T(8,128)}), f32[16,512,128]{2,1,0:T(8,128)}, u32[]{:S(2)}, u32[]{:S(2)}) async-start(f32[16,512,128]{2,1,0:T(8,128)} %broadcast_in_dim.71), calls=%async_computation.4 | async-start | bytes 8388608 | tf_op jit(solution)/shard_map/all_to_all | solution.py:16
Sparse Core Ops, SparseCore 0:
  52.3 63.2 all-gather.5
  118.0 37.6 all-gather.3
  269.0 59.4 reduce-scatter.2
  330.9 12.5 reduce-scatter.4
where the time goes:
time: 427 us; the launch traced here: 426 us
  waiting for transfers between devices  220 us (52%)
  local copies, waits for them, and re-layouts  134 us (31%)
  other arithmetic  34.3 us (8%)
  starting transfers between devices  16.9 us (4%)
  between operations  14.7 us (3%)
  matrix products  6.16 us (1%)
    all_to_all x2, waiting for transfers between devices, from_everyone(): lax.all_to_all(jnp.broadcast_to(shard[None], (peers, *shard.shape)), axis...  85.1 us
    reduce_scatter x2, waiting for transfers between devices, scatter_axes(): shard = lax.psum_scatter(shard, axis, scatter_dimension=dim, tiled=True)  74.5 us
    all_to_all x1, waiting for transfers between devices, summed_on_arrival(): parts = lax.all_to_all(in_blocks(shard, dim, peers), axis, 0, 0, tiled=True)  60.6 us
    gather x2, local copies, waits for them, and re-layouts, local(): from_super = jnp.take(table_super, super_index, axis=0).astype(jnp.float32)  27 us
    gather x2, local copies, waits for them, and re-layouts, local(): from_trail = jnp.take(table_trail, trail_index, axis=0).astype(jnp.float32)  27 us
    reshape x1, local copies, waits for them, and re-layouts, local(): block.reshape(row_atoms, B, 2, col_atoms, B).transpose(0, 3, 2, 1, 4)  20.7 us
    concatenate x1, other arithmetic, local(): stacked = jnp.concatenate([real_side, imag_side], axis=0)  19.2 us
    transpose x1, local copies, waits for them, and re-layouts, local(): table_super = block.reshape(row_atoms, B, 2, col_atoms, B).transpose(0, 3...  14 us
  transfers between devices with their start and end apart: 7, of which 5 were waited for; matrix products, arithmetic and copies ran while one was open for 19% of the time, Pallas kernels for 0%

commit v1 on v0

v1 whole, which is shorter than its diff:
```python
import jax
import jax.numpy as jnp
from jax import lax
from jax.experimental import pallas as pl
from jax.experimental.pallas import tpu as pltpu
from jax.sharding import Mesh
from jax.sharding import PartitionSpec as P

B = 8
KA = 256
POLE = ("pole_0", "pole_1")
ROWS = 4
COLS = 4
SLOTS = 64
MIB = 1 << 20


def ring(shift, peers):
    return [(i, (i + shift) % peers) for i in range(peers)]


def to_process_rows(shift):
    return [
        (k * COLS + x, x * COLS + (k + shift) % COLS) for k in range(ROWS) for x in range(COLS)
    ]


def atoms_apart(raw):
    rows, _, columns = raw.shape
    return raw.reshape(rows // B, B, 2, columns).transpose(0, 2, 1, 3).reshape(2 * rows, columns)


def whole(shape):
    return pl.BlockSpec(shape, lambda *_: (0,) * len(shape))


def contract(left, right, dim):
    return lax.dot_general(
        left, right, (((1,), (dim,)), ((), ())), preferred_element_type=jnp.float32
    )


def coupling_kernel(base_ref, l0, l1, l2, l3, t_ref, c_ref, ct_ref):
    tile = c_ref.shape[0]
    columns = c_ref.shape[1]
    real = imag = None
    for d, left in enumerate((l0, l1, l2, l3)):
        e = (base_ref[0] + d) % ROWS
        u = contract(left[...], t_ref[e, 0], 0)
        v = contract(left[...], t_ref[e, 1], 0)
        real = u if real is None else real + u
        imag = v if imag is None else imag + v
    u = real.reshape(tile // 16, 2, 8, columns)
    v = imag.reshape(tile // 16, 2, 8, columns)
    re = v[:, 1] - u[:, 0]
    im = -(u[:, 1] + v[:, 0])
    c_ref[...] = jnp.stack([re, im], axis=1).reshape(tile, columns).astype(jnp.bfloat16)
    re_t = re.reshape(tile // 2, columns).T.reshape(columns // 8, 8, tile // 2)
    im_t = im.reshape(tile // 2, columns).T.reshape(columns // 8, 8, tile // 2)
    ct_ref[...] = (
        jnp.stack([re_t, im_t], axis=1).reshape(2 * columns, tile // 2).astype(jnp.bfloat16)
    )


def coupling_call(base, lefts, trail):
    rows, inner = lefts[0].shape
    columns = trail.shape[3]
    tile = 256
    left_spec = pl.BlockSpec((tile, inner), lambda i, *_: (i, 0))
    return pl.pallas_call(
        coupling_kernel,
        out_shape=(
            jax.ShapeDtypeStruct((rows, columns), jnp.bfloat16),
            jax.ShapeDtypeStruct((2 * columns, rows // 2), jnp.bfloat16),
        ),
        grid_spec=pltpu.PrefetchScalarGridSpec(
            num_scalar_prefetch=1,
            grid=(rows // tile,),
            in_specs=[left_spec] * 4 + [whole(trail.shape)],
            out_specs=(
                pl.BlockSpec((tile, columns), lambda i, *_: (i, 0)),
                pl.BlockSpec((2 * columns, tile // 2), lambda i, *_: (0, i)),
            ),
        ),
        cost_estimate=pl.CostEstimate(
            flops=2 * rows * inner * 8 * columns, bytes_accessed=6 << 20, transcendentals=0
        ),
        name="coupling",
    )(base, *lefts, trail)


def block_kernel(
    base_ref, codes_ref, c0, c1, c2, c3, l_ref, diag_ref, ct_ref, mask_ref, out_ref, pairs_ref,
    table, lanes, spread, keep, fold,
):
    rows, columns = diag_ref.shape
    step = pl.program_id(0)
    tile = c0.shape[0]

    @pl.when(step == 0)
    def _():
        table[rows : rows + ct_ref.shape[0], :] = ct_ref[...]
        lane = lax.broadcasted_iota(jnp.int32, (128, 128), 1)
        row = lax.broadcasted_iota(jnp.int32, (128, 128), 0)
        spread[...] = jnp.where(row % 8 == lane % 8, 1.0, 0.0).astype(jnp.bfloat16)
        row = lax.broadcasted_iota(jnp.int32, (16, 128), 0)
        lane = lax.broadcasted_iota(jnp.int32, (16, 128), 1)
        keep[...] = jnp.where(lane // 8 == row, 1.0, 0.0)
        row = lax.broadcasted_iota(jnp.int32, fold.shape, 0)
        lane = lax.broadcasted_iota(jnp.int32, fold.shape, 1)
        fold[...] = jnp.where(lane // 16 == row, 1.0, 0.0).astype(jnp.bfloat16)

    real = imag = None
    for d, left in enumerate((c0, c1, c2, c3)):
        e = (base_ref[0] + d) % ROWS
        u = contract(left[...], l_ref[e, 0], 1)
        v = contract(left[...], l_ref[e, 1], 1)
        real = u if real is None else real + u
        imag = v if imag is None else imag + v
    u = real.reshape(tile // 16, 2, 8, columns)
    v = imag.reshape(tile // 16, 2, 8, columns)
    start = pl.multiple_of(step * tile, tile)
    diag = diag_ref[pl.ds(start, tile), :].astype(jnp.float32).reshape(tile // 16, 2, 8, columns)
    re = diag[:, 0] - (u[:, 0] - v[:, 1])
    im = diag[:, 1] - (u[:, 1] + v[:, 0])
    block = jnp.stack([re, im], axis=1).reshape(tile, columns).astype(jnp.bfloat16)
    out_ref[...] = block
    table[pl.ds(start, tile), :] = block

    @pl.when(step == pl.num_programs(0) - 1)
    def _():
        @pl.loop(0, pairs_ref.shape[0] // SLOTS)
        def _(owner):
            first = owner * SLOTS
            for s in range(SLOTS):
                code = codes_ref[first + s]
                at = pl.multiple_of((code >> 6) * 16, 16)
                across = pl.multiple_of(((code >> 4) & 3) * 128, 128)
                found = table[pl.ds(at, 16), pl.ds(across, 128)]
                lanes[s * 16 : s * 16 + 16, :] = found * mask_ref[code & 15]
            wide = contract(lanes[...], spread[...], 0).reshape(SLOTS, 16, 128)
            wide = (wide * keep[...][None]).reshape(SLOTS * 16, 128).astype(jnp.bfloat16)
            pairs_ref[pl.ds(pl.multiple_of(first, SLOTS), SLOTS), :] = contract(
                fold[...], wide, 0
            ).astype(jnp.bfloat16)


def block_call(base, codes, couplings, lower, diag, coupling_t, masks):
    rows, columns = diag.shape
    inner = couplings[0].shape[1]
    slots = codes.shape[0]
    tile = 256
    return pl.pallas_call(
        block_kernel,
        out_shape=(
            jax.ShapeDtypeStruct((rows, columns), jnp.bfloat16),
            jax.ShapeDtypeStruct((slots, 2 * B * B), jnp.bfloat16),
        ),
        grid_spec=pltpu.PrefetchScalarGridSpec(
            num_scalar_prefetch=2,
            grid=(rows // tile,),
            in_specs=[pl.BlockSpec((tile, inner), lambda i, *_: (i, 0))] * 4
            + [whole(lower.shape), whole(diag.shape), whole(coupling_t.shape), whole(masks.shape)],
            out_specs=(
                pl.BlockSpec((tile, columns), lambda i, *_: (i, 0)),
                whole((slots, 2 * B * B)),
            ),
            scratch_shapes=[
                pltpu.VMEM((rows + coupling_t.shape[0], columns), jnp.bfloat16),
                pltpu.VMEM((SLOTS * 16, 128), jnp.bfloat16),
                pltpu.VMEM((128, 128), jnp.bfloat16),
                pltpu.VMEM((16, 128), jnp.float32),
                pltpu.VMEM((SLOTS, SLOTS * 16), jnp.bfloat16),
            ],
        ),
        compiler_params=pltpu.CompilerParams(vmem_limit_bytes=40 * MIB),
        cost_estimate=pl.CostEstimate(
            flops=2 * rows * inner * 8 * columns, bytes_accessed=12 << 20, transcendentals=0
        ),
        name="block_and_pairs",
    )(base, codes, *couplings, lower, diag, coupling_t, masks)


def pole_sum_kernel(weight_ref, parts_ref, out_ref):
    straight = crossed = None
    for p in range(parts_ref.shape[0]):
        part = parts_ref[p].astype(jnp.float32)
        a = weight_ref[p, 0] * part
        b = weight_ref[p, 1] * part
        straight = a if straight is None else straight + a
        crossed = b if crossed is None else crossed + b
    half = B * B
    lane = lax.broadcasted_iota(jnp.int32, crossed.shape, 1)
    crossed = pltpu.roll(crossed, half, 1)
    out_ref[...] = straight + jnp.where(lane < half, -crossed, crossed)


def pole_sum_call(weights, parts):
    return pl.pallas_call(
        pole_sum_kernel,
        out_shape=jax.ShapeDtypeStruct(parts.shape[1:], jnp.float32),
        in_specs=[pl.BlockSpec(memory_space=pltpu.SMEM), pl.BlockSpec(memory_space=pltpu.VMEM)],
        out_specs=pl.BlockSpec(memory_space=pltpu.VMEM),
        name="pole_sum",
    )(weights, parts)


def density_kernel(index_ref, sums_ref, projector_ref, out_ref):
    @pl.loop(0, out_ref.shape[0] // 16)
    def _(group):
        first = pl.multiple_of(group * 16, 16)
        for s in range(16):
            q = first + s
            out_ref[pl.ds(q, 1), :] = sums_ref[pl.ds(index_ref[q], 1), :]
        here = pl.ds(first, 16)
        out_ref[here, :] = out_ref[here, :] * projector_ref[here, :]


def density_call(index, sums, projector):
    return pl.pallas_call(
        density_kernel,
        out_shape=jax.ShapeDtypeStruct(projector.shape, jnp.float32),
        in_specs=[pl.BlockSpec(memory_space=pltpu.SMEM)]
        + [pl.BlockSpec(memory_space=pltpu.VMEM)] * 2,
        out_specs=pl.BlockSpec(memory_space=pltpu.VMEM),
        name="density",
    )(index, sums, projector)


def pair_tables(pair_row, pair_col, row, col, pole, owners):
    row_atoms, col_atoms, trail_atoms = KA // ROWS, KA // COLS, 128 // COLS
    a = pair_row.reshape(owners, -1)
    b = pair_col.reshape(owners, -1)
    in_super = a < KA
    trail = a - KA
    cell = jnp.where(
        in_super,
        (a // row_atoms) * COLS + b // col_atoms,
        (b // row_atoms) * COLS + trail // trail_atoms,
    )
    code = jnp.where(
        in_super,
        (a % row_atoms) * col_atoms + b % col_atoms,
        (row_atoms + trail % trail_atoms) * col_atoms + b % row_atoms,
    )
    pairs = a.shape[1]
    place = jnp.arange(pairs, dtype=jnp.int32)
    earlier = place[:, None] < place[None, :]
    mine = cell == row * COLS + col
    rank = jnp.dot(
        mine.astype(jnp.bfloat16),
        earlier.astype(jnp.bfloat16),
        preferred_element_type=jnp.float32,
    ).astype(jnp.int32)
    slot = jnp.where(mine, rank, -1)
    hit = slot[:, None, :] == jnp.arange(SLOTS, dtype=jnp.int32)[None, :, None]
    codes = jnp.sum(jnp.where(hit, code[:, None, :], 0), axis=2).reshape(owners * SLOTS)
    own_cell = lax.dynamic_index_in_dim(cell, pole, 0, keepdims=False)
    same = (own_cell[:, None] == own_cell[None, :]) & earlier
    index = own_cell * SLOTS + jnp.sum(same.astype(jnp.int32), axis=0)
    return codes, index


def local(
    inverse_trail, lower_t, diag_inverse, pole_weight, pole_slot, pair_row, pair_col, projector
):
    row = lax.axis_index("row")
    col = lax.axis_index("col")
    pole = lax.axis_index(POLE)
    poles = lax.axis_size(POLE)
    base = ((row - col + COLS) % COLS).astype(jnp.int32).reshape(1)

    trail = inverse_trail[0]
    lower = lower_t[0]

    trails = [trail] + [lax.ppermute(trail, "row", ring(e, ROWS)) for e in range(1, ROWS)]
    lefts = [lax.ppermute(lower, ("row", "col"), to_process_rows(d)) for d in range(COLS)]

    slots = lax.all_gather(pole_slot, POLE, axis=0, tiled=True)
    chosen = slots[:, None] == jnp.arange(pole_weight.shape[0], dtype=jnp.int32)[None, :]
    weights = jnp.sum(jnp.where(chosen[:, :, None], pole_weight[None], 0.0), axis=1)
    codes, index = pair_tables(pair_row, pair_col, row, col, pole, poles)
    diag = atoms_apart(diag_inverse[0])
    wide_projector = jnp.concatenate([projector, projector], axis=1).astype(jnp.float32)
    masks = (
        jnp.arange(16, dtype=jnp.int32)[:, None, None]
        == jnp.broadcast_to(jnp.arange(128, dtype=jnp.int32) // B, (16, 128))[None]
    ).astype(jnp.bfloat16)

    trail_all = jnp.stack([t.transpose(1, 0, 2) for t in trails])
    coupling, coupling_t = coupling_call(base, [atoms_apart(left) for left in lefts], trail_all)

    lower_late, _ = lax.optimization_barrier((lower, lefts))
    couplings = [coupling] + [
        lax.ppermute(coupling, "col", ring(d, COLS)) for d in range(1, COLS)
    ]
    lowers = [lower] + [lax.ppermute(lower_late, "row", ring(e, ROWS)) for e in range(1, ROWS)]
    lower_all = jnp.stack([x.transpose(1, 0, 2) for x in lowers])

    block, pairs = block_call(base, codes, couplings, lower_all, diag, coupling_t, masks)
    super_rows = block.shape[0] // 2
    out = (
        block.reshape(super_rows // B, 2, B, block.shape[1])
        .transpose(0, 2, 1, 3)
        .reshape(1, super_rows, 2, block.shape[1])
    )

    parts = lax.all_to_all(pairs.reshape(poles, SLOTS, 2 * B * B), POLE, 0, 0, tiled=True)
    summed = pole_sum_call(weights, parts)
    cells = ROWS * COLS
    everywhere = lax.all_to_all(
        jnp.broadcast_to(summed[None], (cells, *summed.shape)), ("row", "col"), 0, 0, tiled=True
    )
    density = density_call(index, everywhere.reshape(cells * SLOTS, 2 * B * B), wide_projector)
    return (out, density)


def solution(mesh):
    split = Mesh(
        mesh.devices.reshape(8, 2, mesh.shape["row"], mesh.shape["col"]),
        ("pole_0", "pole_1", "row", "col"),
    )
    in_specs = (
        P(POLE, "row", None, "col"),
        P(POLE, "col", None, "row"),
        P(POLE, "row", None, "col"),
        P(),
        P(POLE),
        P(),
        P(),
        P(POLE, None),
    )
    out_specs = (P(POLE, "row", None, "col"), P(POLE, None))
    return jax.shard_map(local, mesh=split, in_specs=in_specs, out_specs=out_specs, check_vma=False)
```

time: 427 us -> 167 us (0.39)
  waiting for transfers between devices: 220 us -> 34.9 us
  local copies, waits for them, and re-layouts: 134 us -> 16.8 us
  starting transfers between devices: 16.9 us -> 68.6 us
  other arithmetic: 34.3 us -> 6.08 us
  Pallas kernels: 0 us -> 24.4 us
  between operations: 14.7 us -> 1.51 us
  blocking collectives: 0 us -> 12.4 us
  matrix products: 6.16 us -> 0.18 us
    all_to_all x3 -> x2, waiting for transfers between devices: 146 us -> 5.5 us  [the longest x1 5.5 us: local(): lax.all_to_all(jnp.broadcast_to(summed[None], (cells, *summed.shape)), ('...]
    reduce_scatter x2 -> x0, waiting for transfers between devices: 74.5 us -> none  [scatter_axes(): shard = lax.psum_scatter(shard, axis, scatter_dimension=dim, tiled=True)]
    gather x4 -> x0, local copies, waits for them, and re-layouts: 54 us -> none  [the longest x2 27 us: local(): from_super = jnp.take(table_super, super_index, axis=0).astype(jnp.float32)]
    ppermute x0 -> x13, starting transfers between devices: none -> 53.3 us  [the longest x3 17.1 us: local(): lax.ppermute(lower_late, 'row', ring(e, ROWS))]
    ppermute x0 -> x13, waiting for transfers between devices: none -> 29.4 us  [the longest x3 19.3 us: local(): lax.ppermute(coupling, 'col', ring(d, COLS))]
    reshape x7 -> x3, local copies, waits for them, and re-layouts: 29.9 us -> 1.6 us  [the longest x1 0.76 us: pair_tables(): a = pair_row.reshape(owners, -1)]
    pallas_call x0 -> x4, Pallas kernels: none -> 24.4 us  [the longest x1 15.2 us: block_call(): pl.pallas_call(block_kernel, out_shape=(jax.ShapeDtypeStruct((rows, colum...]
    concatenate x1 -> x0, other arithmetic: 19.2 us -> none  [local(): stacked = jnp.concatenate([real_side, imag_side], axis=0)]
  transfers between devices with their start and end apart: 7 -> 15, of which waited for: 5 -> 3; matrix products, arithmetic and copies ran while one was open for 19% -> 11% of each run, Pallas kernels for 0% -> 3%
where the time goes in v1:
time: 167 us; the launch traced here: 165 us
  starting transfers between devices  68.6 us (41%)
  waiting for transfers between devices  34.9 us (21%)
  Pallas kernels  24.4 us (15%)
  local copies, waits for them, and re-layouts  16.8 us (10%)
  blocking collectives  12.4 us (7%)
  other arithmetic  6.08 us (4%)
    ppermute x3, waiting for transfers between devices, local(): lax.ppermute(coupling, 'col', ring(d, COLS))  19.3 us
    ppermute x3, starting transfers between devices, local(): lax.ppermute(lower_late, 'row', ring(e, ROWS))  17.1 us
    pallas_call x1, Pallas kernels, block_call(): pl.pallas_call(block_kernel, out_shape=(jax.ShapeDtypeStruct((rows, colum...  15.2 us
    ppermute x3, starting transfers between devices, local(): lax.ppermute(trail, 'row', ring(e, ROWS))  14.1 us
    ppermute x3, starting transfers between devices, local(): lax.ppermute(coupling, 'col', ring(d, COLS))  13.2 us
    unnamed x1, blocking collectives  12.4 us
    ppermute x4, waiting for transfers between devices, local(): lax.ppermute(lower, ('row', 'col'), to_process_rows(d))  10.1 us
    all_to_all x1, starting transfers between devices, local(): lax.all_to_all(pairs.reshape(poles, SLOTS, 2 * B * B), POLE, 0, 0, tiled=...  9.73 us
  transfers between devices with their start and end apart: 15, of which 3 were waited for; matrix products, arithmetic and copies ran while one was open for 11% of the time, Pallas kernels for 3%

profile of v1, /device:TPU:1, one launch (start us, length us, event | category | flops | bytes accessed | tf_op | source)
XLA Modules:
  0.0 164.9 jit_solution(10146914646071162029)
XLA Ops:
  0.6 1.2 copy.36
  1.8 3.7 %collective-permute-start.2 = (bf16[512,2,256]{2,0,1:T(8,128)(2,1)S(1)}, bf16[512,2,256]{2,0,1:T(8,128)(2,1)S(1)}, u32[]{:S(2)}, u32[]{:S(2)}) collective-permute-start(bf16[512,2,256]{2,0,1:T(8,128)(2,1)S(1)} %bitcast.66), channel_id=1, source_target_pairs={{0,2},{1,6},{2,10},{3,14},{4,3},{5,7},{6,11},{7,15},{8,0},{9,4},{1... | collective-permute-start | bytes 1572872 | tf_op jit(solution)/shard_map/ppermute | solution.py:277
  5.5 2.7 %collective-permute-start.3 = (bf16[512,2,256]{2,0,1:T(8,128)(2,1)S(1)}, bf16[512,2,256]{2,0,1:T(8,128)(2,1)S(1)}, u32[]{:S(2)}, u32[]{:S(2)}) collective-permute-start(bf16[512,2,256]{2,0,1:T(8,128)(2,1)S(1)} %bitcast.67), channel_id=1, source_target_pairs={{0,3},{1,7},{2,11},{3,15},{4,0},{5,4},{6,8},{7,12},{8,1},{9,5},{10... | collective-permute-start | bytes 1572872 | tf_op jit(solution)/shard_map/ppermute | solution.py:277
  8.2 1.4 collective-permute-start
  9.7 1.2 collective-permute-start.1
  10.8 1.0 copy.37
  11.8 4.0 %collective-permute-start.4 = (bf16[256,2,256]{2,0,1:T(8,128)(2,1)S(1)}, bf16[256,2,256]{2,0,1:T(8,128)(2,1)S(1)}, u32[]{:S(2)}, u32[]{:S(2)}) collective-permute-start(bf16[256,2,256]{2,0,1:T(8,128)(2,1)S(1)} %bitcast.76), channel_id=1, source_target_pairs={{0,4},{4,8},{8,12},{12,0},{1,5},{5,9},{9,13},{13,1},{2,6},{6,10},{... | collective-permute-start | bytes 786440 | tf_op jit(solution)/shard_map/ppermute | solution.py:276
  15.8 0.8 reshape.149
  16.5 0.8 reshape.150
  17.3 0.1 fusion.5
  17.4 0.0 collective-permute-done.2
  17.4 3.2 %collective-permute-start.5 = (bf16[256,2,256]{2,0,1:T(8,128)(2,1)S(1)}, bf16[256,2,256]{2,0,1:T(8,128)(2,1)}, u32[]{:S(2)}, u32[]{:S(2)}) collective-permute-start(bf16[256,2,256]{2,0,1:T(8,128)(2,1)S(1)} %bitcast.77), channel_id=1, source_target_pairs={{0,8},{4,12},{8,0},{12,4},{1,9},{5,13},{9,1},{13,5},{2,10},{6,14},... | collective-permute-start | bytes 786440 | tf_op jit(solution)/shard_map/ppermute | solution.py:276
  20.7 10.0 %collective-permute-done.3 = bf16[512,2,256]{2,0,1:T(8,128)(2,1)S(1)} collective-permute-done((bf16[512,2,256]{2,0,1:T(8,128)(2,1)S(1)}, bf16[512,2,256]{2,0,1:T(8,128)(2,1)S(1)}, u32[]{:S(2)}, u32[]{:S(2)}) %collective-permute-start.3) | collective-permute-done | bytes 524320 | tf_op jit(solution)/shard_map/ppermute | solution.py:277
  30.7 6.8 %collective-permute-start.6 = (bf16[256,2,256]{2,0,1:T(8,128)(2,1)S(1)}, bf16[256,2,256]{2,0,1:T(8,128)(2,1)}, u32[]{:S(2)}, u32[]{:S(2)}) collective-permute-start(bf16[256,2,256]{2,0,1:T(8,128)(2,1)S(1)} %bitcast.78), channel_id=1, source_target_pairs={{0,12},{4,0},{8,4},{12,8},{1,13},{5,1},{9,5},{13,9},{2,14},{6,2},{... | collective-permute-start | bytes 786440 | tf_op jit(solution)/shard_map/ppermute | solution.py:276
  37.6 0.0 collective-permute-done
  37.6 0.0 collective-permute-done.1
  37.6 14.6 %collective-permute-start.10 = (bf16[512,2,256]{2,0,1:T(8,128)(2,1)S(1)}, bf16[512,2,256]{2,0,1:T(8,128)(2,1)}, u32[]{:S(2)}, u32[]{:S(2)}) collective-permute-start(bf16[512,2,256]{2,0,1:T(8,128)(2,1)S(1)} %bitcast.70), channel_id=1, source_target_pairs={{0,4},{4,8},{8,12},{12,0},{1,5},{5,9},{9,13},{13,1},{2,6},{6,10},{... | collective-permute-start | bytes 1572872 | tf_op jit(solution)/shard_map/ppermute | solution.py:297
  52.2 0.2 fusion
  52.4 0.4 select_reduce_fusion
  52.7 0.1 reshape.151.codes_ref
  52.8 0.2 copy.27
  53.1 0.1 collective-permute-start.11
  53.2 0.0 collective-permute-done.4
  53.2 2.4 %collective-permute-start.12 = (bf16[512,2,256]{2,0,1:T(8,128)(2,1)S(1)}, bf16[512,2,256]{2,0,1:T(8,128)(2,1)}, u32[]{:S(2)}, u32[]{:S(2)}) collective-permute-start(bf16[512,2,256]{2,0,1:T(8,128)(2,1)S(1)} %bitcast.72), channel_id=1, source_target_pairs={{0,12},{4,0},{8,4},{12,8},{1,13},{5,1},{9,5},{13,9},{2,14},{6,2},{... | collective-permute-start | bytes 1572872 | tf_op jit(solution)/shard_map/ppermute | solution.py:297
  55.6 0.0 collective-permute-done.5
  55.6 0.0 collective-permute-done.6
  55.6 2.1 %pad_maximum_fusion.1.t_ref = bf16[4,2,256,256]{3,2,1,0:T(8,128)(2,1)} fusion(bf16[1,2,256,256]{3,2,1,0:T(8,128)(2,1)} %bitcast.22, bf16[1,2,256,256]{3,2,1,0:T(8,128)(2,1)} %bitcast.20, bf16[1,2,256,256]{3,2,1,0:T(8,128)(2,1)S(1)} %bitcast.86, bf16[1,2,256,256]{3,2,1,0:T(8,128)(2,1)S(1)} %bitcast.79), kind=kLoop, calls=%fused_computation.5 | loop fusion | flops 1572864 | bytes 2097152 | tf_op jit(solution)/shard_map/stack | solution.py:290
  57.7 0.8 copy.24
  58.5 0.8 copy.25
  59.4 1.9 %copy.22 = bf16[64,2,8,256]{3,2,1,0:T(8,128)(2,1)} copy(bf16[64,2,8,256]{3,2,0,1:T(8,128)(2,1)} %bitcast.3) | data formatting | bytes 1048576 | tf_op jit(solution)/shard_map/transpose | solution.py:30
  61.2 1.9 %copy.23 = bf16[64,2,8,256]{3,2,1,0:T(8,128)(2,1)} copy(bf16[64,2,8,256]{3,2,0,1:T(8,128)(2,1)} %bitcast.6) | data formatting | bytes 1048576 | tf_op jit(solution)/shard_map/transpose | solution.py:30
  63.1 5.0 %coupling.1 = (bf16[1024,256]{1,0:T(8,128)(2,1)}, bf16[512,512]{1,0:T(8,128)(2,1)}) custom-call(s32[1]{0:T(128)} %bitcast.base_ref, bf16[1024,256]{1,0:T(8,128)(2,1)} %bitcast.84, bf16[1024,256]{1,0:T(8,128)(2,1)} %bitcast.85, bf16[1024,256]{1,0:T(8,128)(2,1)} %bitcast.82, bf16[1024,256]{1,0:T(8,128)(2,1)} %bitcast.83, ...), custom_call_target="tpu_custom_call" | custom-call | flops 1073741824 | bytes 6291456 | tf_op jit(solution)/shard_map/coupling/pallas_call | solution.py:70
  68.1 0.0 collective-permute-start.7
  68.1 11.2 %collective-permute-start.8 = (bf16[1024,256]{1,0:T(8,128)(2,1)}, bf16[1024,256]{1,0:T(8,128)(2,1)S(1)}, u32[]{:S(2)}, u32[]{:S(2)}) collective-permute-start(bf16[1024,256]{1,0:T(8,128)(2,1)} %get-tuple-element.7.c0), channel_id=1, source_target_pairs={{0,2},{1,3},{2,0},{3,1},{4,6},{5,7},{6,4},{7,5},{8,10},{9,11},{10,... | collective-permute-start | bytes 1572872 | tf_op jit(solution)/shard_map/ppermute | solution.py:295
  79.4 0.0 collective-permute-done.10
  79.4 2.0 %collective-permute-start.9 = (bf16[1024,256]{1,0:T(8,128)(2,1)}, bf16[1024,256]{1,0:T(8,128)(2,1)S(1)}, u32[]{:S(2)}, u32[]{:S(2)}) collective-permute-start(bf16[1024,256]{1,0:T(8,128)(2,1)} %get-tuple-element.7.c0), channel_id=1, source_target_pairs={{0,3},{1,0},{2,1},{3,2},{4,7},{5,4},{6,5},{7,6},{8,11},{9,8},{10,9... | collective-permute-start | bytes 1572872 | tf_op jit(solution)/shard_map/ppermute | solution.py:295
  81.4 0.0 collective-permute-done.11
  81.4 0.0 collective-permute-done.12
  81.4 1.7 %pad_maximum_fusion.l_ref = bf16[4,2,512,256]{3,2,1,0:T(8,128)(2,1)S(1)} fusion(bf16[1,2,512,256]{3,2,1,0:T(8,128)(2,1)} %bitcast.30, bf16[1,2,512,256]{3,2,1,0:T(8,128)(2,1)} %bitcast.28, bf16[1,2,512,256]{3,2,1,0:T(8,128)(2,1)} %bitcast.26, bf16[1,2,512,256]{3,2,1,0:T(8,128)(2,1)S(1)} %bitcast.73), kind=kLoop, calls=%fused_computation | loop fusion | flops 3145728 | bytes 4194304 | tf_op jit(solution)/shard_map/stack | solution.py:298
  83.1 0.0 collective-permute-done.7.c1
  83.2 19.3 %collective-permute-done.8.c2 = bf16[1024,256]{1,0:T(8,128)(2,1)S(1)} collective-permute-done((bf16[1024,256]{1,0:T(8,128)(2,1)}, bf16[1024,256]{1,0:T(8,128)(2,1)S(1)}, u32[]{:S(2)}, u32[]{:S(2)}) %collective-permute-start.8) | collective-permute-done | bytes 524320 | tf_op jit(solution)/shard_map/ppermute | solution.py:295
  102.5 0.0 collective-permute-done.9.c3
  102.5 0.0 copy-start.11
  102.5 0.0 copy-start.10
  102.5 15.2 %block_and_pairs.1 = (bf16[1024,512]{1,0:T(8,128)(2,1)S(1)}, bf16[1024,128]{1,0:T(8,128)(2,1)}) custom-call(s32[1]{0:T(128)} %bitcast.base_ref, s32[1024]{0:T(1024)S(1)} %reshape.151.codes_ref, bf16[1024,256]{1,0:T(8,128)(2,1)S(1)} %copy-done, bf16[1024,256]{1,0:T(8,128)(2,1)S(1)} %collective-permute-done.7.c1, ...), custom_call_target="tpu_custom_call" | custom-call | flops 2147483648 | bytes 12582912 | tf_op jit(solution)/shard_map/block_and_pairs/pallas_call | solution.py:153
  117.7 9.7 %all-to-all-start = ((bf16[16,64,128]{2,1,0:T(8,128)(2,1)}), bf16[16,64,128]{2,1,0:T(8,128)(2,1)S(1)}, u32[]{:S(2)}, u32[]{:S(2)}) async-start(bf16[16,64,128]{2,1,0:T(8,128)(2,1)} %bitcast.39), calls=%async_computation | async-start | bytes 524288 | tf_op jit(solution)/shard_map/all_to_all | solution.py:308
  128.1 0.6 dynamic-slice
  128.7 0.8 dynamic-update-slice
  129.4 12.4 %all-reduce = s32[16]{0:T(128)S(1)} all-reduce(s32[16]{0:T(128)S(1)} %dynamic-update-slice), channel_id=1, replica_groups=mesh['pole_0'=8,'pole_1'=2,'row'=4,'col'=4] {'pole_0','pole_1'}, use_global_device_ids=true, to_apply=%add | all-reduce | flops 16 | bytes 128
  141.8 0.1 iota_compare_fusion.4
  141.9 0.1 select_reduce_fusion.1
  142.0 0.7 copy.29.weight_ref
  142.7 0.7 copy-done.4
  143.4 1.7 %pole_sum.1 = f32[64,128]{1,0:T(8,128)} custom-call(f32[16,2]{1,0:T(8,128)} %copy.29.weight_ref, bf16[16,64,128]{2,1,0:T(8,128)(2,1)} %copy-done.4), custom_call_target="tpu_custom_call" | custom-call | tf_op jit(solution)/shard_map/pole_sum/pallas_call | solution.py:199
  145.1 1.6 broadcast_in_dim.57
  146.7 5.6 %all-to-all-start.1 = ((f32[16,64,128]{2,1,0:T(8,128)}), f32[16,64,128]{2,1,0:T(8,128)S(1)}, u32[]{:S(2)}, u32[]{:S(2)}) async-start(f32[16,64,128]{2,1,0:T(8,128)} %broadcast_in_dim.57), calls=%async_computation.1 | async-start | bytes 1048576 | tf_op jit(solution)/shard_map/all_to_all | solution.py:311
  152.3 0.1 copy.30
  152.4 0.8 maximum_convert_fusion.projector_ref
  153.2 0.2 convert_reduce_fusion
  153.4 0.6 multiply_add_fusion.index_ref
  154.0 2.1 %copy.28 = bf16[64,8,2,512]{3,2,1,0:T(2,128)(2,1)} copy(bf16[64,8,2,512]{3,1,2,0:T(8,128)(2,1)S(1)} %bitcast.63) | data formatting | bytes 2097152 | tf_op jit(solution)/shard_map/transpose | solution.py:304
  156.1 5.5 %all-to-all-done.1 = f32[16,64,128]{2,1,0:T(8,128)S(1)} async-done(((f32[16,64,128]{2,1,0:T(8,128)}), f32[16,64,128]{2,1,0:T(8,128)S(1)}, u32[]{:S(2)}, u32[]{:S(2)}) %all-to-all-start.1) | async-done | bytes 524320 | tf_op jit(solution)/shard_map/all_to_all | solution.py:311
  161.6 0.8 copy-done.2
  162.4 2.5 %density.1 = f32[512,128]{1,0:T(8,128)} custom-call(s32[512]{0:T(512)} %multiply_add_fusion.index_ref, f32[1024,128]{1,0:T(8,128)} %bitcast.65, f32[512,128]{1,0:T(8,128)} %maximum_convert_fusion.projector_ref), custom_call_target="tpu_custom_call" | custom-call | tf_op jit(solution)/shard_map/density/pallas_call | solution.py:220
  (25 shorter events, 0.1 us)
Async XLA Ops:
  0.6 52.2 %copy-start.3 = (bf16[1,512,2,512]{3,2,1,0:T(2,128)(2,1)S(1)}, bf16[1,512,2,512]{3,2,1,0:T(2,128)(2,1)}, u32[]{:S(2)}) copy-start(bf16[1,512,2,512]{3,2,1,0:T(2,128)(2,1)} %param.10) | copy-start | bytes 3145732
  1.8 15.6 %collective-permute-start.2 = (bf16[512,2,256]{2,0,1:T(8,128)(2,1)S(1)}, bf16[512,2,256]{2,0,1:T(8,128)(2,1)S(1)}, u32[]{:S(2)}, u32[]{:S(2)}) collective-permute-start(bf16[512,2,256]{2,0,1:T(8,128)(2,1)S(1)} %bitcast.66), channel_id=1, source_target_pairs={{0,2},{1,6},{2,10},{3,14},{4,3},{5,7},{6,11},{7,15},{8,0},{9,4},{1... | collective-permute-start | bytes 1572872 | tf_op jit(solution)/shard_map/ppermute | solution.py:277
  5.5 25.2 %collective-permute-start.3 = (bf16[512,2,256]{2,0,1:T(8,128)(2,1)S(1)}, bf16[512,2,256]{2,0,1:T(8,128)(2,1)S(1)}, u32[]{:S(2)}, u32[]{:S(2)}) collective-permute-start(bf16[512,2,256]{2,0,1:T(8,128)(2,1)S(1)} %bitcast.67), channel_id=1, source_target_pairs={{0,3},{1,7},{2,11},{3,15},{4,0},{5,4},{6,8},{7,12},{8,1},{9,5},{10... | collective-permute-start | bytes 1572872 | tf_op jit(solution)/shard_map/ppermute | solution.py:277
  8.2 29.3 %collective-permute-start = (bf16[512,2,256]{2,0,1:T(8,128)(2,1)S(1)}, bf16[512,2,256]{2,0,1:T(8,128)(2,1)}, u32[]{:S(2)}, u32[]{:S(2)}) collective-permute-start(bf16[512,2,256]{2,0,1:T(8,128)(2,1)S(1)} %bitcast.68), channel_id=1, source_target_pairs={{0,0},{1,4},{2,8},{3,12},{4,1},{5,5},{6,9},{7,13},{8,2},{9,6},{10,... | collective-permute-start | bytes 1572872 | tf_op jit(solution)/shard_map/ppermute | solution.py:277
  9.7 27.9 %collective-permute-start.1 = (bf16[512,2,256]{2,0,1:T(8,128)(2,1)S(1)}, bf16[512,2,256]{2,0,1:T(8,128)(2,1)}, u32[]{:S(2)}, u32[]{:S(2)}) collective-permute-start(bf16[512,2,256]{2,0,1:T(8,128)(2,1)S(1)} %bitcast.69), channel_id=1, source_target_pairs={{0,1},{1,5},{2,9},{3,13},{4,2},{5,6},{6,10},{7,14},{8,3},{9,7},{10... | collective-permute-start | bytes 1572872 | tf_op jit(solution)/shard_map/ppermute | solution.py:277
  11.8 41.4 %collective-permute-start.4 = (bf16[256,2,256]{2,0,1:T(8,128)(2,1)S(1)}, bf16[256,2,256]{2,0,1:T(8,128)(2,1)S(1)}, u32[]{:S(2)}, u32[]{:S(2)}) collective-permute-start(bf16[256,2,256]{2,0,1:T(8,128)(2,1)S(1)} %bitcast.76), channel_id=1, source_target_pairs={{0,4},{4,8},{8,12},{12,0},{1,5},{5,9},{9,13},{13,1},{2,6},{6,10},{... | collective-permute-start | bytes 786440 | tf_op jit(solution)/shard_map/ppermute | solution.py:276
  17.4 35.4 %copy-start.5 = (bf16[512,2,256]{2,0,1:T(8,128)(2,1)}, bf16[512,2,256]{2,0,1:T(8,128)(2,1)S(1)}, u32[]{:S(2)}) copy-start(bf16[512,2,256]{2,0,1:T(8,128)(2,1)S(1)} %collective-permute-done.2) | copy-start | bytes 1572868
  17.4 38.1 %collective-permute-start.5 = (bf16[256,2,256]{2,0,1:T(8,128)(2,1)S(1)}, bf16[256,2,256]{2,0,1:T(8,128)(2,1)}, u32[]{:S(2)}, u32[]{:S(2)}) collective-permute-start(bf16[256,2,256]{2,0,1:T(8,128)(2,1)S(1)} %bitcast.77), channel_id=1, source_target_pairs={{0,8},{4,12},{8,0},{12,4},{1,9},{5,13},{9,1},{13,5},{2,10},{6,14},... | collective-permute-start | bytes 786440 | tf_op jit(solution)/shard_map/ppermute | solution.py:276
  30.7 22.1 %copy-start.7 = (bf16[512,2,256]{2,0,1:T(8,128)(2,1)}, bf16[512,2,256]{2,0,1:T(8,128)(2,1)S(1)}, u32[]{:S(2)}) copy-start(bf16[512,2,256]{2,0,1:T(8,128)(2,1)S(1)} %collective-permute-done.3) | copy-start | bytes 1572868
  30.7 24.8 %collective-permute-start.6 = (bf16[256,2,256]{2,0,1:T(8,128)(2,1)S(1)}, bf16[256,2,256]{2,0,1:T(8,128)(2,1)}, u32[]{:S(2)}, u32[]{:S(2)}) collective-permute-start(bf16[256,2,256]{2,0,1:T(8,128)(2,1)S(1)} %bitcast.78), channel_id=1, source_target_pairs={{0,12},{4,0},{8,4},{12,8},{1,13},{5,1},{9,5},{13,9},{2,14},{6,2},{... | collective-permute-start | bytes 786440 | tf_op jit(solution)/shard_map/ppermute | solution.py:276
  37.6 41.8 %collective-permute-start.10 = (bf16[512,2,256]{2,0,1:T(8,128)(2,1)S(1)}, bf16[512,2,256]{2,0,1:T(8,128)(2,1)}, u32[]{:S(2)}, u32[]{:S(2)}) collective-permute-start(bf16[512,2,256]{2,0,1:T(8,128)(2,1)S(1)} %bitcast.70), channel_id=1, source_target_pairs={{0,4},{4,8},{8,12},{12,0},{1,5},{5,9},{9,13},{13,1},{2,6},{6,10},{... | collective-permute-start | bytes 1572872 | tf_op jit(solution)/shard_map/ppermute | solution.py:297
  53.0 4.7 %copy-start.6 = (bf16[512,2,256]{2,0,1:T(8,128)(2,1)S(1)}, bf16[512,2,256]{2,0,1:T(8,128)(2,1)}, u32[]{:S(2)}) copy-start(bf16[512,2,256]{2,0,1:T(8,128)(2,1)} %copy-done.5) | copy-start | bytes 1572868
  53.1 5.5 %copy-start.8 = (bf16[512,2,256]{2,0,1:T(8,128)(2,1)S(1)}, bf16[512,2,256]{2,0,1:T(8,128)(2,1)}, u32[]{:S(2)}) copy-start(bf16[512,2,256]{2,0,1:T(8,128)(2,1)} %copy-done.7) | copy-start | bytes 1572868
  53.1 28.3 %collective-permute-start.11 = (bf16[512,2,256]{2,0,1:T(8,128)(2,1)S(1)}, bf16[512,2,256]{2,0,1:T(8,128)(2,1)}, u32[]{:S(2)}, u32[]{:S(2)}) collective-permute-start(bf16[512,2,256]{2,0,1:T(8,128)(2,1)S(1)} %bitcast.71), channel_id=1, source_target_pairs={{0,8},{4,12},{8,0},{12,4},{1,9},{5,13},{9,1},{13,5},{2,10},{6,14},... | collective-permute-start | bytes 1572872 | tf_op jit(solution)/shard_map/ppermute | solution.py:297
  53.2 28.2 %collective-permute-start.12 = (bf16[512,2,256]{2,0,1:T(8,128)(2,1)S(1)}, bf16[512,2,256]{2,0,1:T(8,128)(2,1)}, u32[]{:S(2)}, u32[]{:S(2)}) collective-permute-start(bf16[512,2,256]{2,0,1:T(8,128)(2,1)S(1)} %bitcast.72), channel_id=1, source_target_pairs={{0,12},{4,0},{8,4},{12,8},{1,13},{5,1},{9,5},{13,9},{2,14},{6,2},{... | collective-permute-start | bytes 1572872 | tf_op jit(solution)/shard_map/ppermute | solution.py:297
  68.1 15.0 %collective-permute-start.7 = (bf16[1024,256]{1,0:T(8,128)(2,1)}, bf16[1024,256]{1,0:T(8,128)(2,1)S(1)}, u32[]{:S(2)}, u32[]{:S(2)}) collective-permute-start(bf16[1024,256]{1,0:T(8,128)(2,1)} %get-tuple-element.7.c0), channel_id=1, source_target_pairs={{0,1},{1,2},{2,3},{3,0},{4,5},{5,6},{6,7},{7,4},{8,9},{9,10},{10,1... | collective-permute-start | bytes 1572872 | tf_op jit(solution)/shard_map/ppermute | solution.py:295
  68.1 34.3 %collective-permute-start.8 = (bf16[1024,256]{1,0:T(8,128)(2,1)}, bf16[1024,256]{1,0:T(8,128)(2,1)S(1)}, u32[]{:S(2)}, u32[]{:S(2)}) collective-permute-start(bf16[1024,256]{1,0:T(8,128)(2,1)} %get-tuple-element.7.c0), channel_id=1, source_target_pairs={{0,2},{1,3},{2,0},{3,1},{4,6},{5,7},{6,4},{7,5},{8,10},{9,11},{10,... | collective-permute-start | bytes 1572872 | tf_op jit(solution)/shard_map/ppermute | solution.py:295
  79.4 23.1 %collective-permute-start.9 = (bf16[1024,256]{1,0:T(8,128)(2,1)}, bf16[1024,256]{1,0:T(8,128)(2,1)S(1)}, u32[]{:S(2)}, u32[]{:S(2)}) collective-permute-start(bf16[1024,256]{1,0:T(8,128)(2,1)} %get-tuple-element.7.c0), channel_id=1, source_target_pairs={{0,3},{1,0},{2,1},{3,2},{4,7},{5,4},{6,5},{7,6},{8,11},{9,8},{10,9... | collective-permute-start | bytes 1572872 | tf_op jit(solution)/shard_map/ppermute | solution.py:295
  81.4 21.1 %copy-start = (bf16[1024,256]{1,0:T(8,128)(2,1)S(1)}, bf16[1024,256]{1,0:T(8,128)(2,1)}, u32[]{:S(2)}) copy-start(bf16[1024,256]{1,0:T(8,128)(2,1)} %get-tuple-element.7.c0) | copy-start | bytes 1572868
  81.4 21.1 %copy-start.1 = (bf16[512,512]{1,0:T(8,128)(2,1)S(1)}, bf16[512,512]{1,0:T(8,128)(2,1)}, u32[]{:S(2)}) copy-start(bf16[512,512]{1,0:T(8,128)(2,1)} %get-tuple-element.9.ct_ref) | copy-start | bytes 1572868
  102.5 25.6 %copy-start.11 = (u32[256]{0:T(256)S(1)}, u32[256]{0:T(256)}, u32[]{:S(2)}) copy-start(u32[256]{0:T(256)} %constant.134) | copy-start | bytes 3076
  102.5 39.4 %copy-start.10 = (f32[256,2]{0,1:T(2,128)S(1)}, f32[256,2]{0,1:T(2,128)}, u32[]{:S(2)}) copy-start(f32[256,2]{0,1:T(2,128)} %param.11) | copy-start | bytes 6148
  117.7 34.6 %copy-start.9 = (bf16[512,64]{0,1:T(8,128)(2,1)S(1)}, bf16[512,64]{0,1:T(8,128)(2,1)}, u32[]{:S(2)}) copy-start(bf16[512,64]{0,1:T(8,128)(2,1)} %param.15) | copy-start | bytes 196612
  117.7 25.0 %all-to-all-start = ((bf16[16,64,128]{2,1,0:T(8,128)(2,1)}), bf16[16,64,128]{2,1,0:T(8,128)(2,1)S(1)}, u32[]{:S(2)}, u32[]{:S(2)}) async-start(bf16[16,64,128]{2,1,0:T(8,128)(2,1)} %bitcast.39), calls=%async_computation | async-start | bytes 524288 | tf_op jit(solution)/shard_map/all_to_all | solution.py:308
  142.7 0.7 copy-start.4
  146.7 14.9 %all-to-all-start.1 = ((f32[16,64,128]{2,1,0:T(8,128)}), f32[16,64,128]{2,1,0:T(8,128)S(1)}, u32[]{:S(2)}, u32[]{:S(2)}) async-start(f32[16,64,128]{2,1,0:T(8,128)} %broadcast_in_dim.57), calls=%async_computation.1 | async-start | bytes 1048576 | tf_op jit(solution)/shard_map/all_to_all | solution.py:311
  161.6 0.8 copy-start.2

commit v2 on v1

v2 whole, which is shorter than its diff:
```python
import jax
import jax.numpy as jnp
from jax import lax
from jax.experimental import pallas as pl
from jax.experimental.pallas import tpu as pltpu
from jax.sharding import Mesh
from jax.sharding import PartitionSpec as P

B = 8
KA = 256
POLE = ("pole_0", "pole_1")
ROWS = 4
COLS = 4
SLOTS = 64
MIB = 1 << 20


def ring(shift, peers):
    return [(i, (i + shift) % peers) for i in range(peers)]


def to_process_rows(shift):
    return [
        (k * COLS + x, x * COLS + (k + shift) % COLS) for k in range(ROWS) for x in range(COLS)
    ]


def parts_apart(raw):
    return raw.transpose(1, 0, 2)


def whole(shape):
    return pl.BlockSpec(shape, lambda *_: (0,) * len(shape))


def product(left, right, dim):
    return lax.dot_general(
        left, right, (((1,), (dim,)), ((), ())), preferred_element_type=jnp.float32
    )


def complex_product(lefts, rights, dim, order):
    left = jnp.concatenate([x[...].reshape(-1, x.shape[2]) for x in lefts], axis=1)
    real = jnp.concatenate([rights[e][0] for e in order], axis=dim)
    imag = jnp.concatenate([rights[e][1] for e in order], axis=dim)
    half = left.shape[0] // 2
    u = product(left, real, dim)
    v = product(left, imag, dim)
    return u[:half] - v[half:], u[half:] + v[:half]


def by_atom(re, im):
    rows, columns = re.shape
    pair = [x.reshape(rows // B, B, columns) for x in (re, im)]
    return jnp.stack(pair, axis=1).reshape(2 * rows, columns).astype(jnp.bfloat16)


def coupling_kernel(base_ref, l0, l1, l2, l3, t0, t1, t2, t3, c_ref, ct_ref):
    def run(order):
        re, im = complex_product((l0, l1, l2, l3), (t0, t1, t2, t3), 0, order)
        c_ref[0] = (-re).astype(jnp.bfloat16)
        c_ref[1] = (-im).astype(jnp.bfloat16)
        ct_ref[...] = by_atom((-re).T, (-im).T)

    for base in range(ROWS):

        @pl.when(base_ref[0] == base)
        def _():
            run([(base + d) % ROWS for d in range(ROWS)])


def coupling_call(base, lefts, trails):
    _, rows, inner = lefts[0].shape
    columns = trails[0].shape[2]
    tile = 256
    left_spec = pl.BlockSpec((2, tile, inner), lambda i, *_: (0, i, 0))
    return pl.pallas_call(
        coupling_kernel,
        out_shape=(
            jax.ShapeDtypeStruct((2, rows, columns), jnp.bfloat16),
            jax.ShapeDtypeStruct((2 * columns, rows), jnp.bfloat16),
        ),
        grid_spec=pltpu.PrefetchScalarGridSpec(
            num_scalar_prefetch=1,
            grid=(rows // tile,),
            in_specs=[left_spec] * 4 + [whole(trails[0].shape)] * 4,
            out_specs=(
                pl.BlockSpec((2, tile, columns), lambda i, *_: (0, i, 0)),
                pl.BlockSpec((2 * columns, tile), lambda i, *_: (0, i)),
            ),
        ),
        compiler_params=pltpu.CompilerParams(vmem_limit_bytes=24 * MIB),
        cost_estimate=pl.CostEstimate(
            flops=2 * rows * inner * 16 * columns, bytes_accessed=6 << 20, transcendentals=0
        ),
        name="coupling",
    )(base, *lefts, *trails)


def take_pairs(codes_ref, mask_ref, pairs_ref, table, lanes, spread, keep, fold):
    @pl.loop(0, pairs_ref.shape[0])
    def _(owner):
        for s in range(SLOTS):
            code = codes_ref[owner * SLOTS + s]
            found = table[pl.ds(pl.multiple_of(code & ~15, 16), 16), :]
            lanes[s * 16 : s * 16 + 16, :] = found * mask_ref[code & 15]
        wide = product(lanes[...], spread[...], 0).reshape(SLOTS, 2, 8, 2 * B * B)
        wide = wide * keep[...][None]
        wide = (wide[:, 0] + wide[:, 1]).reshape(SLOTS * 8, 2 * B * B).astype(jnp.bfloat16)
        pairs_ref[owner, :SLOTS, :] = product(fold[...], wide, 0).astype(jnp.bfloat16)


def block_kernel(
    base_ref, slot_ref, codes_ref, c0, c1, c2, c3, l0, l1, l2, l3, diag_ref, ct_ref, mask_ref,
    out_ref, pairs_ref, table, lanes, spread, keep, fold,
):
    step = pl.program_id(0)
    last = pl.num_programs(0) - 1
    tile = out_ref.shape[1]
    per_tile = table.shape[0] // 4
    super_rows = per_tile - ct_ref.shape[0]

    @pl.when(step == 0)
    def _():
        for t in range(4):
            first = t * per_tile + super_rows
            table[first : first + ct_ref.shape[0], :] = ct_ref[:, t * 128 : t * 128 + 128]
        lane = lax.broadcasted_iota(jnp.int32, (128, 128), 1)
        row = lax.broadcasted_iota(jnp.int32, (128, 128), 0)
        spread[...] = jnp.where(row % 8 == lane % 8, 1.0, 0.0).astype(jnp.bfloat16)
        part = lax.broadcasted_iota(jnp.int32, (2, 8, 128), 0)
        row = lax.broadcasted_iota(jnp.int32, (2, 8, 128), 1)
        lane = lax.broadcasted_iota(jnp.int32, (2, 8, 128), 2)
        keep[...] = jnp.where(lane // 8 == part * 8 + row, 1.0, 0.0)
        row = lax.broadcasted_iota(jnp.int32, fold.shape, 0)
        lane = lax.broadcasted_iota(jnp.int32, fold.shape, 1)
        fold[...] = jnp.where(lane // 8 == row, 1.0, 0.0).astype(jnp.bfloat16)
        slot = jnp.full((16, 128), slot_ref[0], jnp.int32).astype(jnp.float32)
        for owner in range(pairs_ref.shape[0]):
            pairs_ref[owner, SLOTS:, :] = slot.astype(jnp.bfloat16)

    def run(order):
        re, im = complex_product((c0, c1, c2, c3), (l0, l1, l2, l3), 1, order)
        re = diag_ref[0].astype(jnp.float32) - re
        im = diag_ref[1].astype(jnp.float32) - im
        out_ref[0] = re.astype(jnp.bfloat16)
        out_ref[1] = im.astype(jnp.bfloat16)
        rows = by_atom(re, im)
        for t in range(4):
            first = pl.multiple_of(t * per_tile + step * 2 * tile, 2 * tile)
            table[pl.ds(first, 2 * tile), :] = rows[:, t * 128 : t * 128 + 128]

    for base in range(ROWS):

        @pl.when(base_ref[0] == base)
        def _():
            run([(base + d) % ROWS for d in range(ROWS)])

    @pl.when(step == last)
    def _():
        take_pairs(codes_ref, mask_ref, pairs_ref, table, lanes, spread, keep, fold)


def block_call(base, slot, codes, couplings, lowers, diag, coupling_t, masks):
    _, rows, columns = diag.shape
    inner = couplings[0].shape[2]
    owners = codes.shape[0] // SLOTS
    tile = 256
    row_spec = lambda last: pl.BlockSpec((2, tile, last), lambda i, *_: (0, i, 0))
    return pl.pallas_call(
        block_kernel,
        out_shape=(
            jax.ShapeDtypeStruct((2, rows, columns), jnp.bfloat16),
            jax.ShapeDtypeStruct((owners, SLOTS + 16, 2 * B * B), jnp.bfloat16),
        ),
        grid_spec=pltpu.PrefetchScalarGridSpec(
            num_scalar_prefetch=3,
            grid=(rows // tile,),
            in_specs=[row_spec(inner)] * 4
            + [whole(lowers[0].shape)] * 4
            + [row_spec(columns), whole(coupling_t.shape), whole(masks.shape)],
            out_specs=(row_spec(columns), whole((owners, SLOTS + 16, 2 * B * B))),
            scratch_shapes=[
                pltpu.VMEM((4 * (2 * rows + coupling_t.shape[0]), 128), jnp.bfloat16),
                pltpu.VMEM((SLOTS * 16, 128), jnp.bfloat16),
                pltpu.VMEM((128, 128), jnp.bfloat16),
                pltpu.VMEM((2, 8, 128), jnp.float32),
                pltpu.VMEM((SLOTS, SLOTS * 8), jnp.bfloat16),
            ],
        ),
        compiler_params=pltpu.CompilerParams(vmem_limit_bytes=40 * MIB),
        cost_estimate=pl.CostEstimate(
            flops=2 * rows * inner * 16 * columns, bytes_accessed=12 << 20, transcendentals=0
        ),
        name="block_and_pairs",
    )(base, slot, codes, *couplings, *lowers, diag, coupling_t, masks)


def pole_sum_kernel(weight_ref, parts_ref, out_ref):
    lane = lax.broadcasted_iota(jnp.int32, (1, 128), 1).astype(jnp.float32)
    straight = crossed = None
    for p in range(parts_ref.shape[0]):
        part = parts_ref[p, :SLOTS, :].astype(jnp.float32)
        slot = parts_ref[p, SLOTS:, :].astype(jnp.float32)[:1]
        weight = []
        for c in range(2):
            found = jnp.where(slot == lane, weight_ref[c : c + 1, :128], 0.0) + jnp.where(
                slot == lane + 128.0, weight_ref[c : c + 1, 128:], 0.0
            )
            weight.append(jnp.sum(found, axis=1, keepdims=True))
        a = weight[0] * part
        b = weight[1] * part
        straight = a if straight is None else straight + a
        crossed = b if crossed is None else crossed + b
    half = B * B
    lane = lax.broadcasted_iota(jnp.int32, crossed.shape, 1)
    crossed = pltpu.roll(crossed, half, 1)
    total = (straight + jnp.where(lane < half, -crossed, crossed)).astype(out_ref.dtype)
    for cell in range(out_ref.shape[0]):
        out_ref[cell] = total


def pole_sum_call(weights, parts, copies):
    return pl.pallas_call(
        pole_sum_kernel,
        out_shape=jax.ShapeDtypeStruct((copies, SLOTS, 2 * B * B), jnp.float32),
        in_specs=[pl.BlockSpec(memory_space=pltpu.VMEM)] * 2,
        out_specs=pl.BlockSpec(memory_space=pltpu.VMEM),
        name="pole_sum",
    )(weights, parts)


def density_kernel(index_ref, sums_ref, projector_ref, out_ref):
    @pl.loop(0, out_ref.shape[0] // 16)
    def _(group):
        first = pl.multiple_of(group * 16, 16)
        for s in range(16):
            q = first + s
            out_ref[pl.ds(q, 1), :] = sums_ref[pl.ds(index_ref[q], 1), :]
        here = pl.ds(first, 16)
        out_ref[here, :] = out_ref[here, :] * projector_ref[here, :]


def density_call(index, sums, projector):
    return pl.pallas_call(
        density_kernel,
        out_shape=jax.ShapeDtypeStruct(projector.shape, jnp.float32),
        in_specs=[pl.BlockSpec(memory_space=pltpu.SMEM)]
        + [pl.BlockSpec(memory_space=pltpu.VMEM)] * 2,
        out_specs=pl.BlockSpec(memory_space=pltpu.VMEM),
        name="density",
    )(index, sums, projector)


def pair_tables(pair_row, pair_col, row, col, pole, owners):
    row_atoms, col_atoms, trail_atoms = KA // ROWS, KA // COLS, 128 // COLS
    a = pair_row.reshape(owners, -1)
    b = pair_col.reshape(owners, -1)
    in_super = a < KA
    trail = a - KA
    cell = jnp.where(
        in_super,
        (a // row_atoms) * COLS + b // col_atoms,
        (b // row_atoms) * COLS + trail // trail_atoms,
    )
    table_atom = jnp.where(in_super, a % row_atoms, row_atoms + trail % trail_atoms)
    column_atom = jnp.where(in_super, b % col_atoms, b % row_atoms)
    tile, place = column_atom // 16, column_atom % 16
    code = (tile * (row_atoms + trail_atoms) + table_atom) * 16 + place
    pairs = a.shape[1]
    place = jnp.arange(pairs, dtype=jnp.int32)
    earlier = place[:, None] < place[None, :]
    mine = cell == row * COLS + col
    rank = jnp.dot(
        mine.astype(jnp.bfloat16),
        earlier.astype(jnp.bfloat16),
        preferred_element_type=jnp.float32,
    ).astype(jnp.int32)
    slot = jnp.where(mine, rank, -1)
    hit = slot[:, None, :] == jnp.arange(SLOTS, dtype=jnp.int32)[None, :, None]
    codes = jnp.sum(jnp.where(hit, code[:, None, :], 0), axis=2).reshape(owners * SLOTS)
    own_cell = lax.dynamic_index_in_dim(cell, pole, 0, keepdims=False)
    same = (own_cell[:, None] == own_cell[None, :]) & earlier
    index = own_cell * SLOTS + jnp.sum(same.astype(jnp.int32), axis=0)
    return codes, index


def local(
    inverse_trail, lower_t, diag_inverse, pole_weight, pole_slot, pair_row, pair_col, projector
):
    row = lax.axis_index("row")
    col = lax.axis_index("col")
    pole = lax.axis_index(POLE)
    poles = lax.axis_size(POLE)
    base = ((row - col + COLS) % COLS).astype(jnp.int32).reshape(1)

    trail = parts_apart(inverse_trail[0])
    lower = parts_apart(lower_t[0])
    lower, trail = lax.optimization_barrier((lower, trail))

    trails = [trail] + [lax.ppermute(trail, "row", ring(e, ROWS)) for e in range(1, ROWS)]
    lefts = [lax.ppermute(lower, ("row", "col"), to_process_rows(d)) for d in range(COLS)]

    codes, index = pair_tables(pair_row, pair_col, row, col, pole, poles)
    diag = parts_apart(diag_inverse[0])
    wide_projector = jnp.concatenate([projector, projector], axis=1).astype(jnp.float32)
    masks = (
        jnp.arange(16, dtype=jnp.int32)[:, None, None]
        == jnp.broadcast_to(jnp.arange(128, dtype=jnp.int32) // B, (16, 128))[None]
    ).astype(jnp.bfloat16)

    coupling, coupling_t = coupling_call(base, lefts, trails)
    lower_late, coupling = lax.optimization_barrier((lower, coupling))
    couplings = [coupling] + [
        lax.ppermute(coupling, "col", ring(d, COLS)) for d in range(1, COLS)
    ]
    lowers = [lower] + [lax.ppermute(lower_late, "row", ring(e, ROWS)) for e in range(1, ROWS)]

    block, pairs = block_call(
        base, pole_slot, codes, couplings, lowers, diag, coupling_t, masks
    )
    out = block.transpose(1, 0, 2)[None]

    parts = lax.all_to_all(pairs, POLE, 0, 0, tiled=True)
    cells = ROWS * COLS
    summed = pole_sum_call(pole_weight.T, parts, cells)
    everywhere = lax.all_to_all(summed, ("row", "col"), 0, 0, tiled=True)
    density = density_call(index, everywhere.reshape(cells * SLOTS, 2 * B * B), wide_projector)
    return (out, density)


def solution(mesh):
    split = Mesh(
        mesh.devices.reshape(8, 2, mesh.shape["row"], mesh.shape["col"]),
        ("pole_0", "pole_1", "row", "col"),
    )
    in_specs = (
        P(POLE, "row", None, "col"),
        P(POLE, "col", None, "row"),
        P(POLE, "row", None, "col"),
        P(),
        P(POLE),
        P(),
        P(),
        P(POLE, None),
    )
    out_specs = (P(POLE, "row", None, "col"), P(POLE, None))
    return jax.shard_map(local, mesh=split, in_specs=in_specs, out_specs=out_specs, check_vma=False)
```

time: 167 us -> 157 us (0.940)
  waiting for transfers between devices: 34.9 us -> 68.8 us
  starting transfers between devices: 68.6 us -> 50 us
  blocking collectives: 12.4 us -> 0 us
  local copies, waits for them, and re-layouts: 16.8 us -> 12.7 us
  other arithmetic: 6.08 us -> 2.11 us
  Pallas kernels: 24.4 us -> 20.6 us
    ppermute x3, waiting for transfers between devices: 0.01 us -> 29.2 us  [local(): lax.ppermute(trail, 'row', ring(e, ROWS))]
    all_to_all x2, waiting for transfers between devices: 5.5 us -> 21.4 us  [the longest x1 13.1 us: local(): parts = lax.all_to_all(pairs, POLE, 0, 0, tiled=True)]
    ppermute x3, waiting for transfers between devices: 19.3 us -> 3.86 us  [local(): lax.ppermute(coupling, 'col', ring(d, COLS))]
    ppermute x3, waiting for transfers between devices: 0.01 us -> 14.3 us  [local(): lax.ppermute(lower_late, 'row', ring(e, ROWS))]
    unnamed x1 -> x0, blocking collectives: 12.4 us -> none
    ppermute x4, waiting for transfers between devices: 10.1 us -> 0.01 us  [local(): lax.ppermute(lower, ('row', 'col'), to_process_rows(d))]
    ppermute x3, starting transfers between devices: 13.2 us -> 3.74 us  [local(): lax.ppermute(coupling, 'col', ring(d, COLS))]
    ppermute x3, starting transfers between devices: 14.1 us -> 4.83 us  [local(): lax.ppermute(trail, 'row', ring(e, ROWS))]
  transfers between devices with their start and end apart: 15 -> 15, of which waited for: 3 -> 8; matrix products, arithmetic and copies ran while one was open for 11% -> 4% of each run, Pallas kernels for 3% -> 0%
where the time goes in v2:
time: 157 us; the launch traced here: 156 us
  waiting for transfers between devices  68.8 us (44%)
  starting transfers between devices  50 us (32%)
  Pallas kernels  20.6 us (13%)
  local copies, waits for them, and re-layouts  12.7 us (8%)
  other arithmetic  2.11 us (1%)
    ppermute x3, waiting for transfers between devices, local(): lax.ppermute(trail, 'row', ring(e, ROWS))  29.2 us
    ppermute x3, starting transfers between devices, local(): lax.ppermute(lower_late, 'row', ring(e, ROWS))  15.1 us
    ppermute x3, waiting for transfers between devices, local(): lax.ppermute(lower_late, 'row', ring(e, ROWS))  14.3 us
    pallas_call x1, Pallas kernels, block_call(): pl.pallas_call(block_kernel, out_shape=(jax.ShapeDtypeStruct((2, rows, co...  13.3 us
    all_to_all x1, waiting for transfers between devices, local(): parts = lax.all_to_all(pairs, POLE, 0, 0, tiled=True)  13.1 us
    unnamed x33, local copies, waits for them, and re-layouts  12.6 us
    ppermute x4, starting transfers between devices, local(): lax.ppermute(lower, ('row', 'col'), to_process_rows(d))  10.4 us
    all_to_all x1, starting transfers between devices, local(): parts = lax.all_to_all(pairs, POLE, 0, 0, tiled=True)  10.1 us
  transfers between devices with their start and end apart: 15, of which 8 were waited for; matrix products, arithmetic and copies ran while one was open for 4% of the time, Pallas kernels for 0%

profile of v2, /device:TPU:1, one launch (start us, length us, event | category | flops | bytes accessed | tf_op | source)
XLA Modules:
  0.0 156.0 jit_solution(5096765643752847065)
XLA Ops:
  0.6 0.0 copy-start.10
  0.6 1.2 copy.26
  1.8 0.0 copy-done.10
  1.8 2.2 %collective-permute-start.4 = (bf16[2,256,256]{2,1,0:T(8,128)(2,1)S(1)}, bf16[2,256,256]{2,1,0:T(8,128)(2,1)S(1)}, u32[]{:S(2)}, u32[]{:S(2)}) collective-permute-start(bf16[2,256,256]{2,1,0:T(8,128)(2,1)S(1)} %bitcast.32), channel_id=1, source_target_pairs={{0,4},{4,8},{8,12},{12,0},{1,5},{5,9},{9,13},{13,1},{2,6},{6,10},{... | collective-permute-start | bytes 786440 | tf_op jit(solution)/shard_map/ppermute | solution.py:301
  4.0 2.6 %collective-permute-start.5 = (bf16[2,256,256]{2,1,0:T(8,128)(2,1)S(1)}, bf16[2,256,256]{2,1,0:T(8,128)(2,1)S(1)}, u32[]{:S(2)}, u32[]{:S(2)}) collective-permute-start(bf16[2,256,256]{2,1,0:T(8,128)(2,1)S(1)} %bitcast.33), channel_id=1, source_target_pairs={{0,8},{4,12},{8,0},{12,4},{1,9},{5,13},{9,1},{13,5},{2,10},{6,14},... | collective-permute-start | bytes 786440 | tf_op jit(solution)/shard_map/ppermute | solution.py:301
  6.7 0.7 collective-permute-start
  7.4 2.5 %collective-permute-start.1 = (bf16[2,512,256]{2,1,0:T(8,128)(2,1)S(1)}, bf16[2,512,256]{2,1,0:T(8,128)(2,1)S(1)}, u32[]{:S(2)}, u32[]{:S(2)}) collective-permute-start(bf16[2,512,256]{2,1,0:T(8,128)(2,1)S(1)} %bitcast.25), channel_id=1, source_target_pairs={{0,1},{1,5},{2,9},{3,13},{4,2},{5,6},{6,10},{7,14},{8,3},{9,7},{10... | collective-permute-start | bytes 1572872 | tf_op jit(solution)/shard_map/ppermute | solution.py:302
  9.9 3.7 %collective-permute-start.2 = (bf16[2,512,256]{2,1,0:T(8,128)(2,1)S(1)}, bf16[2,512,256]{2,1,0:T(8,128)(2,1)S(1)}, u32[]{:S(2)}, u32[]{:S(2)}) collective-permute-start(bf16[2,512,256]{2,1,0:T(8,128)(2,1)S(1)} %bitcast.26), channel_id=1, source_target_pairs={{0,2},{1,6},{2,10},{3,14},{4,3},{5,7},{6,11},{7,15},{8,0},{9,4},{1... | collective-permute-start | bytes 1572872 | tf_op jit(solution)/shard_map/ppermute | solution.py:302
  13.6 0.0 collective-permute-done.4.t1
  13.6 3.5 %collective-permute-start.3 = (bf16[2,512,256]{2,1,0:T(8,128)(2,1)S(1)}, bf16[2,512,256]{2,1,0:T(8,128)(2,1)S(1)}, u32[]{:S(2)}, u32[]{:S(2)}) collective-permute-start(bf16[2,512,256]{2,1,0:T(8,128)(2,1)S(1)} %bitcast.27), channel_id=1, source_target_pairs={{0,3},{1,7},{2,11},{3,15},{4,0},{5,4},{6,8},{7,12},{8,1},{9,5},{10... | collective-permute-start | bytes 1572872 | tf_op jit(solution)/shard_map/ppermute | solution.py:302
  17.1 23.5 %collective-permute-done.5.t2 = bf16[2,256,256]{2,1,0:T(8,128)(2,1)S(1)} collective-permute-done((bf16[2,256,256]{2,1,0:T(8,128)(2,1)S(1)}, bf16[2,256,256]{2,1,0:T(8,128)(2,1)S(1)}, u32[]{:S(2)}, u32[]{:S(2)}) %collective-permute-start.5) | collective-permute-done | bytes 262176 | tf_op jit(solution)/shard_map/ppermute | solution.py:301
  40.5 0.0 collective-permute-start.6
  40.5 5.7 %collective-permute-done.6.t3 = bf16[2,256,256]{2,1,0:T(8,128)(2,1)} collective-permute-done((bf16[2,256,256]{2,1,0:T(8,128)(2,1)S(1)}, bf16[2,256,256]{2,1,0:T(8,128)(2,1)}, u32[]{:S(2)}, u32[]{:S(2)}) %collective-permute-start.6) | collective-permute-done | bytes 262176 | tf_op jit(solution)/shard_map/ppermute | solution.py:301
  46.2 0.0 collective-permute-done.l0
  46.2 0.0 collective-permute-done.1.l1
  46.2 0.0 collective-permute-done.2.l2
  46.3 0.0 collective-permute-done.3.l3
  46.3 0.0 copy-start
  46.3 0.8 copy-done
  47.1 0.0 copy-start.1
  47.1 1.0 copy-done.1
  48.1 0.0 copy-start.12
  48.1 2.8 %coupling.1 = (bf16[2,512,256]{2,1,0:T(8,128)(2,1)S(1)}, bf16[512,512]{1,0:T(8,128)(2,1)S(1)}) custom-call(s32[1]{0:T(128)} %bitcast.base_ref, bf16[2,512,256]{2,1,0:T(8,128)(2,1)S(1)} %collective-permute-done.l0, bf16[2,512,256]{2,1,0:T(8,128)(2,1)S(1)} %collective-permute-done.1.l1, bf16[2,512,256]{2,1,0:T(8,128)(2,1)S(1)} %collective-permute-done.2.l2, ...), custom_call_target="tpu_custom_call" | custom-call | flops 1073741824 | bytes 6291456 | tf_op jit(solution)/shard_map/coupling/pallas_call | solution.py:77
  50.9 0.0 copy-start.6
  50.9 0.8 copy-done.6
  51.7 12.6 %collective-permute-start.10 = (bf16[2,512,256]{2,1,0:T(8,128)(2,1)S(1)}, bf16[2,512,256]{2,1,0:T(8,128)(2,1)S(1)}, u32[]{:S(2)}, u32[]{:S(2)}) collective-permute-start(bf16[2,512,256]{2,1,0:T(8,128)(2,1)S(1)} %bitcast.28), channel_id=1, source_target_pairs={{0,4},{4,8},{8,12},{12,0},{1,5},{5,9},{9,13},{13,1},{2,6},{6,10},{... | collective-permute-start | bytes 1572872 | tf_op jit(solution)/shard_map/ppermute | solution.py:317
  64.4 0.0 copy-done.12
  64.4 0.0 copy-done.13
  64.4 0.1 fusion.5
  64.5 0.1 collective-permute-start.11
  64.6 2.4 %collective-permute-start.12 = (bf16[2,512,256]{2,1,0:T(8,128)(2,1)S(1)}, bf16[2,512,256]{2,1,0:T(8,128)(2,1)S(1)}, u32[]{:S(2)}, u32[]{:S(2)}) collective-permute-start(bf16[2,512,256]{2,1,0:T(8,128)(2,1)S(1)} %bitcast.30), channel_id=1, source_target_pairs={{0,12},{4,0},{8,4},{12,8},{1,13},{5,1},{9,5},{13,9},{2,14},{6,2},{... | collective-permute-start | bytes 1572872 | tf_op jit(solution)/shard_map/ppermute | solution.py:317
  67.0 0.0 collective-permute-start.7
  67.0 3.7 %collective-permute-start.8 = (bf16[2,512,256]{2,1,0:T(8,128)(2,1)S(1)}, bf16[2,512,256]{2,1,0:T(8,128)(2,1)}, u32[]{:S(2)}, u32[]{:S(2)}) collective-permute-start(bf16[2,512,256]{2,1,0:T(8,128)(2,1)S(1)} %get-tuple-element.13.c0), channel_id=1, source_target_pairs={{0,2},{1,3},{2,0},{3,1},{4,6},{5,7},{6,4},{7,5},{8,10},{9,11},{10,... | collective-permute-start | bytes 1572872 | tf_op jit(solution)/shard_map/ppermute | solution.py:315
  70.8 4.4 %collective-permute-done.10.l1 = bf16[2,512,256]{2,1,0:T(8,128)(2,1)S(1)} collective-permute-done((bf16[2,512,256]{2,1,0:T(8,128)(2,1)S(1)}, bf16[2,512,256]{2,1,0:T(8,128)(2,1)S(1)}, u32[]{:S(2)}, u32[]{:S(2)}) %collective-permute-start.10) | collective-permute-done | bytes 524320 | tf_op jit(solution)/shard_map/ppermute | solution.py:317
  75.2 0.0 collective-permute-start.9
  75.2 0.2 fusion
  75.4 0.4 select_reduce_fusion
  75.7 0.1 reshape.118.codes_ref
  75.8 1.5 copy.25
  77.9 8.5 %collective-permute-done.11.l2 = bf16[2,512,256]{2,1,0:T(8,128)(2,1)S(1)} collective-permute-done((bf16[2,512,256]{2,1,0:T(8,128)(2,1)S(1)}, bf16[2,512,256]{2,1,0:T(8,128)(2,1)S(1)}, u32[]{:S(2)}, u32[]{:S(2)}) %collective-permute-start.11) | collective-permute-done | bytes 524320 | tf_op jit(solution)/shard_map/ppermute | solution.py:317
  86.4 1.5 collective-permute-done.12.l3
  87.9 0.8 copy-done.2
  88.7 0.0 collective-permute-done.7.c1
  88.7 0.8 copy-done.4
  89.5 3.9 %collective-permute-done.8.c2 = bf16[2,512,256]{2,1,0:T(8,128)(2,1)} collective-permute-done((bf16[2,512,256]{2,1,0:T(8,128)(2,1)S(1)}, bf16[2,512,256]{2,1,0:T(8,128)(2,1)}, u32[]{:S(2)}, u32[]{:S(2)}) %collective-permute-start.8) | collective-permute-done | bytes 524320 | tf_op jit(solution)/shard_map/ppermute | solution.py:315
  93.3 0.0 collective-permute-done.9.c3
  93.3 0.0 copy-done.7
  93.3 1.0 copy-done.3
  94.4 1.0 copy-done.5
  95.4 13.3 %block_and_pairs.1 = (bf16[2,512,512]{2,1,0:T(8,128)(2,1)S(1)}, bf16[16,80,128]{2,1,0:T(8,128)(2,1)}) custom-call(s32[1]{0:T(128)} %bitcast.base_ref, s32[1]{0:T(128)S(6)} %copy.28.slot_ref, s32[1024]{0:T(1024)S(1)} %reshape.118.codes_ref, bf16[2,512,256]{2,1,0:T(8,128)(2,1)S(1)} %get-tuple-element.13.c0, bf16[2,512,256]{2,1,0:T(8,128)(2,1)S(1)} %copy-done.5, ...), custom_call_target="tpu_custom_call" | custom-call | flops 2147483648 | bytes 12582912 | tf_op jit(solution)/shard_map/block_and_pairs/pallas_call | solution.py:170
  108.7 10.1 %all-to-all-start = ((bf16[16,80,128]{2,1,0:T(8,128)(2,1)}), bf16[16,80,128]{2,1,0:T(8,128)(2,1)S(1)}, u32[]{:S(2)}, u32[]{:S(2)}) async-start(bf16[16,80,128]{2,1,0:T(8,128)(2,1)} %get-tuple-element.17), calls=%async_computation | async-start | bytes 655360 | tf_op jit(solution)/shard_map/all_to_all | solution.py:324
  118.9 13.1 %all-to-all-done.parts_ref = bf16[16,80,128]{2,1,0:T(8,128)(2,1)S(1)} async-done(((bf16[16,80,128]{2,1,0:T(8,128)(2,1)}), bf16[16,80,128]{2,1,0:T(8,128)(2,1)S(1)}, u32[]{:S(2)}, u32[]{:S(2)}) %all-to-all-start) | async-done | bytes 327712 | tf_op jit(solution)/shard_map/all_to_all | solution.py:324
  131.9 0.7 copy-done.9
  132.6 2.0 %pole_sum.1 = f32[16,64,128]{2,1,0:T(8,128)} custom-call(f32[2,256]{1,0:T(2,128)} %bitcast.39, bf16[16,80,128]{2,1,0:T(8,128)(2,1)} %copy-done.9), custom_call_target="tpu_custom_call" | custom-call | tf_op jit(solution)/shard_map/pole_sum/pallas_call | solution.py:224
  134.7 5.8 %all-to-all-start.1 = ((f32[16,64,128]{2,1,0:T(8,128)}), f32[16,64,128]{2,1,0:T(8,128)S(1)}, u32[]{:S(2)}, u32[]{:S(2)}) async-start(f32[16,64,128]{2,1,0:T(8,128)} %pole_sum.1), calls=%async_computation.1 | async-start | bytes 1048576 | tf_op jit(solution)/shard_map/all_to_all | solution.py:327
  140.6 0.0 copy-done.11
  140.6 0.1 copy.19
  140.7 0.8 maximum_convert_fusion.projector_ref
  141.5 0.2 convert_reduce_fusion
  141.7 0.6 multiply_add_fusion.index_ref
  142.3 2.0 %copy.21 = bf16[1,512,2,512]{3,2,1,0:T(2,128)(2,1)} copy(bf16[1,512,2,512]{3,1,2,0:T(8,128)(2,1)S(1)} %bitcast.22) | data formatting | bytes 2097152
  144.3 8.4 %all-to-all-done.1 = f32[16,64,128]{2,1,0:T(8,128)S(1)} async-done(((f32[16,64,128]{2,1,0:T(8,128)}), f32[16,64,128]{2,1,0:T(8,128)S(1)}, u32[]{:S(2)}, u32[]{:S(2)}) %all-to-all-start.1) | async-done | bytes 524320 | tf_op jit(solution)/shard_map/all_to_all | solution.py:327
  152.7 0.8 copy-done.8
  153.5 2.5 %density.1 = f32[512,128]{1,0:T(8,128)} custom-call(s32[512]{0:T(512)} %multiply_add_fusion.index_ref, f32[1024,128]{1,0:T(8,128)} %bitcast.36, f32[512,128]{1,0:T(8,128)} %maximum_convert_fusion.projector_ref), custom_call_target="tpu_custom_call" | custom-call | tf_op jit(solution)/shard_map/density/pallas_call | solution.py:245
  (15 shorter events, 0.1 us)
Async XLA Ops:
  0.6 1.2 copy-start.10
  1.8 11.7 %collective-permute-start.4 = (bf16[2,256,256]{2,1,0:T(8,128)(2,1)S(1)}, bf16[2,256,256]{2,1,0:T(8,128)(2,1)S(1)}, u32[]{:S(2)}, u32[]{:S(2)}) collective-permute-start(bf16[2,256,256]{2,1,0:T(8,128)(2,1)S(1)} %bitcast.32), channel_id=1, source_target_pairs={{0,4},{4,8},{8,12},{12,0},{1,5},{5,9},{9,13},{13,1},{2,6},{6,10},{... | collective-permute-start | bytes 786440 | tf_op jit(solution)/shard_map/ppermute | solution.py:301
  4.0 36.5 %collective-permute-start.5 = (bf16[2,256,256]{2,1,0:T(8,128)(2,1)S(1)}, bf16[2,256,256]{2,1,0:T(8,128)(2,1)S(1)}, u32[]{:S(2)}, u32[]{:S(2)}) collective-permute-start(bf16[2,256,256]{2,1,0:T(8,128)(2,1)S(1)} %bitcast.33), channel_id=1, source_target_pairs={{0,8},{4,12},{8,0},{12,4},{1,9},{5,13},{9,1},{13,5},{2,10},{6,14},... | collective-permute-start | bytes 786440 | tf_op jit(solution)/shard_map/ppermute | solution.py:301
  6.7 39.6 %collective-permute-start = (bf16[2,512,256]{2,1,0:T(8,128)(2,1)S(1)}, bf16[2,512,256]{2,1,0:T(8,128)(2,1)S(1)}, u32[]{:S(2)}, u32[]{:S(2)}) collective-permute-start(bf16[2,512,256]{2,1,0:T(8,128)(2,1)S(1)} %bitcast.24), channel_id=1, source_target_pairs={{0,0},{1,4},{2,8},{3,12},{4,1},{5,5},{6,9},{7,13},{8,2},{9,6},{10,... | collective-permute-start | bytes 1572872 | tf_op jit(solution)/shard_map/ppermute | solution.py:302
  7.4 38.9 %collective-permute-start.1 = (bf16[2,512,256]{2,1,0:T(8,128)(2,1)S(1)}, bf16[2,512,256]{2,1,0:T(8,128)(2,1)S(1)}, u32[]{:S(2)}, u32[]{:S(2)}) collective-permute-start(bf16[2,512,256]{2,1,0:T(8,128)(2,1)S(1)} %bitcast.25), channel_id=1, source_target_pairs={{0,1},{1,5},{2,9},{3,13},{4,2},{5,6},{6,10},{7,14},{8,3},{9,7},{10... | collective-permute-start | bytes 1572872 | tf_op jit(solution)/shard_map/ppermute | solution.py:302
  9.9 36.4 %collective-permute-start.2 = (bf16[2,512,256]{2,1,0:T(8,128)(2,1)S(1)}, bf16[2,512,256]{2,1,0:T(8,128)(2,1)S(1)}, u32[]{:S(2)}, u32[]{:S(2)}) collective-permute-start(bf16[2,512,256]{2,1,0:T(8,128)(2,1)S(1)} %bitcast.26), channel_id=1, source_target_pairs={{0,2},{1,6},{2,10},{3,14},{4,3},{5,7},{6,11},{7,15},{8,0},{9,4},{1... | collective-permute-start | bytes 1572872 | tf_op jit(solution)/shard_map/ppermute | solution.py:302
  13.6 32.7 %collective-permute-start.3 = (bf16[2,512,256]{2,1,0:T(8,128)(2,1)S(1)}, bf16[2,512,256]{2,1,0:T(8,128)(2,1)S(1)}, u32[]{:S(2)}, u32[]{:S(2)}) collective-permute-start(bf16[2,512,256]{2,1,0:T(8,128)(2,1)S(1)} %bitcast.27), channel_id=1, source_target_pairs={{0,3},{1,7},{2,11},{3,15},{4,0},{5,4},{6,8},{7,12},{8,1},{9,5},{10... | collective-permute-start | bytes 1572872 | tf_op jit(solution)/shard_map/ppermute | solution.py:302
  40.5 5.7 %collective-permute-start.6 = (bf16[2,256,256]{2,1,0:T(8,128)(2,1)S(1)}, bf16[2,256,256]{2,1,0:T(8,128)(2,1)}, u32[]{:S(2)}, u32[]{:S(2)}) collective-permute-start(bf16[2,256,256]{2,1,0:T(8,128)(2,1)S(1)} %bitcast.34), channel_id=1, source_target_pairs={{0,12},{4,0},{8,4},{12,8},{1,13},{5,1},{9,5},{13,9},{2,14},{6,2},{... | collective-permute-start | bytes 786440 | tf_op jit(solution)/shard_map/ppermute | solution.py:301
  46.3 0.8 copy-start
  47.1 1.0 copy-start.1
  48.1 16.3 %copy-start.12 = (s32[8192]{0:T(1024)S(1)}, s32[8192]{0:T(1024)}, u32[]{:S(2)}) copy-start(s32[8192]{0:T(1024)} %param.13) | copy-start | bytes 98308
  48.1 16.3 %copy-start.13 = (s32[8192]{0:T(1024)S(1)}, s32[8192]{0:T(1024)}, u32[]{:S(2)}) copy-start(s32[8192]{0:T(1024)} %param.14) | copy-start | bytes 98308
  50.9 0.8 copy-start.6
  51.7 23.4 %collective-permute-start.10 = (bf16[2,512,256]{2,1,0:T(8,128)(2,1)S(1)}, bf16[2,512,256]{2,1,0:T(8,128)(2,1)S(1)}, u32[]{:S(2)}, u32[]{:S(2)}) collective-permute-start(bf16[2,512,256]{2,1,0:T(8,128)(2,1)S(1)} %bitcast.28), channel_id=1, source_target_pairs={{0,4},{4,8},{8,12},{12,0},{1,5},{5,9},{9,13},{13,1},{2,6},{6,10},{... | collective-permute-start | bytes 1572872 | tf_op jit(solution)/shard_map/ppermute | solution.py:317
  64.5 21.9 %collective-permute-start.11 = (bf16[2,512,256]{2,1,0:T(8,128)(2,1)S(1)}, bf16[2,512,256]{2,1,0:T(8,128)(2,1)S(1)}, u32[]{:S(2)}, u32[]{:S(2)}) collective-permute-start(bf16[2,512,256]{2,1,0:T(8,128)(2,1)S(1)} %bitcast.29), channel_id=1, source_target_pairs={{0,8},{4,12},{8,0},{12,4},{1,9},{5,13},{9,1},{13,5},{2,10},{6,14},... | collective-permute-start | bytes 1572872 | tf_op jit(solution)/shard_map/ppermute | solution.py:317
  64.6 23.2 %collective-permute-start.12 = (bf16[2,512,256]{2,1,0:T(8,128)(2,1)S(1)}, bf16[2,512,256]{2,1,0:T(8,128)(2,1)S(1)}, u32[]{:S(2)}, u32[]{:S(2)}) collective-permute-start(bf16[2,512,256]{2,1,0:T(8,128)(2,1)S(1)} %bitcast.30), channel_id=1, source_target_pairs={{0,12},{4,0},{8,4},{12,8},{1,13},{5,1},{9,5},{13,9},{2,14},{6,2},{... | collective-permute-start | bytes 1572872 | tf_op jit(solution)/shard_map/ppermute | solution.py:317
  67.0 21.6 %collective-permute-start.7 = (bf16[2,512,256]{2,1,0:T(8,128)(2,1)S(1)}, bf16[2,512,256]{2,1,0:T(8,128)(2,1)S(1)}, u32[]{:S(2)}, u32[]{:S(2)}) collective-permute-start(bf16[2,512,256]{2,1,0:T(8,128)(2,1)S(1)} %get-tuple-element.13.c0), channel_id=1, source_target_pairs={{0,1},{1,2},{2,3},{3,0},{4,5},{5,6},{6,7},{7,4},{8,9},{9,10},{10,1... | collective-permute-start | bytes 1572872 | tf_op jit(solution)/shard_map/ppermute | solution.py:315
  67.0 26.3 %collective-permute-start.8 = (bf16[2,512,256]{2,1,0:T(8,128)(2,1)S(1)}, bf16[2,512,256]{2,1,0:T(8,128)(2,1)}, u32[]{:S(2)}, u32[]{:S(2)}) collective-permute-start(bf16[2,512,256]{2,1,0:T(8,128)(2,1)S(1)} %get-tuple-element.13.c0), channel_id=1, source_target_pairs={{0,2},{1,3},{2,0},{3,1},{4,6},{5,7},{6,4},{7,5},{8,10},{9,11},{10,... | collective-permute-start | bytes 1572872 | tf_op jit(solution)/shard_map/ppermute | solution.py:315
  75.2 18.1 %collective-permute-start.9 = (bf16[2,512,256]{2,1,0:T(8,128)(2,1)S(1)}, bf16[2,512,256]{2,1,0:T(8,128)(2,1)}, u32[]{:S(2)}, u32[]{:S(2)}) collective-permute-start(bf16[2,512,256]{2,1,0:T(8,128)(2,1)S(1)} %get-tuple-element.13.c0), channel_id=1, source_target_pairs={{0,3},{1,0},{2,1},{3,2},{4,7},{5,4},{6,5},{7,6},{8,11},{9,8},{10,9... | collective-permute-start | bytes 1572872 | tf_op jit(solution)/shard_map/ppermute | solution.py:315
  75.8 17.5 %copy-start.7 = (bf16[512,512]{1,0:T(8,128)(2,1)S(1)}, bf16[512,512]{1,0:T(8,128)(2,1)}, u32[]{:S(2)}) copy-start(bf16[512,512]{1,0:T(8,128)(2,1)} %copy-done.6) | copy-start | bytes 1572868
  87.9 0.8 copy-start.2
  88.7 0.8 copy-start.4
  93.3 1.0 copy-start.3
  94.4 1.0 copy-start.5
  108.7 23.2 %all-to-all-start = ((bf16[16,80,128]{2,1,0:T(8,128)(2,1)}), bf16[16,80,128]{2,1,0:T(8,128)(2,1)S(1)}, u32[]{:S(2)}, u32[]{:S(2)}) async-start(bf16[16,80,128]{2,1,0:T(8,128)(2,1)} %get-tuple-element.17), calls=%async_computation | async-start | bytes 655360 | tf_op jit(solution)/shard_map/all_to_all | solution.py:324
  118.9 21.7 %copy-start.11 = (bf16[512,64]{0,1:T(8,128)(2,1)S(1)}, bf16[512,64]{0,1:T(8,128)(2,1)}, u32[]{:S(2)}) copy-start(bf16[512,64]{0,1:T(8,128)(2,1)} %param.15) | copy-start | bytes 196612
  131.9 0.7 copy-start.9
  134.7 18.0 %all-to-all-start.1 = ((f32[16,64,128]{2,1,0:T(8,128)}), f32[16,64,128]{2,1,0:T(8,128)S(1)}, u32[]{:S(2)}, u32[]{:S(2)}) async-start(f32[16,64,128]{2,1,0:T(8,128)} %pole_sum.1), calls=%async_computation.1 | async-start | bytes 1048576 | tf_op jit(solution)/shard_map/all_to_all | solution.py:327
  152.7 0.8 copy-start.8

commit v3 on v2

--- a/solution.py
+++ b/solution.py
@@ -12,6 +12,7 @@
 ROWS = 4
 COLS = 4
 SLOTS = 64
+GROUP = 32
 MIB = 1 << 20
 
 
@@ -89,7 +90,7 @@
                 pl.BlockSpec((2 * columns, tile), lambda i, *_: (0, i)),
             ),
         ),
-        compiler_params=pltpu.CompilerParams(vmem_limit_bytes=24 * MIB),
+        compiler_params=pltpu.CompilerParams(vmem_limit_bytes=14 * MIB),
         cost_estimate=pl.CostEstimate(
             flops=2 * rows * inner * 16 * columns, bytes_accessed=6 << 20, transcendentals=0
         ),
@@ -98,16 +99,29 @@
 
 
 def take_pairs(codes_ref, mask_ref, pairs_ref, table, lanes, spread, keep, fold):
-    @pl.loop(0, pairs_ref.shape[0])
-    def _(owner):
-        for s in range(SLOTS):
-            code = codes_ref[owner * SLOTS + s]
+    owners = pairs_ref.shape[0]
+
+    @pl.loop(0, owners * SLOTS // GROUP)
+    def _(group):
+        first = group * GROUP
+        to = pl.multiple_of(first * 16, GROUP * 16)
+        for s in range(GROUP):
+            code = codes_ref[first + s]
             found = table[pl.ds(pl.multiple_of(code & ~15, 16), 16), :]
-            lanes[s * 16 : s * 16 + 16, :] = found * mask_ref[code & 15]
-        wide = product(lanes[...], spread[...], 0).reshape(SLOTS, 2, 8, 2 * B * B)
-        wide = wide * keep[...][None]
-        wide = (wide[:, 0] + wide[:, 1]).reshape(SLOTS * 8, 2 * B * B).astype(jnp.bfloat16)
-        pairs_ref[owner, :SLOTS, :] = product(fold[...], wide, 0).astype(jnp.bfloat16)
+            lanes[pl.ds(to + s * 16, 16), :] = found * mask_ref[code & 15]
+
+    many = 4
+
+    @pl.loop(0, owners // many)
+    def _(chunk):
+        rows = many * SLOTS * 16
+        wide = product(lanes[pl.ds(pl.multiple_of(chunk * rows, rows), rows), :], spread[...], 0)
+        wide = wide.reshape(many * SLOTS, 2, 8, 2 * B * B) * keep[...][None]
+        wide = (wide[:, 0] + wide[:, 1]).reshape(many, SLOTS * 8, 2 * B * B).astype(jnp.bfloat16)
+        for o in range(many):
+            pairs_ref[chunk * many + o, :SLOTS, :] = product(fold[...], wide[o], 0).astype(
+                jnp.bfloat16
+            )
 
 
 def block_kernel(
@@ -182,13 +196,13 @@
             out_specs=(row_spec(columns), whole((owners, SLOTS + 16, 2 * B * B))),
             scratch_shapes=[
                 pltpu.VMEM((4 * (2 * rows + coupling_t.shape[0]), 128), jnp.bfloat16),
-                pltpu.VMEM((SLOTS * 16, 128), jnp.bfloat16),
+                pltpu.VMEM((owners * SLOTS * 16, 128), jnp.bfloat16),
                 pltpu.VMEM((128, 128), jnp.bfloat16),
                 pltpu.VMEM((2, 8, 128), jnp.float32),
                 pltpu.VMEM((SLOTS, SLOTS * 8), jnp.bfloat16),
             ],
         ),
-        compiler_params=pltpu.CompilerParams(vmem_limit_bytes=40 * MIB),
+        compiler_params=pltpu.CompilerParams(vmem_limit_bytes=24 * MIB),
         cost_estimate=pl.CostEstimate(
             flops=2 * rows * inner * 16 * columns, bytes_accessed=12 << 20, transcendentals=0
         ),
@@ -223,22 +237,25 @@
 def pole_sum_call(weights, parts, copies):
     return pl.pallas_call(
         pole_sum_kernel,
-        out_shape=jax.ShapeDtypeStruct((copies, SLOTS, 2 * B * B), jnp.float32),
+        out_shape=jax.ShapeDtypeStruct((copies, SLOTS, 2 * B * B), jnp.bfloat16),
         in_specs=[pl.BlockSpec(memory_space=pltpu.VMEM)] * 2,
         out_specs=pl.BlockSpec(memory_space=pltpu.VMEM),
+        compiler_params=pltpu.CompilerParams(vmem_limit_bytes=6 * MIB),
         name="pole_sum",
     )(weights, parts)
 
 
-def density_kernel(index_ref, sums_ref, projector_ref, out_ref):
-    @pl.loop(0, out_ref.shape[0] // 16)
+def density_kernel(index_ref, sums_ref, projector_ref, out_ref, sums):
+    sums[...] = sums_ref[...].astype(jnp.float32)
+
+    @pl.loop(0, out_ref.shape[0] // 32)
     def _(group):
-        first = pl.multiple_of(group * 16, 16)
-        for s in range(16):
+        first = pl.multiple_of(group * 32, 32)
+        for s in range(32):
             q = first + s
-            out_ref[pl.ds(q, 1), :] = sums_ref[pl.ds(index_ref[q], 1), :]
-        here = pl.ds(first, 16)
-        out_ref[here, :] = out_ref[here, :] * projector_ref[here, :]
+            out_ref[pl.ds(q, 1), :] = sums[pl.ds(index_ref[q], 1), :]
+
+    out_ref[...] = out_ref[...] * projector_ref[...]
 
 
 def density_call(index, sums, projector):
@@ -248,6 +265,8 @@
         in_specs=[pl.BlockSpec(memory_space=pltpu.SMEM)]
         + [pl.BlockSpec(memory_space=pltpu.VMEM)] * 2,
         out_specs=pl.BlockSpec(memory_space=pltpu.VMEM),
+        scratch_shapes=[pltpu.VMEM(sums.shape, jnp.float32)],
+        compiler_params=pltpu.CompilerParams(vmem_limit_bytes=6 * MIB),
         name="density",
     )(index, sums, projector)
 

time: 157 us -> 150 us (0.955)
  Pallas kernels: 20.6 us -> 16.4 us
  waiting for transfers between devices: 68.8 us -> 66.5 us
  local copies, waits for them, and re-layouts: 12.7 us -> 14.5 us
    unnamed x33 -> x39, local copies, waits for them, and re-layouts: 12.6 us -> 14.4 us
    pallas_call x1, Pallas kernels: 13.3 us -> 11.7 us  [block_call(): pl.pallas_call(block_kernel, out_shape=(jax.ShapeDtypeStruct((2, rows, co...]
  transfers between devices with their start and end apart: 15 -> 15, of which waited for: 8 -> 8; matrix products, arithmetic and copies ran while one was open for 4% -> 3% of each run, Pallas kernels for 0% -> 0%
where the time goes in v3:
time: 150 us
  waiting for transfers between devices  66.5 us (44%)
  starting transfers between devices  49.7 us (33%)
  Pallas kernels  16.4 us (11%)
  local copies, waits for them, and re-layouts  14.5 us (10%)
    ppermute x3, waiting for transfers between devices, local(): lax.ppermute(trail, 'row', ring(e, ROWS))  28.7 us
    ppermute x3, starting transfers between devices, local(): lax.ppermute(lower_late, 'row', ring(e, ROWS))  14.8 us
    unnamed x39, local copies, waits for them, and re-layouts  14.4 us
    ppermute x3, waiting for transfers between devices, local(): lax.ppermute(lower_late, 'row', ring(e, ROWS))  14.3 us
    all_to_all x1, waiting for transfers between devices, local(): parts = lax.all_to_all(pairs, POLE, 0, 0, tiled=True)  12.7 us
    pallas_call x1, Pallas kernels, block_call(): pl.pallas_call(block_kernel, out_shape=(jax.ShapeDtypeStruct((2, rows, co...  11.7 us
    ppermute x4, starting transfers between devices, local(): lax.ppermute(lower, ('row', 'col'), to_process_rows(d))  10.4 us
    all_to_all x1, starting transfers between devices, local(): parts = lax.all_to_all(pairs, POLE, 0, 0, tiled=True)  10.1 us
  transfers between devices with their start and end apart: 15, of which 8 were waited for; matrix products, arithmetic and copies ran while one was open for 3% of the time, Pallas kernels for 0%

profile of v3, /device:TPU:1, one launch (start us, length us, event | category | flops | bytes accessed | tf_op | source)
XLA Modules:
  0.0 149.6 jit_solution(5297888854793962576)
XLA Ops:
  0.6 0.0 copy-start.13
  0.6 1.2 copy.26
  1.8 0.0 copy-done.13
  1.8 2.2 %collective-permute-start.4 = (bf16[2,256,256]{2,1,0:T(8,128)(2,1)S(1)}, bf16[2,256,256]{2,1,0:T(8,128)(2,1)S(1)}, u32[]{:S(2)}, u32[]{:S(2)}) collective-permute-start(bf16[2,256,256]{2,1,0:T(8,128)(2,1)S(1)} %bitcast.33), channel_id=1, source_target_pairs={{0,4},{4,8},{8,12},{12,0},{1,5},{5,9},{9,13},{13,1},{2,6},{6,10},{... | collective-permute-start | bytes 786440 | tf_op jit(solution)/shard_map/ppermute | solution.py:320
  4.0 2.6 %collective-permute-start.5 = (bf16[2,256,256]{2,1,0:T(8,128)(2,1)S(1)}, bf16[2,256,256]{2,1,0:T(8,128)(2,1)S(1)}, u32[]{:S(2)}, u32[]{:S(2)}) collective-permute-start(bf16[2,256,256]{2,1,0:T(8,128)(2,1)S(1)} %bitcast.34), channel_id=1, source_target_pairs={{0,8},{4,12},{8,0},{12,4},{1,9},{5,13},{9,1},{13,5},{2,10},{6,14},... | collective-permute-start | bytes 786440 | tf_op jit(solution)/shard_map/ppermute | solution.py:320
  6.7 0.7 collective-permute-start
  7.4 2.5 %collective-permute-start.1 = (bf16[2,512,256]{2,1,0:T(8,128)(2,1)S(1)}, bf16[2,512,256]{2,1,0:T(8,128)(2,1)S(1)}, u32[]{:S(2)}, u32[]{:S(2)}) collective-permute-start(bf16[2,512,256]{2,1,0:T(8,128)(2,1)S(1)} %bitcast.26), channel_id=1, source_target_pairs={{0,1},{1,5},{2,9},{3,13},{4,2},{5,6},{6,10},{7,14},{8,3},{9,7},{10... | collective-permute-start | bytes 1572872 | tf_op jit(solution)/shard_map/ppermute | solution.py:321
  9.9 3.7 %collective-permute-start.2 = (bf16[2,512,256]{2,1,0:T(8,128)(2,1)S(1)}, bf16[2,512,256]{2,1,0:T(8,128)(2,1)S(1)}, u32[]{:S(2)}, u32[]{:S(2)}) collective-permute-start(bf16[2,512,256]{2,1,0:T(8,128)(2,1)S(1)} %bitcast.27), channel_id=1, source_target_pairs={{0,2},{1,6},{2,10},{3,14},{4,3},{5,7},{6,11},{7,15},{8,0},{9,4},{1... | collective-permute-start | bytes 1572872 | tf_op jit(solution)/shard_map/ppermute | solution.py:321
  13.6 0.0 collective-permute-done.4.t1
  13.6 3.5 %collective-permute-start.3 = (bf16[2,512,256]{2,1,0:T(8,128)(2,1)S(1)}, bf16[2,512,256]{2,1,0:T(8,128)(2,1)S(1)}, u32[]{:S(2)}, u32[]{:S(2)}) collective-permute-start(bf16[2,512,256]{2,1,0:T(8,128)(2,1)S(1)} %bitcast.28), channel_id=1, source_target_pairs={{0,3},{1,7},{2,11},{3,15},{4,0},{5,4},{6,8},{7,12},{8,1},{9,5},{10... | collective-permute-start | bytes 1572872 | tf_op jit(solution)/shard_map/ppermute | solution.py:321
  17.1 23.5 %collective-permute-done.5.t2 = bf16[2,256,256]{2,1,0:T(8,128)(2,1)S(1)} collective-permute-done((bf16[2,256,256]{2,1,0:T(8,128)(2,1)S(1)}, bf16[2,256,256]{2,1,0:T(8,128)(2,1)S(1)}, u32[]{:S(2)}, u32[]{:S(2)}) %collective-permute-start.5) | collective-permute-done | bytes 262176 | tf_op jit(solution)/shard_map/ppermute | solution.py:320
  40.5 0.7 copy-done.7
  41.2 0.0 collective-permute-start.6
  41.2 5.2 %collective-permute-done.6.t3 = bf16[2,256,256]{2,1,0:T(8,128)(2,1)S(1)} collective-permute-done((bf16[2,256,256]{2,1,0:T(8,128)(2,1)S(1)}, bf16[2,256,256]{2,1,0:T(8,128)(2,1)S(1)}, u32[]{:S(2)}, u32[]{:S(2)}) %collective-permute-start.6) | collective-permute-done | bytes 262176 | tf_op jit(solution)/shard_map/ppermute | solution.py:320
  46.5 0.7 copy-done.9
  47.2 0.0 collective-permute-done.l0
  47.2 0.0 collective-permute-done.1.l1
  47.2 0.0 collective-permute-done.2.l2
  47.2 0.0 collective-permute-done.3.l3
  47.2 0.0 copy-start.1
  47.2 0.8 copy-done.1
  48.0 1.0 copy-done.2
  49.0 0.9 copy-done.8
  50.0 0.9 copy-done.10
  50.9 1.9 %coupling.1 = (bf16[2,512,256]{2,1,0:T(8,128)(2,1)S(1)}, bf16[512,512]{1,0:T(8,128)(2,1)S(1)}) custom-call(s32[1]{0:T(128)} %bitcast.base_ref, bf16[2,512,256]{2,1,0:T(8,128)(2,1)S(1)} %collective-permute-done.l0, bf16[2,512,256]{2,1,0:T(8,128)(2,1)S(1)} %collective-permute-done.1.l1, bf16[2,512,256]{2,1,0:T(8,128)(2,1)S(1)} %collective-permute-done.2.l2, ...), custom_call_target="tpu_custom_call" | custom-call | flops 1073741824 | bytes 6291456 | tf_op jit(solution)/shard_map/coupling/pallas_call | solution.py:78
  52.9 0.0 copy-start.11
  52.9 0.8 copy-done.11
  53.7 12.3 %collective-permute-start.10 = (bf16[2,512,256]{2,1,0:T(8,128)(2,1)S(1)}, bf16[2,512,256]{2,1,0:T(8,128)(2,1)S(1)}, u32[]{:S(2)}, u32[]{:S(2)}) collective-permute-start(bf16[2,512,256]{2,1,0:T(8,128)(2,1)S(1)} %bitcast.29), channel_id=1, source_target_pairs={{0,4},{4,8},{8,12},{12,0},{1,5},{5,9},{9,13},{13,1},{2,6},{6,10},{... | collective-permute-start | bytes 1572872 | tf_op jit(solution)/shard_map/ppermute | solution.py:336
  66.0 0.0 copy-done.15
  66.0 0.0 copy-done.16
  66.1 0.1 fusion.5
  66.2 0.1 collective-permute-start.11
  66.3 2.4 %collective-permute-start.12 = (bf16[2,512,256]{2,1,0:T(8,128)(2,1)S(1)}, bf16[2,512,256]{2,1,0:T(8,128)(2,1)S(1)}, u32[]{:S(2)}, u32[]{:S(2)}) collective-permute-start(bf16[2,512,256]{2,1,0:T(8,128)(2,1)S(1)} %bitcast.31), channel_id=1, source_target_pairs={{0,12},{4,0},{8,4},{12,8},{1,13},{5,1},{9,5},{13,9},{2,14},{6,2},{... | collective-permute-start | bytes 1572872 | tf_op jit(solution)/shard_map/ppermute | solution.py:336
  68.7 0.0 collective-permute-start.7
  68.7 3.7 %collective-permute-start.8 = (bf16[2,512,256]{2,1,0:T(8,128)(2,1)S(1)}, bf16[2,512,256]{2,1,0:T(8,128)(2,1)}, u32[]{:S(2)}, u32[]{:S(2)}) collective-permute-start(bf16[2,512,256]{2,1,0:T(8,128)(2,1)S(1)} %get-tuple-element.13.c0), channel_id=1, source_target_pairs={{0,2},{1,3},{2,0},{3,1},{4,6},{5,7},{6,4},{7,5},{8,10},{9,11},{10,... | collective-permute-start | bytes 1572872 | tf_op jit(solution)/shard_map/ppermute | solution.py:334
  72.4 4.4 %collective-permute-done.10.l1 = bf16[2,512,256]{2,1,0:T(8,128)(2,1)S(1)} collective-permute-done((bf16[2,512,256]{2,1,0:T(8,128)(2,1)S(1)}, bf16[2,512,256]{2,1,0:T(8,128)(2,1)S(1)}, u32[]{:S(2)}, u32[]{:S(2)}) %collective-permute-start.10) | collective-permute-done | bytes 524320 | tf_op jit(solution)/shard_map/ppermute | solution.py:336
  76.8 0.0 collective-permute-start.9
  76.8 0.2 fusion
  77.0 0.4 select_reduce_fusion
  77.4 0.1 reshape.118.codes_ref
  77.5 1.5 copy.25
  79.6 8.7 %collective-permute-done.11.l2 = bf16[2,512,256]{2,1,0:T(8,128)(2,1)S(1)} collective-permute-done((bf16[2,512,256]{2,1,0:T(8,128)(2,1)S(1)}, bf16[2,512,256]{2,1,0:T(8,128)(2,1)S(1)}, u32[]{:S(2)}, u32[]{:S(2)}) %collective-permute-start.11) | collective-permute-done | bytes 524320 | tf_op jit(solution)/shard_map/ppermute | solution.py:336
  88.3 1.2 collective-permute-done.12.l3
  89.5 0.8 copy-done.3
  90.3 0.0 collective-permute-done.7.c1
  90.3 0.8 copy-done.5
  91.1 3.8 %collective-permute-done.8.c2 = bf16[2,512,256]{2,1,0:T(8,128)(2,1)} collective-permute-done((bf16[2,512,256]{2,1,0:T(8,128)(2,1)S(1)}, bf16[2,512,256]{2,1,0:T(8,128)(2,1)}, u32[]{:S(2)}, u32[]{:S(2)}) %collective-permute-start.8) | collective-permute-done | bytes 524320 | tf_op jit(solution)/shard_map/ppermute | solution.py:334
  95.0 0.0 collective-permute-done.9.c3
  95.0 0.0 copy-done.12
  95.0 1.0 copy-done.4
  96.0 1.0 copy-done.6
  97.1 11.7 %block_and_pairs.1 = (bf16[2,512,512]{2,1,0:T(8,128)(2,1)S(1)}, bf16[16,80,128]{2,1,0:T(8,128)(2,1)}) custom-call(s32[1]{0:T(128)} %bitcast.base_ref, s32[1]{0:T(128)S(6)} %copy.28.slot_ref, s32[1024]{0:T(1024)S(1)} %reshape.118.codes_ref, bf16[2,512,256]{2,1,0:T(8,128)(2,1)S(1)} %get-tuple-element.13.c0, bf16[2,512,256]{2,1,0:T(8,128)(2,1)S(1)} %copy-done.6, ...), custom_call_target="tpu_custom_call" | custom-call | flops 2147483648 | bytes 12582912 | tf_op jit(solution)/shard_map/block_and_pairs/pallas_call | solution.py:184
  108.8 10.1 %all-to-all-start = ((bf16[16,80,128]{2,1,0:T(8,128)(2,1)}), bf16[16,80,128]{2,1,0:T(8,128)(2,1)S(1)}, u32[]{:S(2)}, u32[]{:S(2)}) async-start(bf16[16,80,128]{2,1,0:T(8,128)(2,1)} %get-tuple-element.17), calls=%async_computation | async-start | bytes 655360 | tf_op jit(solution)/shard_map/all_to_all | solution.py:343
  118.9 0.0 copy-done.14
  118.9 0.1 copy.19
  119.1 0.2 convert_reduce_fusion
  119.3 12.7 %all-to-all-done.parts_ref = bf16[16,80,128]{2,1,0:T(8,128)(2,1)S(1)} async-done(((bf16[16,80,128]{2,1,0:T(8,128)(2,1)}), bf16[16,80,128]{2,1,0:T(8,128)(2,1)S(1)}, u32[]{:S(2)}, u32[]{:S(2)}) %all-to-all-start) | async-done | bytes 327712 | tf_op jit(solution)/shard_map/all_to_all | solution.py:343
  132.0 0.0 copy-done
  132.0 0.9 pole_sum.1
  132.9 5.8 %all-to-all-start.1 = ((bf16[16,64,128]{2,1,0:T(8,128)(2,1)}), bf16[16,64,128]{2,1,0:T(8,128)(2,1)S(1)}, u32[]{:S(2)}, u32[]{:S(2)}) async-start(bf16[16,64,128]{2,1,0:T(8,128)(2,1)} %pole_sum.1), calls=%async_computation.1 | async-start | bytes 524288 | tf_op jit(solution)/shard_map/all_to_all | solution.py:346
  138.8 0.1 maximum_convert_fusion.projector_ref
  138.9 2.0 %copy.21 = bf16[1,512,2,512]{3,2,1,0:T(2,128)(2,1)} copy(bf16[1,512,2,512]{3,1,2,0:T(8,128)(2,1)S(1)} %bitcast.23) | data formatting | bytes 2097152
  140.9 6.9 %all-to-all-done.1 = bf16[16,64,128]{2,1,0:T(8,128)(2,1)S(1)} async-done(((bf16[16,64,128]{2,1,0:T(8,128)(2,1)}), bf16[16,64,128]{2,1,0:T(8,128)(2,1)S(1)}, u32[]{:S(2)}, u32[]{:S(2)}) %all-to-all-start.1) | async-done | bytes 262176 | tf_op jit(solution)/shard_map/all_to_all | solution.py:346
  147.8 1.8 %density.1 = f32[512,128]{1,0:T(8,128)} custom-call(s32[512]{0:T(512)S(1)} %multiply_add_fusion.index_ref, bf16[1024,128]{1,0:T(8,128)(2,1)S(1)} %bitcast.22, f32[512,128]{1,0:T(8,128)S(1)} %maximum_convert_fusion.projector_ref), custom_call_target="tpu_custom_call" | custom-call | tf_op jit(solution)/shard_map/density/pallas_call | solution.py:262
  (21 shorter events, 0.1 us)
Async XLA Ops:
  0.6 1.2 copy-start.13
  1.8 11.7 %collective-permute-start.4 = (bf16[2,256,256]{2,1,0:T(8,128)(2,1)S(1)}, bf16[2,256,256]{2,1,0:T(8,128)(2,1)S(1)}, u32[]{:S(2)}, u32[]{:S(2)}) collective-permute-start(bf16[2,256,256]{2,1,0:T(8,128)(2,1)S(1)} %bitcast.33), channel_id=1, source_target_pairs={{0,4},{4,8},{8,12},{12,0},{1,5},{5,9},{9,13},{13,1},{2,6},{6,10},{... | collective-permute-start | bytes 786440 | tf_op jit(solution)/shard_map/ppermute | solution.py:320
  4.0 36.5 %collective-permute-start.5 = (bf16[2,256,256]{2,1,0:T(8,128)(2,1)S(1)}, bf16[2,256,256]{2,1,0:T(8,128)(2,1)S(1)}, u32[]{:S(2)}, u32[]{:S(2)}) collective-permute-start(bf16[2,256,256]{2,1,0:T(8,128)(2,1)S(1)} %bitcast.34), channel_id=1, source_target_pairs={{0,8},{4,12},{8,0},{12,4},{1,9},{5,13},{9,1},{13,5},{2,10},{6,14},... | collective-permute-start | bytes 786440 | tf_op jit(solution)/shard_map/ppermute | solution.py:320
  6.7 40.5 %collective-permute-start = (bf16[2,512,256]{2,1,0:T(8,128)(2,1)S(1)}, bf16[2,512,256]{2,1,0:T(8,128)(2,1)S(1)}, u32[]{:S(2)}, u32[]{:S(2)}) collective-permute-start(bf16[2,512,256]{2,1,0:T(8,128)(2,1)S(1)} %bitcast.25), channel_id=1, source_target_pairs={{0,0},{1,4},{2,8},{3,12},{4,1},{5,5},{6,9},{7,13},{8,2},{9,6},{10,... | collective-permute-start | bytes 1572872 | tf_op jit(solution)/shard_map/ppermute | solution.py:321
  7.4 39.8 %collective-permute-start.1 = (bf16[2,512,256]{2,1,0:T(8,128)(2,1)S(1)}, bf16[2,512,256]{2,1,0:T(8,128)(2,1)S(1)}, u32[]{:S(2)}, u32[]{:S(2)}) collective-permute-start(bf16[2,512,256]{2,1,0:T(8,128)(2,1)S(1)} %bitcast.26), channel_id=1, source_target_pairs={{0,1},{1,5},{2,9},{3,13},{4,2},{5,6},{6,10},{7,14},{8,3},{9,7},{10... | collective-permute-start | bytes 1572872 | tf_op jit(solution)/shard_map/ppermute | solution.py:321
  9.9 37.3 %collective-permute-start.2 = (bf16[2,512,256]{2,1,0:T(8,128)(2,1)S(1)}, bf16[2,512,256]{2,1,0:T(8,128)(2,1)S(1)}, u32[]{:S(2)}, u32[]{:S(2)}) collective-permute-start(bf16[2,512,256]{2,1,0:T(8,128)(2,1)S(1)} %bitcast.27), channel_id=1, source_target_pairs={{0,2},{1,6},{2,10},{3,14},{4,3},{5,7},{6,11},{7,15},{8,0},{9,4},{1... | collective-permute-start | bytes 1572872 | tf_op jit(solution)/shard_map/ppermute | solution.py:321
  13.6 33.6 %collective-permute-start.3 = (bf16[2,512,256]{2,1,0:T(8,128)(2,1)S(1)}, bf16[2,512,256]{2,1,0:T(8,128)(2,1)S(1)}, u32[]{:S(2)}, u32[]{:S(2)}) collective-permute-start(bf16[2,512,256]{2,1,0:T(8,128)(2,1)S(1)} %bitcast.28), channel_id=1, source_target_pairs={{0,3},{1,7},{2,11},{3,15},{4,0},{5,4},{6,8},{7,12},{8,1},{9,5},{10... | collective-permute-start | bytes 1572872 | tf_op jit(solution)/shard_map/ppermute | solution.py:321
  40.5 0.7 copy-start.7
  41.2 5.2 %collective-permute-start.6 = (bf16[2,256,256]{2,1,0:T(8,128)(2,1)S(1)}, bf16[2,256,256]{2,1,0:T(8,128)(2,1)S(1)}, u32[]{:S(2)}, u32[]{:S(2)}) collective-permute-start(bf16[2,256,256]{2,1,0:T(8,128)(2,1)S(1)} %bitcast.35), channel_id=1, source_target_pairs={{0,12},{4,0},{8,4},{12,8},{1,13},{5,1},{9,5},{13,9},{2,14},{6,2},{... | collective-permute-start | bytes 786440 | tf_op jit(solution)/shard_map/ppermute | solution.py:320
  46.5 0.7 copy-start.9
  47.2 0.8 copy-start.1
  48.0 1.0 copy-start.2
  49.0 0.9 copy-start.8
  50.0 0.9 copy-start.10
  50.9 15.1 %copy-start.15 = (s32[8192]{0:T(1024)S(1)}, s32[8192]{0:T(1024)}, u32[]{:S(2)}) copy-start(s32[8192]{0:T(1024)} %param.13) | copy-start | bytes 98308
  50.9 15.1 %copy-start.16 = (s32[8192]{0:T(1024)S(1)}, s32[8192]{0:T(1024)}, u32[]{:S(2)}) copy-start(s32[8192]{0:T(1024)} %param.14) | copy-start | bytes 98308
  52.9 0.8 copy-start.11
  53.7 23.1 %collective-permute-start.10 = (bf16[2,512,256]{2,1,0:T(8,128)(2,1)S(1)}, bf16[2,512,256]{2,1,0:T(8,128)(2,1)S(1)}, u32[]{:S(2)}, u32[]{:S(2)}) collective-permute-start(bf16[2,512,256]{2,1,0:T(8,128)(2,1)S(1)} %bitcast.29), channel_id=1, source_target_pairs={{0,4},{4,8},{8,12},{12,0},{1,5},{5,9},{9,13},{13,1},{2,6},{6,10},{... | collective-permute-start | bytes 1572872 | tf_op jit(solution)/shard_map/ppermute | solution.py:336
  66.2 22.1 %collective-permute-start.11 = (bf16[2,512,256]{2,1,0:T(8,128)(2,1)S(1)}, bf16[2,512,256]{2,1,0:T(8,128)(2,1)S(1)}, u32[]{:S(2)}, u32[]{:S(2)}) collective-permute-start(bf16[2,512,256]{2,1,0:T(8,128)(2,1)S(1)} %bitcast.30), channel_id=1, source_target_pairs={{0,8},{4,12},{8,0},{12,4},{1,9},{5,13},{9,1},{13,5},{2,10},{6,14},... | collective-permute-start | bytes 1572872 | tf_op jit(solution)/shard_map/ppermute | solution.py:336
  66.3 23.2 %collective-permute-start.12 = (bf16[2,512,256]{2,1,0:T(8,128)(2,1)S(1)}, bf16[2,512,256]{2,1,0:T(8,128)(2,1)S(1)}, u32[]{:S(2)}, u32[]{:S(2)}) collective-permute-start(bf16[2,512,256]{2,1,0:T(8,128)(2,1)S(1)} %bitcast.31), channel_id=1, source_target_pairs={{0,12},{4,0},{8,4},{12,8},{1,13},{5,1},{9,5},{13,9},{2,14},{6,2},{... | collective-permute-start | bytes 1572872 | tf_op jit(solution)/shard_map/ppermute | solution.py:336
  68.7 21.6 %collective-permute-start.7 = (bf16[2,512,256]{2,1,0:T(8,128)(2,1)S(1)}, bf16[2,512,256]{2,1,0:T(8,128)(2,1)S(1)}, u32[]{:S(2)}, u32[]{:S(2)}) collective-permute-start(bf16[2,512,256]{2,1,0:T(8,128)(2,1)S(1)} %get-tuple-element.13.c0), channel_id=1, source_target_pairs={{0,1},{1,2},{2,3},{3,0},{4,5},{5,6},{6,7},{7,4},{8,9},{9,10},{10,1... | collective-permute-start | bytes 1572872 | tf_op jit(solution)/shard_map/ppermute | solution.py:334
  68.7 26.3 %collective-permute-start.8 = (bf16[2,512,256]{2,1,0:T(8,128)(2,1)S(1)}, bf16[2,512,256]{2,1,0:T(8,128)(2,1)}, u32[]{:S(2)}, u32[]{:S(2)}) collective-permute-start(bf16[2,512,256]{2,1,0:T(8,128)(2,1)S(1)} %get-tuple-element.13.c0), channel_id=1, source_target_pairs={{0,2},{1,3},{2,0},{3,1},{4,6},{5,7},{6,4},{7,5},{8,10},{9,11},{10,... | collective-permute-start | bytes 1572872 | tf_op jit(solution)/shard_map/ppermute | solution.py:334
  76.8 18.1 %collective-permute-start.9 = (bf16[2,512,256]{2,1,0:T(8,128)(2,1)S(1)}, bf16[2,512,256]{2,1,0:T(8,128)(2,1)}, u32[]{:S(2)}, u32[]{:S(2)}) collective-permute-start(bf16[2,512,256]{2,1,0:T(8,128)(2,1)S(1)} %get-tuple-element.13.c0), channel_id=1, source_target_pairs={{0,3},{1,0},{2,1},{3,2},{4,7},{5,4},{6,5},{7,6},{8,11},{9,8},{10,9... | collective-permute-start | bytes 1572872 | tf_op jit(solution)/shard_map/ppermute | solution.py:334
  77.5 17.5 %copy-start.12 = (bf16[512,512]{1,0:T(8,128)(2,1)S(1)}, bf16[512,512]{1,0:T(8,128)(2,1)}, u32[]{:S(2)}) copy-start(bf16[512,512]{1,0:T(8,128)(2,1)} %copy-done.11) | copy-start | bytes 1572868
  89.5 0.8 copy-start.3
  90.3 0.8 copy-start.5
  95.0 1.0 copy-start.4
  96.0 1.0 copy-start.6
  97.1 21.9 %copy-start.14 = (bf16[512,64]{0,1:T(8,128)(2,1)S(1)}, bf16[512,64]{0,1:T(8,128)(2,1)}, u32[]{:S(2)}) copy-start(bf16[512,64]{0,1:T(8,128)(2,1)} %param.15) | copy-start | bytes 196612
  97.1 34.9 %copy-start = (f32[256,2]{0,1:T(2,128)S(1)}, f32[256,2]{0,1:T(2,128)}, u32[]{:S(2)}) copy-start(f32[256,2]{0,1:T(2,128)} %param.11) | copy-start | bytes 6148
  108.8 23.2 %all-to-all-start = ((bf16[16,80,128]{2,1,0:T(8,128)(2,1)}), bf16[16,80,128]{2,1,0:T(8,128)(2,1)S(1)}, u32[]{:S(2)}, u32[]{:S(2)}) async-start(bf16[16,80,128]{2,1,0:T(8,128)(2,1)} %get-tuple-element.17), calls=%async_computation | async-start | bytes 655360 | tf_op jit(solution)/shard_map/all_to_all | solution.py:343
  132.9 14.9 %all-to-all-start.1 = ((bf16[16,64,128]{2,1,0:T(8,128)(2,1)}), bf16[16,64,128]{2,1,0:T(8,128)(2,1)S(1)}, u32[]{:S(2)}, u32[]{:S(2)}) async-start(bf16[16,64,128]{2,1,0:T(8,128)(2,1)} %pole_sum.1), calls=%async_computation.1 | async-start | bytes 524288 | tf_op jit(solution)/shard_map/all_to_all | solution.py:346

commit v4 on v3

--- a/solution.py
+++ b/solution.py
@@ -20,9 +20,15 @@
     return [(i, (i + shift) % peers) for i in range(peers)]
 
 
-def to_process_rows(shift):
+def along_row(e):
     return [
-        (k * COLS + x, x * COLS + (k + shift) % COLS) for k in range(ROWS) for x in range(COLS)
+        (k * COLS + x, k * COLS + (x - k - e) % COLS) for k in range(ROWS) for x in range(COLS)
+    ]
+
+
+def along_column(e):
+    return [
+        (k * COLS + c, (c + k + e) % ROWS * COLS + c) for k in range(ROWS) for c in range(COLS)
     ]
 
 
@@ -42,8 +48,8 @@
 
 def complex_product(lefts, rights, dim, order):
     left = jnp.concatenate([x[...].reshape(-1, x.shape[2]) for x in lefts], axis=1)
-    real = jnp.concatenate([rights[e][0] for e in order], axis=dim)
-    imag = jnp.concatenate([rights[e][1] for e in order], axis=dim)
+    real = jnp.concatenate([rights(e)[0] for e in order], axis=dim)
+    imag = jnp.concatenate([rights(e)[1] for e in order], axis=dim)
     half = left.shape[0] // 2
     u = product(left, real, dim)
     v = product(left, imag, dim)
@@ -56,9 +62,9 @@
     return jnp.stack(pair, axis=1).reshape(2 * rows, columns).astype(jnp.bfloat16)
 
 
-def coupling_kernel(base_ref, l0, l1, l2, l3, t0, t1, t2, t3, c_ref, ct_ref):
+def coupling_kernel(base_ref, l0, l1, l2, l3, t_ref, c_ref, ct_ref):
     def run(order):
-        re, im = complex_product((l0, l1, l2, l3), (t0, t1, t2, t3), 0, order)
+        re, im = complex_product((l0, l1, l2, l3), t_ref.at.__getitem__, 0, order)
         c_ref[0] = (-re).astype(jnp.bfloat16)
         c_ref[1] = (-im).astype(jnp.bfloat16)
         ct_ref[...] = by_atom((-re).T, (-im).T)
@@ -67,12 +73,12 @@
 
         @pl.when(base_ref[0] == base)
         def _():
-            run([(base + d) % ROWS for d in range(ROWS)])
-
-
-def coupling_call(base, lefts, trails):
+            run([(base - e) % ROWS for e in range(ROWS)])
+
+
+def coupling_call(base, lefts, trail):
     _, rows, inner = lefts[0].shape
-    columns = trails[0].shape[2]
+    columns = trail.shape[3]
     tile = 256
     left_spec = pl.BlockSpec((2, tile, inner), lambda i, *_: (0, i, 0))
     return pl.pallas_call(
@@ -84,7 +90,7 @@
         grid_spec=pltpu.PrefetchScalarGridSpec(
             num_scalar_prefetch=1,
             grid=(rows // tile,),
-            in_specs=[left_spec] * 4 + [whole(trails[0].shape)] * 4,
+            in_specs=[left_spec] * 4 + [whole(trail.shape)],
             out_specs=(
                 pl.BlockSpec((2, tile, columns), lambda i, *_: (0, i, 0)),
                 pl.BlockSpec((2 * columns, tile), lambda i, *_: (0, i)),
@@ -95,7 +101,7 @@
             flops=2 * rows * inner * 16 * columns, bytes_accessed=6 << 20, transcendentals=0
         ),
         name="coupling",
-    )(base, *lefts, *trails)
+    )(base, *lefts, trail)
 
 
 def take_pairs(codes_ref, mask_ref, pairs_ref, table, lanes, spread, keep, fold):
@@ -154,7 +160,7 @@
             pairs_ref[owner, SLOTS:, :] = slot.astype(jnp.bfloat16)
 
     def run(order):
-        re, im = complex_product((c0, c1, c2, c3), (l0, l1, l2, l3), 1, order)
+        re, im = complex_product((c0, c1, c2, c3), (l0, l1, l2, l3).__getitem__, 1, order)
         re = diag_ref[0].astype(jnp.float32) - re
         im = diag_ref[1].astype(jnp.float32) - im
         out_ref[0] = re.astype(jnp.bfloat16)
@@ -202,7 +208,7 @@
                 pltpu.VMEM((SLOTS, SLOTS * 8), jnp.bfloat16),
             ],
         ),
-        compiler_params=pltpu.CompilerParams(vmem_limit_bytes=24 * MIB),
+        compiler_params=pltpu.CompilerParams(vmem_limit_bytes=60 * MIB),
         cost_estimate=pl.CostEstimate(
             flops=2 * rows * inner * 16 * columns, bytes_accessed=12 << 20, transcendentals=0
         ),
@@ -317,8 +323,11 @@
     lower = parts_apart(lower_t[0])
     lower, trail = lax.optimization_barrier((lower, trail))
 
-    trails = [trail] + [lax.ppermute(trail, "row", ring(e, ROWS)) for e in range(1, ROWS)]
-    lefts = [lax.ppermute(lower, ("row", "col"), to_process_rows(d)) for d in range(COLS)]
+    pair_axes = ("row", "col")
+    trail_all = lax.all_gather(trail[None], "row", axis=0, tiled=True)
+    lefts = [lax.ppermute(lower, pair_axes, along_row(e)) for e in range(COLS)]
+    lower_first = lax.ppermute(lower, "row", ring(1, ROWS))
+    lefts = [lax.ppermute(left, pair_axes, along_column(e)) for e, left in enumerate(lefts)]
 
     codes, index = pair_tables(pair_row, pair_col, row, col, pole, poles)
     diag = parts_apart(diag_inverse[0])
@@ -328,12 +337,14 @@
         == jnp.broadcast_to(jnp.arange(128, dtype=jnp.int32) // B, (16, 128))[None]
     ).astype(jnp.bfloat16)
 
-    coupling, coupling_t = coupling_call(base, lefts, trails)
+    coupling, coupling_t = coupling_call(base, lefts, trail_all)
     lower_late, coupling = lax.optimization_barrier((lower, coupling))
     couplings = [coupling] + [
         lax.ppermute(coupling, "col", ring(d, COLS)) for d in range(1, COLS)
     ]
-    lowers = [lower] + [lax.ppermute(lower_late, "row", ring(e, ROWS)) for e in range(1, ROWS)]
+    lowers = [lower, lower_first] + [
+        lax.ppermute(lower_late, "row", ring(e, ROWS)) for e in range(2, ROWS)
+    ]
 
     block, pairs = block_call(
         base, pole_slot, codes, couplings, lowers, diag, coupling_t, masks

time: 150 us -> 164 us (1.093)
  between operations: 1.48 us -> 15 us
  starting transfers between devices: 49.7 us -> 56.5 us
  local copies, waits for them, and re-layouts: 14.5 us -> 9.26 us
  waiting for transfers between devices: 66.5 us -> 63.2 us
    ppermute x7 -> x9, starting transfers between devices: 15.2 us -> 34.4 us  [the longest x4 22.7 us: local(): lax.ppermute(left, pair_axes, along_column(e))]
    ppermute x3 -> x2, starting transfers between devices: 14.8 us -> 6.02 us  [local(): lax.ppermute(lower_late, 'row', ring(e, ROWS))]
    ppermute x3 -> x2, waiting for transfers between devices: 14.3 us -> 8.03 us  [local(): lax.ppermute(lower_late, 'row', ring(e, ROWS))]
    ppermute x3, waiting for transfers between devices: 3.85 us -> 10.1 us  [local(): lax.ppermute(coupling, 'col', ring(d, COLS))]
    unnamed x39 -> x31, local copies, waits for them, and re-layouts: 14.4 us -> 8.57 us
    ppermute x7 -> x9, waiting for transfers between devices: 28.7 us -> 25.6 us  [the longest x4 18.6 us: local(): lax.ppermute(left, pair_axes, along_column(e))]
    all_to_all x1, starting transfers between devices: 5.83 us -> 3.53 us  [local(): everywhere = lax.all_to_all(summed, ('row', 'col'), 0, 0, tiled=True)]
    ppermute x3, starting transfers between devices: 3.74 us -> 1.47 us  [local(): lax.ppermute(coupling, 'col', ring(d, COLS))]
  transfers between devices with their start and end apart: 15 -> 17, of which waited for: 8 -> 8; matrix products, arithmetic and copies ran while one was open for 3% -> 4% of each run, Pallas kernels for 0% -> 1%
where the time goes in v4:
time: 164 us
  waiting for transfers between devices  63.2 us (39%)
  starting transfers between devices  56.5 us (34%)
  Pallas kernels  17.9 us (11%)
  between operations  15 us (9%)
  local copies, waits for them, and re-layouts  9.26 us (6%)
    ppermute x4, starting transfers between devices, local(): lax.ppermute(left, pair_axes, along_column(e))  22.7 us
    ppermute x4, waiting for transfers between devices, local(): lax.ppermute(left, pair_axes, along_column(e))  18.6 us
    pallas_call x1, Pallas kernels, block_call(): pl.pallas_call(block_kernel, out_shape=(jax.ShapeDtypeStruct((2, rows, co...  13.2 us
    all_to_all x1, waiting for transfers between devices, local(): parts = lax.all_to_all(pairs, POLE, 0, 0, tiled=True)  12.7 us
    ppermute x4, starting transfers between devices, local(): lefts = [lax.ppermute(lower, pair_axes, along_row(e)) for e in range(COLS)]  11.6 us
    all_to_all x1, starting transfers between devices, local(): parts = lax.all_to_all(pairs, POLE, 0, 0, tiled=True)  11.1 us
    ppermute x3, waiting for transfers between devices, local(): lax.ppermute(coupling, 'col', ring(d, COLS))  10.1 us
    unnamed x31, local copies, waits for them, and re-layouts  8.57 us
  transfers between devices with their start and end apart: 17, of which 8 were waited for; matrix products, arithmetic and copies ran while one was open for 4% of the time, Pallas kernels for 1%

profile of v4, /device:TPU:1, one launch (start us, length us, event | category | flops | bytes accessed | tf_op | source)
XLA Modules:
  0.0 163.5 jit_solution(15839234171718428681)
XLA Ops:
  7.2 0.0 copy-start.6
  7.2 0.0 copy-start.8
  7.2 0.0 copy-start.9
  7.2 0.0 all-gather.3.cloned.1.call-start
  7.2 1.1 copy.32
  8.4 0.0 copy-done.6
  8.4 0.0 copy-start.5
  8.4 0.8 copy.33
  9.2 0.0 all-gather.3.cloned.1.call-update
  9.2 1.5 collective-permute-start
  10.7 5.2 %collective-permute-start.2 = (bf16[2,512,256]{2,1,0:T(8,128)(2,1)S(1)}, bf16[2,512,256]{2,1,0:T(8,128)(2,1)}, u32[]{:S(2)}, u32[]{:S(2)}) collective-permute-start(bf16[2,512,256]{2,1,0:T(8,128)(2,1)S(1)} %bitcast.30), channel_id=1, source_target_pairs={{0,3},{1,0},{2,1},{3,2},{4,6},{5,7},{6,4},{7,5},{8,9},{9,10},{10,1... | collective-permute-start | bytes 1572872 | tf_op jit(solution)/shard_map/ppermute | solution.py:328
  15.9 2.4 %collective-permute-start.4 = (bf16[2,512,256]{2,1,0:T(8,128)(2,1)S(1)}, bf16[2,512,256]{2,1,0:T(8,128)(2,1)}, u32[]{:S(2)}, u32[]{:S(2)}) collective-permute-start(bf16[2,512,256]{2,1,0:T(8,128)(2,1)S(1)} %bitcast.31), channel_id=1, source_target_pairs={{0,2},{1,3},{2,0},{3,1},{4,5},{5,6},{6,7},{7,4},{8,8},{9,9},{10,10... | collective-permute-start | bytes 1572872 | tf_op jit(solution)/shard_map/ppermute | solution.py:328
  18.4 2.5 %collective-permute-start.6 = (bf16[2,512,256]{2,1,0:T(8,128)(2,1)S(1)}, bf16[2,512,256]{2,1,0:T(8,128)(2,1)}, u32[]{:S(2)}, u32[]{:S(2)}) collective-permute-start(bf16[2,512,256]{2,1,0:T(8,128)(2,1)S(1)} %bitcast.32), channel_id=1, source_target_pairs={{0,1},{1,2},{2,3},{3,0},{4,4},{5,5},{6,6},{7,7},{8,11},{9,8},{10,9... | collective-permute-start | bytes 1572872 | tf_op jit(solution)/shard_map/ppermute | solution.py:328
  20.9 0.0 collective-permute-done
  20.9 1.7 %collective-permute-start.1 = (bf16[2,512,256]{2,1,0:T(8,128)(2,1)}, bf16[2,512,256]{2,1,0:T(8,128)(2,1)S(1)}, u32[]{:S(2)}, u32[]{:S(2)}) collective-permute-start(bf16[2,512,256]{2,1,0:T(8,128)(2,1)} %collective-permute-done), channel_id=1, source_target_pairs={{0,0},{1,5},{2,10},{3,15},{4,4},{5,9},{6,14},{7,3},{8,8},{9,13},{1... | collective-permute-start | bytes 1572872 | tf_op jit(solution)/shard_map/ppermute | solution.py:330
  22.6 6.9 %collective-permute-done.2 = bf16[2,512,256]{2,1,0:T(8,128)(2,1)} collective-permute-done((bf16[2,512,256]{2,1,0:T(8,128)(2,1)S(1)}, bf16[2,512,256]{2,1,0:T(8,128)(2,1)}, u32[]{:S(2)}, u32[]{:S(2)}) %collective-permute-start.2) | collective-permute-done | bytes 524320 | tf_op jit(solution)/shard_map/ppermute | solution.py:328
  29.5 4.1 %collective-permute-start.3 = (bf16[2,512,256]{2,1,0:T(8,128)(2,1)}, bf16[2,512,256]{2,1,0:T(8,128)(2,1)S(1)}, u32[]{:S(2)}, u32[]{:S(2)}) collective-permute-start(bf16[2,512,256]{2,1,0:T(8,128)(2,1)} %collective-permute-done.2), channel_id=1, source_target_pairs={{0,4},{1,9},{2,14},{3,3},{4,8},{5,13},{6,2},{7,7},{8,12},{9,1},{10... | collective-permute-start | bytes 1572872 | tf_op jit(solution)/shard_map/ppermute | solution.py:330
  33.7 0.0 collective-permute-done.4
  33.7 11.7 %collective-permute-start.5 = (bf16[2,512,256]{2,1,0:T(8,128)(2,1)}, bf16[2,512,256]{2,1,0:T(8,128)(2,1)S(1)}, u32[]{:S(2)}, u32[]{:S(2)}) collective-permute-start(bf16[2,512,256]{2,1,0:T(8,128)(2,1)} %collective-permute-done.4), channel_id=1, source_target_pairs={{0,8},{1,13},{2,2},{3,7},{4,12},{5,1},{6,6},{7,11},{8,0},{9,5},{10... | collective-permute-start | bytes 1572872 | tf_op jit(solution)/shard_map/ppermute | solution.py:330
  45.4 0.0 collective-permute-done.6
  45.4 5.1 %collective-permute-start.7 = (bf16[2,512,256]{2,1,0:T(8,128)(2,1)}, bf16[2,512,256]{2,1,0:T(8,128)(2,1)S(1)}, u32[]{:S(2)}, u32[]{:S(2)}) collective-permute-start(bf16[2,512,256]{2,1,0:T(8,128)(2,1)} %collective-permute-done.6), channel_id=1, source_target_pairs={{0,12},{1,1},{2,6},{3,11},{4,0},{5,5},{6,10},{7,15},{8,4},{9,9},{1... | collective-permute-start | bytes 1572872 | tf_op jit(solution)/shard_map/ppermute | solution.py:330
  50.6 0.1 collective-permute-start.11
  50.7 0.0 copy-done.8
  50.7 0.0 copy-done.9
  50.7 0.1 fusion.5
  50.9 0.0 collective-permute-done.1.l0
  50.9 0.0 collective-permute-done.3.l1
  50.9 15.9 %collective-permute-done.5.l2 = bf16[2,512,256]{2,1,0:T(8,128)(2,1)S(1)} collective-permute-done((bf16[2,512,256]{2,1,0:T(8,128)(2,1)}, bf16[2,512,256]{2,1,0:T(8,128)(2,1)S(1)}, u32[]{:S(2)}, u32[]{:S(2)}) %collective-permute-start.5) | collective-permute-done | bytes 524320 | tf_op jit(solution)/shard_map/ppermute | solution.py:330
  66.8 2.7 %collective-permute-done.7.l3 = bf16[2,512,256]{2,1,0:T(8,128)(2,1)S(1)} collective-permute-done((bf16[2,512,256]{2,1,0:T(8,128)(2,1)}, bf16[2,512,256]{2,1,0:T(8,128)(2,1)S(1)}, u32[]{:S(2)}, u32[]{:S(2)}) %collective-permute-start.7) | collective-permute-done | bytes 524320 | tf_op jit(solution)/shard_map/ppermute | solution.py:330
  69.5 1.2 copy-done.1
  70.7 1.9 %coupling.1 = (bf16[2,512,256]{2,1,0:T(8,128)(2,1)S(1)}, bf16[512,512]{1,0:T(8,128)(2,1)S(1)}) custom-call(s32[1]{0:T(128)} %bitcast.base_ref, bf16[2,512,256]{2,1,0:T(8,128)(2,1)S(1)} %collective-permute-done.1.l0, bf16[2,512,256]{2,1,0:T(8,128)(2,1)S(1)} %collective-permute-done.3.l1, bf16[2,512,256]{2,1,0:T(8,128)(2,1)S(1)} %collective-permute-done.5.l2, ...), custom_call_target="tpu_custom_call" | custom-call | flops 1073741824 | bytes 6291456 | tf_op jit(solution)/shard_map/coupling/pallas_call | solution.py:84
  72.7 0.8 copy-done.3
  73.5 3.4 %collective-permute-start.12 = (bf16[2,512,256]{2,1,0:T(8,128)(2,1)S(1)}, bf16[2,512,256]{2,1,0:T(8,128)(2,1)S(1)}, u32[]{:S(2)}, u32[]{:S(2)}) collective-permute-start(bf16[2,512,256]{2,1,0:T(8,128)(2,1)S(1)} %bitcast.34), channel_id=1, source_target_pairs={{0,8},{4,12},{8,0},{12,4},{1,9},{5,13},{9,1},{13,5},{2,10},{6,14},... | collective-permute-start | bytes 1572872 | tf_op jit(solution)/shard_map/ppermute | solution.py:346
  76.9 2.6 %collective-permute-start.13 = (bf16[2,512,256]{2,1,0:T(8,128)(2,1)S(1)}, bf16[2,512,256]{2,1,0:T(8,128)(2,1)S(1)}, u32[]{:S(2)}, u32[]{:S(2)}) collective-permute-start(bf16[2,512,256]{2,1,0:T(8,128)(2,1)S(1)} %bitcast.35), channel_id=1, source_target_pairs={{0,12},{4,0},{8,4},{12,8},{1,13},{5,1},{9,5},{13,9},{2,14},{6,2},{... | collective-permute-start | bytes 1572872 | tf_op jit(solution)/shard_map/ppermute | solution.py:346
  79.5 0.0 collective-permute-start.10
  79.5 1.5 collective-permute-start.8
  81.0 0.0 collective-permute-done.11.l1
  81.0 0.0 collective-permute-start.9
  81.0 0.2 fusion
  81.2 0.4 select_reduce_fusion
  81.6 0.7 reshape.118.codes_ref
  82.2 2.4 %copy.31 = bf16[1,512,2,512]{3,1,2,0:T(8,128)(2,1)} copy(bf16[1,512,2,512]{3,2,1,0:T(2,128)(2,1)} %param.10) | data formatting | bytes 2097152 | tf_op args[2]
  85.2 0.6 fusion.2.mask_ref
  85.9 6.2 %collective-permute-done.10.c3 = bf16[2,512,256]{2,1,0:T(8,128)(2,1)S(1)} collective-permute-done((bf16[2,512,256]{2,1,0:T(8,128)(2,1)S(1)}, bf16[2,512,256]{2,1,0:T(8,128)(2,1)S(1)}, u32[]{:S(2)}, u32[]{:S(2)}) %collective-permute-start.10) | collective-permute-done | bytes 524320 | tf_op jit(solution)/shard_map/ppermute | solution.py:343
  92.1 0.0 collective-permute-done.12.l2
  92.1 8.0 %collective-permute-done.13.l3 = bf16[2,512,256]{2,1,0:T(8,128)(2,1)S(1)} collective-permute-done((bf16[2,512,256]{2,1,0:T(8,128)(2,1)S(1)}, bf16[2,512,256]{2,1,0:T(8,128)(2,1)S(1)}, u32[]{:S(2)}, u32[]{:S(2)}) %collective-permute-start.13) | collective-permute-done | bytes 524320 | tf_op jit(solution)/shard_map/ppermute | solution.py:346
  100.2 3.8 %collective-permute-done.8.c1 = bf16[2,512,256]{2,1,0:T(8,128)(2,1)} collective-permute-done((bf16[2,512,256]{2,1,0:T(8,128)(2,1)S(1)}, bf16[2,512,256]{2,1,0:T(8,128)(2,1)}, u32[]{:S(2)}, u32[]{:S(2)}) %collective-permute-start.8) | collective-permute-done | bytes 524320 | tf_op jit(solution)/shard_map/ppermute | solution.py:343
  104.0 0.0 collective-permute-done.9.c2
  104.0 0.0 copy-done.10
  104.0 0.0 copy-done.11
  104.0 0.0 copy-start.7
  104.0 0.0 copy-start
  104.0 13.2 %block_and_pairs.1 = (bf16[2,512,512]{2,1,0:T(8,128)(2,1)}, bf16[16,80,128]{2,1,0:T(8,128)(2,1)}) custom-call(s32[1]{0:T(128)} %bitcast.base_ref, s32[1]{0:T(128)S(6)} %copy.34.slot_ref, s32[1024]{0:T(1024)} %reshape.118.codes_ref, bf16[2,512,256]{2,1,0:T(8,128)(2,1)} %copy-done.2, bf16[2,512,256]{2,1,0:T(8,128)(2,1)} %collective-permute-done.8.c1, ...), custom_call_target="tpu_custom_call" | custom-call | flops 2147483648 | bytes 12582912 | tf_op jit(solution)/shard_map/block_and_pairs/pallas_call | solution.py:190
  117.3 11.1 %all-to-all-start = ((bf16[16,80,128]{2,1,0:T(8,128)(2,1)}), bf16[16,80,128]{2,1,0:T(8,128)(2,1)S(1)}, u32[]{:S(2)}, u32[]{:S(2)}) async-start(bf16[16,80,128]{2,1,0:T(8,128)(2,1)} %get-tuple-element.17), calls=%async_computation | async-start | bytes 655360 | tf_op jit(solution)/shard_map/all_to_all | solution.py:354
  128.3 0.1 copy.25
  128.5 0.2 convert_reduce_fusion
  128.6 12.7 %all-to-all-done.parts_ref = bf16[16,80,128]{2,1,0:T(8,128)(2,1)S(1)} async-done(((bf16[16,80,128]{2,1,0:T(8,128)(2,1)}), bf16[16,80,128]{2,1,0:T(8,128)(2,1)S(1)}, u32[]{:S(2)}, u32[]{:S(2)}) %all-to-all-start) | async-done | bytes 327712 | tf_op jit(solution)/shard_map/all_to_all | solution.py:354
  141.4 0.0 copy-done
  141.4 0.9 pole_sum.1
  142.3 3.5 %all-to-all-start.1 = ((bf16[16,64,128]{2,1,0:T(8,128)(2,1)}), bf16[16,64,128]{2,1,0:T(8,128)(2,1)S(1)}, u32[]{:S(2)}, u32[]{:S(2)}) async-start(bf16[16,64,128]{2,1,0:T(8,128)(2,1)} %pole_sum.1), calls=%async_computation.1 | async-start | bytes 524288 | tf_op jit(solution)/shard_map/all_to_all | solution.py:357
  145.9 0.1 maximum_convert_fusion.projector_ref
  146.0 2.0 %copy.27 = bf16[1,512,2,512]{3,2,1,0:T(2,128)(2,1)} copy(bf16[1,512,2,512]{3,1,2,0:T(8,128)(2,1)S(1)} %bitcast.26) | data formatting | bytes 2097152
  148.0 6.8 %all-to-all-done.1 = bf16[16,64,128]{2,1,0:T(8,128)(2,1)S(1)} async-done(((bf16[16,64,128]{2,1,0:T(8,128)(2,1)}), bf16[16,64,128]{2,1,0:T(8,128)(2,1)S(1)}, u32[]{:S(2)}, u32[]{:S(2)}) %all-to-all-start.1) | async-done | bytes 262176 | tf_op jit(solution)/shard_map/all_to_all | solution.py:357
  154.9 1.8 %density.1 = f32[512,128]{1,0:T(8,128)} custom-call(s32[512]{0:T(512)S(1)} %multiply_add_fusion.index_ref, bf16[1024,128]{1,0:T(8,128)(2,1)S(1)} %bitcast.23, f32[512,128]{1,0:T(8,128)S(1)} %maximum_convert_fusion.projector_ref), custom_call_target="tpu_custom_call" | custom-call | tf_op jit(solution)/shard_map/density/pallas_call | solution.py:268
  (18 shorter events, 0.1 us)
Async XLA Ops:
  7.2 1.2 copy-start.6
  7.2 43.5 %copy-start.8 = (s32[8192]{0:T(1024)S(1)}, s32[8192]{0:T(1024)}, u32[]{:S(2)}) copy-start(s32[8192]{0:T(1024)} %param.13) | copy-start | bytes 98308
  7.2 43.5 %copy-start.9 = (s32[8192]{0:T(1024)S(1)}, s32[8192]{0:T(1024)}, u32[]{:S(2)}) copy-start(s32[8192]{0:T(1024)} %param.14) | copy-start | bytes 98308
  7.2 62.3 %all-gather.3.cloned.1.call-start = ((), (), s32[]{:S(2)}) async-start(), calls=%async_computation.2 | async-start | bytes 1310720 | tf_op jit(solution)/shard_map/all_gather | solution.py:327
  8.4 68.5 %copy-start.5 = (bf16[1,512,2,256]{3,1,2,0:T(8,128)(2,1)}, bf16[1,512,2,256]{3,1,2,0:T(8,128)(2,1)S(1)}, u32[]{:S(2)}) copy-start(bf16[1,512,2,256]{3,1,2,0:T(8,128)(2,1)S(1)} %copy.32) | copy-start | bytes 1572868
  9.2 11.6 %collective-permute-start = (bf16[2,512,256]{2,1,0:T(8,128)(2,1)S(1)}, bf16[2,512,256]{2,1,0:T(8,128)(2,1)}, u32[]{:S(2)}, u32[]{:S(2)}) collective-permute-start(bf16[2,512,256]{2,1,0:T(8,128)(2,1)S(1)} %bitcast.29), channel_id=1, source_target_pairs={{0,0},{1,1},{2,2},{3,3},{4,7},{5,4},{6,5},{7,6},{8,10},{9,11},{10,... | collective-permute-start | bytes 1572872 | tf_op jit(solution)/shard_map/ppermute | solution.py:328
  10.7 18.8 %collective-permute-start.2 = (bf16[2,512,256]{2,1,0:T(8,128)(2,1)S(1)}, bf16[2,512,256]{2,1,0:T(8,128)(2,1)}, u32[]{:S(2)}, u32[]{:S(2)}) collective-permute-start(bf16[2,512,256]{2,1,0:T(8,128)(2,1)S(1)} %bitcast.30), channel_id=1, source_target_pairs={{0,3},{1,0},{2,1},{3,2},{4,6},{5,7},{6,4},{7,5},{8,9},{9,10},{10,1... | collective-permute-start | bytes 1572872 | tf_op jit(solution)/shard_map/ppermute | solution.py:328
  15.9 17.8 %collective-permute-start.4 = (bf16[2,512,256]{2,1,0:T(8,128)(2,1)S(1)}, bf16[2,512,256]{2,1,0:T(8,128)(2,1)}, u32[]{:S(2)}, u32[]{:S(2)}) collective-permute-start(bf16[2,512,256]{2,1,0:T(8,128)(2,1)S(1)} %bitcast.31), channel_id=1, source_target_pairs={{0,2},{1,3},{2,0},{3,1},{4,5},{5,6},{6,7},{7,4},{8,8},{9,9},{10,10... | collective-permute-start | bytes 1572872 | tf_op jit(solution)/shard_map/ppermute | solution.py:328
  18.4 27.1 %collective-permute-start.6 = (bf16[2,512,256]{2,1,0:T(8,128)(2,1)S(1)}, bf16[2,512,256]{2,1,0:T(8,128)(2,1)}, u32[]{:S(2)}, u32[]{:S(2)}) collective-permute-start(bf16[2,512,256]{2,1,0:T(8,128)(2,1)S(1)} %bitcast.32), channel_id=1, source_target_pairs={{0,1},{1,2},{2,3},{3,0},{4,4},{5,5},{6,6},{7,7},{8,11},{9,8},{10,9... | collective-permute-start | bytes 1572872 | tf_op jit(solution)/shard_map/ppermute | solution.py:328
  20.9 30.0 %collective-permute-start.1 = (bf16[2,512,256]{2,1,0:T(8,128)(2,1)}, bf16[2,512,256]{2,1,0:T(8,128)(2,1)S(1)}, u32[]{:S(2)}, u32[]{:S(2)}) collective-permute-start(bf16[2,512,256]{2,1,0:T(8,128)(2,1)} %collective-permute-done), channel_id=1, source_target_pairs={{0,0},{1,5},{2,10},{3,15},{4,4},{5,9},{6,14},{7,3},{8,8},{9,13},{1... | collective-permute-start | bytes 1572872 | tf_op jit(solution)/shard_map/ppermute | solution.py:330
  29.5 21.3 %collective-permute-start.3 = (bf16[2,512,256]{2,1,0:T(8,128)(2,1)}, bf16[2,512,256]{2,1,0:T(8,128)(2,1)S(1)}, u32[]{:S(2)}, u32[]{:S(2)}) collective-permute-start(bf16[2,512,256]{2,1,0:T(8,128)(2,1)} %collective-permute-done.2), channel_id=1, source_target_pairs={{0,4},{1,9},{2,14},{3,3},{4,8},{5,13},{6,2},{7,7},{8,12},{9,1},{10... | collective-permute-start | bytes 1572872 | tf_op jit(solution)/shard_map/ppermute | solution.py:330
  33.7 33.1 %collective-permute-start.5 = (bf16[2,512,256]{2,1,0:T(8,128)(2,1)}, bf16[2,512,256]{2,1,0:T(8,128)(2,1)S(1)}, u32[]{:S(2)}, u32[]{:S(2)}) collective-permute-start(bf16[2,512,256]{2,1,0:T(8,128)(2,1)} %collective-permute-done.4), channel_id=1, source_target_pairs={{0,8},{1,13},{2,2},{3,7},{4,12},{5,1},{6,6},{7,11},{8,0},{9,5},{10... | collective-permute-start | bytes 1572872 | tf_op jit(solution)/shard_map/ppermute | solution.py:330
  45.4 24.1 %collective-permute-start.7 = (bf16[2,512,256]{2,1,0:T(8,128)(2,1)}, bf16[2,512,256]{2,1,0:T(8,128)(2,1)S(1)}, u32[]{:S(2)}, u32[]{:S(2)}) collective-permute-start(bf16[2,512,256]{2,1,0:T(8,128)(2,1)} %collective-permute-done.6), channel_id=1, source_target_pairs={{0,12},{1,1},{2,6},{3,11},{4,0},{5,5},{6,10},{7,15},{8,4},{9,9},{1... | collective-permute-start | bytes 1572872 | tf_op jit(solution)/shard_map/ppermute | solution.py:330
  50.6 30.4 %collective-permute-start.11 = (bf16[2,512,256]{2,1,0:T(8,128)(2,1)S(1)}, bf16[2,512,256]{2,1,0:T(8,128)(2,1)}, u32[]{:S(2)}, u32[]{:S(2)}) collective-permute-start(bf16[2,512,256]{2,1,0:T(8,128)(2,1)S(1)} %bitcast.33), channel_id=1, source_target_pairs={{0,4},{4,8},{8,12},{12,0},{1,5},{5,9},{9,13},{13,1},{2,6},{6,10},{... | collective-permute-start | bytes 1572872 | tf_op jit(solution)/shard_map/ppermute | solution.py:329
  69.5 1.2 copy-start.1
  72.7 0.8 copy-start.3
  73.5 11.1 %copy-start.2 = (bf16[2,512,256]{2,1,0:T(8,128)(2,1)}, bf16[2,512,256]{2,1,0:T(8,128)(2,1)S(1)}, u32[]{:S(2)}) copy-start(bf16[2,512,256]{2,1,0:T(8,128)(2,1)S(1)} %get-tuple-element.13.c0) | copy-start | bytes 1572868
  73.5 18.6 %collective-permute-start.12 = (bf16[2,512,256]{2,1,0:T(8,128)(2,1)S(1)}, bf16[2,512,256]{2,1,0:T(8,128)(2,1)S(1)}, u32[]{:S(2)}, u32[]{:S(2)}) collective-permute-start(bf16[2,512,256]{2,1,0:T(8,128)(2,1)S(1)} %bitcast.34), channel_id=1, source_target_pairs={{0,8},{4,12},{8,0},{12,4},{1,9},{5,13},{9,1},{13,5},{2,10},{6,14},... | collective-permute-start | bytes 1572872 | tf_op jit(solution)/shard_map/ppermute | solution.py:346
  76.9 23.2 %collective-permute-start.13 = (bf16[2,512,256]{2,1,0:T(8,128)(2,1)S(1)}, bf16[2,512,256]{2,1,0:T(8,128)(2,1)S(1)}, u32[]{:S(2)}, u32[]{:S(2)}) collective-permute-start(bf16[2,512,256]{2,1,0:T(8,128)(2,1)S(1)} %bitcast.35), channel_id=1, source_target_pairs={{0,12},{4,0},{8,4},{12,8},{1,13},{5,1},{9,5},{13,9},{2,14},{6,2},{... | collective-permute-start | bytes 1572872 | tf_op jit(solution)/shard_map/ppermute | solution.py:346
  79.5 12.6 %collective-permute-start.10 = (bf16[2,512,256]{2,1,0:T(8,128)(2,1)S(1)}, bf16[2,512,256]{2,1,0:T(8,128)(2,1)S(1)}, u32[]{:S(2)}, u32[]{:S(2)}) collective-permute-start(bf16[2,512,256]{2,1,0:T(8,128)(2,1)S(1)} %get-tuple-element.13.c0), channel_id=1, source_target_pairs={{0,3},{1,0},{2,1},{3,2},{4,7},{5,4},{6,5},{7,6},{8,11},{9,8},{10,9... | collective-permute-start | bytes 1572872 | tf_op jit(solution)/shard_map/ppermute | solution.py:343
  79.5 24.5 %collective-permute-start.8 = (bf16[2,512,256]{2,1,0:T(8,128)(2,1)S(1)}, bf16[2,512,256]{2,1,0:T(8,128)(2,1)}, u32[]{:S(2)}, u32[]{:S(2)}) collective-permute-start(bf16[2,512,256]{2,1,0:T(8,128)(2,1)S(1)} %get-tuple-element.13.c0), channel_id=1, source_target_pairs={{0,1},{1,2},{2,3},{3,0},{4,5},{5,6},{6,7},{7,4},{8,9},{9,10},{10,1... | collective-permute-start | bytes 1572872 | tf_op jit(solution)/shard_map/ppermute | solution.py:343
  81.0 23.0 %collective-permute-start.9 = (bf16[2,512,256]{2,1,0:T(8,128)(2,1)S(1)}, bf16[2,512,256]{2,1,0:T(8,128)(2,1)}, u32[]{:S(2)}, u32[]{:S(2)}) collective-permute-start(bf16[2,512,256]{2,1,0:T(8,128)(2,1)S(1)} %get-tuple-element.13.c0), channel_id=1, source_target_pairs={{0,2},{1,3},{2,0},{3,1},{4,6},{5,7},{6,4},{7,5},{8,10},{9,11},{10,... | collective-permute-start | bytes 1572872 | tf_op jit(solution)/shard_map/ppermute | solution.py:343
  92.1 11.9 %copy-start.12 = (bf16[2,512,256]{2,1,0:T(8,128)(2,1)}, bf16[2,512,256]{2,1,0:T(8,128)(2,1)S(1)}, u32[]{:S(2)}) copy-start(bf16[2,512,256]{2,1,0:T(8,128)(2,1)S(1)} %collective-permute-done.10.c3) | copy-start | bytes 1572868
  92.1 11.9 %copy-start.10 = (bf16[2,512,256]{2,1,0:T(8,128)(2,1)}, bf16[2,512,256]{2,1,0:T(8,128)(2,1)S(1)}, u32[]{:S(2)}) copy-start(bf16[2,512,256]{2,1,0:T(8,128)(2,1)S(1)} %collective-permute-done.12.l2) | copy-start | bytes 1572868
  100.2 3.9 %copy-start.11 = (bf16[2,512,256]{2,1,0:T(8,128)(2,1)}, bf16[2,512,256]{2,1,0:T(8,128)(2,1)S(1)}, u32[]{:S(2)}) copy-start(bf16[2,512,256]{2,1,0:T(8,128)(2,1)S(1)} %collective-permute-done.13.l3) | copy-start | bytes 1572868
  104.0 24.3 %copy-start.7 = (bf16[512,64]{0,1:T(8,128)(2,1)S(1)}, bf16[512,64]{0,1:T(8,128)(2,1)}, u32[]{:S(2)}) copy-start(bf16[512,64]{0,1:T(8,128)(2,1)} %param.15) | copy-start | bytes 196612
  104.0 37.4 %copy-start = (f32[256,2]{0,1:T(2,128)S(1)}, f32[256,2]{0,1:T(2,128)}, u32[]{:S(2)}) copy-start(f32[256,2]{0,1:T(2,128)} %param.11) | copy-start | bytes 6148
  117.3 28.7 %copy-start.4 = (bf16[2,512,512]{2,1,0:T(8,128)(2,1)S(1)}, bf16[2,512,512]{2,1,0:T(8,128)(2,1)}, u32[]{:S(2)}) copy-start(bf16[2,512,512]{2,1,0:T(8,128)(2,1)} %get-tuple-element.16) | copy-start | bytes 3145732
  117.3 24.1 %all-to-all-start = ((bf16[16,80,128]{2,1,0:T(8,128)(2,1)}), bf16[16,80,128]{2,1,0:T(8,128)(2,1)S(1)}, u32[]{:S(2)}, u32[]{:S(2)}) async-start(bf16[16,80,128]{2,1,0:T(8,128)(2,1)} %get-tuple-element.17), calls=%async_computation | async-start | bytes 655360 | tf_op jit(solution)/shard_map/all_to_all | solution.py:354
  142.3 12.5 %all-to-all-start.1 = ((bf16[16,64,128]{2,1,0:T(8,128)(2,1)}), bf16[16,64,128]{2,1,0:T(8,128)(2,1)S(1)}, u32[]{:S(2)}, u32[]{:S(2)}) async-start(bf16[16,64,128]{2,1,0:T(8,128)(2,1)} %pole_sum.1), calls=%async_computation.1 | async-start | bytes 524288 | tf_op jit(solution)/shard_map/all_to_all | solution.py:357
Sparse Core Ops, SparseCore 0:
  10.4 30.2 all-gather.2

commit v5 on v3

--- a/solution.py
+++ b/solution.py
@@ -12,7 +12,7 @@
 ROWS = 4
 COLS = 4
 SLOTS = 64
-GROUP = 32
+GROUP = 16
 MIB = 1 << 20
 
 
@@ -56,12 +56,11 @@
     return jnp.stack(pair, axis=1).reshape(2 * rows, columns).astype(jnp.bfloat16)
 
 
-def coupling_kernel(base_ref, l0, l1, l2, l3, t0, t1, t2, t3, c_ref, ct_ref):
+def coupling_kernel(base_ref, l0, l1, l2, l3, t0, t1, t2, t3, c_ref):
     def run(order):
         re, im = complex_product((l0, l1, l2, l3), (t0, t1, t2, t3), 0, order)
         c_ref[0] = (-re).astype(jnp.bfloat16)
         c_ref[1] = (-im).astype(jnp.bfloat16)
-        ct_ref[...] = by_atom((-re).T, (-im).T)
 
     for base in range(ROWS):
 
@@ -77,18 +76,12 @@
     left_spec = pl.BlockSpec((2, tile, inner), lambda i, *_: (0, i, 0))
     return pl.pallas_call(
         coupling_kernel,
-        out_shape=(
-            jax.ShapeDtypeStruct((2, rows, columns), jnp.bfloat16),
-            jax.ShapeDtypeStruct((2 * columns, rows), jnp.bfloat16),
-        ),
+        out_shape=jax.ShapeDtypeStruct((2, rows, columns), jnp.bfloat16),
         grid_spec=pltpu.PrefetchScalarGridSpec(
             num_scalar_prefetch=1,
             grid=(rows // tile,),
             in_specs=[left_spec] * 4 + [whole(trails[0].shape)] * 4,
-            out_specs=(
-                pl.BlockSpec((2, tile, columns), lambda i, *_: (0, i, 0)),
-                pl.BlockSpec((2 * columns, tile), lambda i, *_: (0, i)),
-            ),
+            out_specs=pl.BlockSpec((2, tile, columns), lambda i, *_: (0, i, 0)),
         ),
         compiler_params=pltpu.CompilerParams(vmem_limit_bytes=14 * MIB),
         cost_estimate=pl.CostEstimate(
@@ -98,17 +91,25 @@
     )(base, *lefts, *trails)
 
 
-def take_pairs(codes_ref, mask_ref, pairs_ref, table, lanes, spread, keep, fold):
+def take_pairs(codes_ref, counts_ref, mask_ref, pairs_ref, table, lanes, spread, keep, fold):
     owners = pairs_ref.shape[0]
 
     @pl.loop(0, owners * SLOTS // GROUP)
     def _(group):
         first = group * GROUP
         to = pl.multiple_of(first * 16, GROUP * 16)
-        for s in range(GROUP):
-            code = codes_ref[first + s]
-            found = table[pl.ds(pl.multiple_of(code & ~15, 16), 16), :]
-            lanes[pl.ds(to + s * 16, 16), :] = found * mask_ref[code & 15]
+        used = counts_ref[first // SLOTS] > first % SLOTS
+
+        @pl.when(used)
+        def _():
+            for s in range(GROUP):
+                code = codes_ref[first + s]
+                found = table[pl.ds(pl.multiple_of(code & ~15, 16), 16), :]
+                lanes[pl.ds(to + s * 16, 16), :] = found * mask_ref[code & 15]
+
+        @pl.when(jnp.logical_not(used))
+        def _():
+            lanes[pl.ds(to, GROUP * 16), :] = jnp.zeros((GROUP * 16, 128), jnp.bfloat16)
 
     many = 4
 
@@ -125,20 +126,18 @@
 
 
 def block_kernel(
-    base_ref, slot_ref, codes_ref, c0, c1, c2, c3, l0, l1, l2, l3, diag_ref, ct_ref, mask_ref,
+    base_ref, slot_ref, codes_ref, counts_ref, c0, c1, c2, c3, l0, l1, l2, l3, diag_ref, mask_ref,
     out_ref, pairs_ref, table, lanes, spread, keep, fold,
 ):
     step = pl.program_id(0)
     last = pl.num_programs(0) - 1
     tile = out_ref.shape[1]
     per_tile = table.shape[0] // 4
-    super_rows = per_tile - ct_ref.shape[0]
+    trail_rows = 2 * c0.shape[2]
+    super_rows = per_tile - trail_rows
 
     @pl.when(step == 0)
     def _():
-        for t in range(4):
-            first = t * per_tile + super_rows
-            table[first : first + ct_ref.shape[0], :] = ct_ref[:, t * 128 : t * 128 + 128]
         lane = lax.broadcasted_iota(jnp.int32, (128, 128), 1)
         row = lax.broadcasted_iota(jnp.int32, (128, 128), 0)
         spread[...] = jnp.where(row % 8 == lane % 8, 1.0, 0.0).astype(jnp.bfloat16)
@@ -163,6 +162,11 @@
         for t in range(4):
             first = pl.multiple_of(t * per_tile + step * 2 * tile, 2 * tile)
             table[pl.ds(first, 2 * tile), :] = rows[:, t * 128 : t * 128 + 128]
+        own = [c0[part].astype(jnp.float32).T for part in range(2)]
+        rows = by_atom(own[0], own[1])
+        for t in range(tile // 128):
+            first = pl.multiple_of((step * (tile // 128) + t) * per_tile + super_rows, trail_rows)
+            table[pl.ds(first, trail_rows), :] = rows[:, t * 128 : t * 128 + 128]
 
     for base in range(ROWS):
 
@@ -172,10 +176,10 @@
 
     @pl.when(step == last)
     def _():
-        take_pairs(codes_ref, mask_ref, pairs_ref, table, lanes, spread, keep, fold)
-
-
-def block_call(base, slot, codes, couplings, lowers, diag, coupling_t, masks):
+        take_pairs(codes_ref, counts_ref, mask_ref, pairs_ref, table, lanes, spread, keep, fold)
+
+
+def block_call(base, slot, codes, counts, couplings, lowers, diag, masks):
     _, rows, columns = diag.shape
     inner = couplings[0].shape[2]
     owners = codes.shape[0] // SLOTS
@@ -188,26 +192,26 @@
             jax.ShapeDtypeStruct((owners, SLOTS + 16, 2 * B * B), jnp.bfloat16),
         ),
         grid_spec=pltpu.PrefetchScalarGridSpec(
-            num_scalar_prefetch=3,
+            num_scalar_prefetch=4,
             grid=(rows // tile,),
             in_specs=[row_spec(inner)] * 4
             + [whole(lowers[0].shape)] * 4
-            + [row_spec(columns), whole(coupling_t.shape), whole(masks.shape)],
+            + [row_spec(columns), whole(masks.shape)],
             out_specs=(row_spec(columns), whole((owners, SLOTS + 16, 2 * B * B))),
             scratch_shapes=[
-                pltpu.VMEM((4 * (2 * rows + coupling_t.shape[0]), 128), jnp.bfloat16),
+                pltpu.VMEM((4 * (2 * rows + 2 * inner), 128), jnp.bfloat16),
                 pltpu.VMEM((owners * SLOTS * 16, 128), jnp.bfloat16),
                 pltpu.VMEM((128, 128), jnp.bfloat16),
                 pltpu.VMEM((2, 8, 128), jnp.float32),
                 pltpu.VMEM((SLOTS, SLOTS * 8), jnp.bfloat16),
             ],
         ),
-        compiler_params=pltpu.CompilerParams(vmem_limit_bytes=24 * MIB),
+        compiler_params=pltpu.CompilerParams(vmem_limit_bytes=60 * MIB),
         cost_estimate=pl.CostEstimate(
             flops=2 * rows * inner * 16 * columns, bytes_accessed=12 << 20, transcendentals=0
         ),
         name="block_and_pairs",
-    )(base, slot, codes, *couplings, *lowers, diag, coupling_t, masks)
+    )(base, slot, codes, counts, *couplings, *lowers, diag, masks)
 
 
 def pole_sum_kernel(weight_ref, parts_ref, out_ref):
@@ -301,7 +305,8 @@
     own_cell = lax.dynamic_index_in_dim(cell, pole, 0, keepdims=False)
     same = (own_cell[:, None] == own_cell[None, :]) & earlier
     index = own_cell * SLOTS + jnp.sum(same.astype(jnp.int32), axis=0)
-    return codes, index
+    counts = jnp.sum(mine.astype(jnp.int32), axis=1)
+    return codes, counts, index
 
 
 def local(
@@ -320,7 +325,7 @@
     trails = [trail] + [lax.ppermute(trail, "row", ring(e, ROWS)) for e in range(1, ROWS)]
     lefts = [lax.ppermute(lower, ("row", "col"), to_process_rows(d)) for d in range(COLS)]
 
-    codes, index = pair_tables(pair_row, pair_col, row, col, pole, poles)
+    codes, counts, index = pair_tables(pair_row, pair_col, row, col, pole, poles)
     diag = parts_apart(diag_inverse[0])
     wide_projector = jnp.concatenate([projector, projector], axis=1).astype(jnp.float32)
     masks = (
@@ -328,7 +333,7 @@
         == jnp.broadcast_to(jnp.arange(128, dtype=jnp.int32) // B, (16, 128))[None]
     ).astype(jnp.bfloat16)
 
-    coupling, coupling_t = coupling_call(base, lefts, trails)
+    coupling = coupling_call(base, lefts, trails)
     lower_late, coupling = lax.optimization_barrier((lower, coupling))
     couplings = [coupling] + [
         lax.ppermute(coupling, "col", ring(d, COLS)) for d in range(1, COLS)
@@ -336,7 +341,7 @@
     lowers = [lower] + [lax.ppermute(lower_late, "row", ring(e, ROWS)) for e in range(1, ROWS)]
 
     block, pairs = block_call(
-        base, pole_slot, codes, couplings, lowers, diag, coupling_t, masks
+        base, pole_slot, codes, counts, couplings, lowers, diag, masks
     )
     out = block.transpose(1, 0, 2)[None]
 

time: 150 us -> 148 us (0.987)
  local copies, waits for them, and re-layouts: 14.5 us -> 8.89 us
    unnamed x39 -> x31, local copies, waits for them, and re-layouts: 14.4 us -> 8.2 us
    ppermute x3, waiting for transfers between devices: 14.3 us -> 12.5 us  [local(): lax.ppermute(lower_late, 'row', ring(e, ROWS))]
    pallas_call x1, Pallas kernels: 11.7 us -> 13.3 us  [block_call(): pl.pallas_call(block_kernel, out_shape=(jax.ShapeDtypeStruct((2, rows, co...]
  transfers between devices with their start and end apart: 15 -> 15, of which waited for: 8 -> 8; matrix products, arithmetic and copies ran while one was open for 3% -> 5% of each run, Pallas kernels for 0% -> 0%
where the time goes in v5:
time: 148 us; the launch traced here: 147 us
  waiting for transfers between devices  66.6 us (45%)
  starting transfers between devices  50.3 us (34%)
  Pallas kernels  17.7 us (12%)
  local copies, waits for them, and re-layouts  8.89 us (6%)
  other arithmetic  2.06 us (1%)
    ppermute x3, waiting for transfers between devices, local(): lax.ppermute(trail, 'row', ring(e, ROWS))  29.3 us
    ppermute x3, starting transfers between devices, local(): lax.ppermute(lower_late, 'row', ring(e, ROWS))  15.2 us
    pallas_call x1, Pallas kernels, block_call(): pl.pallas_call(block_kernel, out_shape=(jax.ShapeDtypeStruct((2, rows, co...  13.3 us
    all_to_all x1, waiting for transfers between devices, local(): parts = lax.all_to_all(pairs, POLE, 0, 0, tiled=True)  12.7 us
    ppermute x3, waiting for transfers between devices, local(): lax.ppermute(lower_late, 'row', ring(e, ROWS))  12.5 us
    ppermute x4, starting transfers between devices, local(): lax.ppermute(lower, ('row', 'col'), to_process_rows(d))  10.4 us
    all_to_all x1, starting transfers between devices, local(): parts = lax.all_to_all(pairs, POLE, 0, 0, tiled=True)  10.3 us
    unnamed x31, local copies, waits for them, and re-layouts  8.2 us
  transfers between devices with their start and end apart: 15, of which 8 were waited for; matrix products, arithmetic and copies ran while one was open for 5% of the time, Pallas kernels for 0%

profile of v5, /device:TPU:1, one launch (start us, length us, event | category | flops | bytes accessed | tf_op | source)
XLA Modules:
  0.0 147.2 jit_solution(10860684330098498293)
XLA Ops:
  0.6 0.0 copy-start.5
  0.6 2.0 %copy.26 = bf16[1,512,2,256]{3,1,2,0:T(8,128)(2,1)} copy(bf16[1,512,2,256]{3,2,1,0:T(2,128)(2,1)} %param.9) | data formatting | bytes 1048576 | tf_op args[1]
  2.6 0.0 copy-done.5
  2.6 2.2 %collective-permute-start.4 = (bf16[2,256,256]{2,1,0:T(8,128)(2,1)S(1)}, bf16[2,256,256]{2,1,0:T(8,128)(2,1)S(1)}, u32[]{:S(2)}, u32[]{:S(2)}) collective-permute-start(bf16[2,256,256]{2,1,0:T(8,128)(2,1)S(1)} %bitcast.24), channel_id=1, source_target_pairs={{0,4},{4,8},{8,12},{12,0},{1,5},{5,9},{9,13},{13,1},{2,6},{6,10},{... | collective-permute-start | bytes 786440 | tf_op jit(solution)/shard_map/ppermute | solution.py:325
  4.8 2.6 %collective-permute-start.5 = (bf16[2,256,256]{2,1,0:T(8,128)(2,1)S(1)}, bf16[2,256,256]{2,1,0:T(8,128)(2,1)S(1)}, u32[]{:S(2)}, u32[]{:S(2)}) collective-permute-start(bf16[2,256,256]{2,1,0:T(8,128)(2,1)S(1)} %bitcast.25), channel_id=1, source_target_pairs={{0,8},{4,12},{8,0},{12,4},{1,9},{5,13},{9,1},{13,5},{2,10},{6,14},... | collective-permute-start | bytes 786440 | tf_op jit(solution)/shard_map/ppermute | solution.py:325
  7.5 1.7 %collective-permute-start = (bf16[2,512,256]{2,1,0:T(8,128)(2,1)}, bf16[2,512,256]{2,1,0:T(8,128)(2,1)S(1)}, u32[]{:S(2)}, u32[]{:S(2)}) collective-permute-start(bf16[2,512,256]{2,1,0:T(8,128)(2,1)} %bitcast.21.l0), channel_id=1, source_target_pairs={{0,0},{1,4},{2,8},{3,12},{4,1},{5,5},{6,9},{7,13},{8,2},{9,6},{10,... | collective-permute-start | bytes 1572872 | tf_op jit(solution)/shard_map/ppermute | solution.py:326
  9.1 1.5 %collective-permute-start.1 = (bf16[2,512,256]{2,1,0:T(8,128)(2,1)}, bf16[2,512,256]{2,1,0:T(8,128)(2,1)S(1)}, u32[]{:S(2)}, u32[]{:S(2)}) collective-permute-start(bf16[2,512,256]{2,1,0:T(8,128)(2,1)} %bitcast.21.l0), channel_id=1, source_target_pairs={{0,1},{1,5},{2,9},{3,13},{4,2},{5,6},{6,10},{7,14},{8,3},{9,7},{10... | collective-permute-start | bytes 1572872 | tf_op jit(solution)/shard_map/ppermute | solution.py:326
  10.7 3.7 %collective-permute-start.2 = (bf16[2,512,256]{2,1,0:T(8,128)(2,1)}, bf16[2,512,256]{2,1,0:T(8,128)(2,1)S(1)}, u32[]{:S(2)}, u32[]{:S(2)}) collective-permute-start(bf16[2,512,256]{2,1,0:T(8,128)(2,1)} %bitcast.21.l0), channel_id=1, source_target_pairs={{0,2},{1,6},{2,10},{3,14},{4,3},{5,7},{6,11},{7,15},{8,0},{9,4},{1... | collective-permute-start | bytes 1572872 | tf_op jit(solution)/shard_map/ppermute | solution.py:326
  14.4 0.0 collective-permute-done.4.t1
  14.4 3.5 %collective-permute-start.3 = (bf16[2,512,256]{2,1,0:T(8,128)(2,1)}, bf16[2,512,256]{2,1,0:T(8,128)(2,1)S(1)}, u32[]{:S(2)}, u32[]{:S(2)}) collective-permute-start(bf16[2,512,256]{2,1,0:T(8,128)(2,1)} %bitcast.21.l0), channel_id=1, source_target_pairs={{0,3},{1,7},{2,11},{3,15},{4,0},{5,4},{6,8},{7,12},{8,1},{9,5},{10... | collective-permute-start | bytes 1572872 | tf_op jit(solution)/shard_map/ppermute | solution.py:326
  17.8 23.4 %collective-permute-done.5.t2 = bf16[2,256,256]{2,1,0:T(8,128)(2,1)S(1)} collective-permute-done((bf16[2,256,256]{2,1,0:T(8,128)(2,1)S(1)}, bf16[2,256,256]{2,1,0:T(8,128)(2,1)S(1)}, u32[]{:S(2)}, u32[]{:S(2)}) %collective-permute-start.5) | collective-permute-done | bytes 262176 | tf_op jit(solution)/shard_map/ppermute | solution.py:325
  41.2 0.0 collective-permute-start.6
  41.2 5.9 %collective-permute-done.6.t3 = bf16[2,256,256]{2,1,0:T(8,128)(2,1)S(1)} collective-permute-done((bf16[2,256,256]{2,1,0:T(8,128)(2,1)S(1)}, bf16[2,256,256]{2,1,0:T(8,128)(2,1)S(1)}, u32[]{:S(2)}, u32[]{:S(2)}) %collective-permute-start.6) | collective-permute-done | bytes 262176 | tf_op jit(solution)/shard_map/ppermute | solution.py:325
  47.1 0.0 copy-start.2
  47.1 0.7 copy-done.2
  47.8 0.0 collective-permute-done.l0
  47.8 0.0 collective-permute-done.1.l1
  47.8 0.0 collective-permute-done.2.l2
  47.8 0.0 collective-permute-done.3.l3
  47.8 0.0 copy-start.3
  47.8 0.9 copy-done.3
  48.8 1.7 %coupling.1.c0 = bf16[2,512,256]{2,1,0:T(8,128)(2,1)S(1)} custom-call(s32[1]{0:T(128)} %bitcast.base_ref, bf16[2,512,256]{2,1,0:T(8,128)(2,1)S(1)} %collective-permute-done.l0, bf16[2,512,256]{2,1,0:T(8,128)(2,1)S(1)} %collective-permute-done.1.l1, bf16[2,512,256]{2,1,0:T(8,128)(2,1)S(1)} %collective-permute-done.2.l2, ...), custom_call_target="tpu_custom_call" | custom-call | flops 1073741824 | bytes 6291456 | tf_op jit(solution)/shard_map/coupling/pallas_call | solution.py:77
  50.5 0.0 copy-start.1
  50.5 12.7 %collective-permute-start.10 = (bf16[2,512,256]{2,1,0:T(8,128)(2,1)}, bf16[2,512,256]{2,1,0:T(8,128)(2,1)S(1)}, u32[]{:S(2)}, u32[]{:S(2)}) collective-permute-start(bf16[2,512,256]{2,1,0:T(8,128)(2,1)} %bitcast.21.l0), channel_id=1, source_target_pairs={{0,4},{4,8},{8,12},{12,0},{1,5},{5,9},{9,13},{13,1},{2,6},{6,10},{... | collective-permute-start | bytes 1572872 | tf_op jit(solution)/shard_map/ppermute | solution.py:341
  63.3 0.0 copy-done.7
  63.3 0.0 copy-done.8
  63.3 0.8 convert_reduce_fusion.1
  64.1 0.0 collective-permute-start.11
  64.1 2.4 %collective-permute-start.12 = (bf16[2,512,256]{2,1,0:T(8,128)(2,1)}, bf16[2,512,256]{2,1,0:T(8,128)(2,1)S(1)}, u32[]{:S(2)}, u32[]{:S(2)}) collective-permute-start(bf16[2,512,256]{2,1,0:T(8,128)(2,1)} %bitcast.21.l0), channel_id=1, source_target_pairs={{0,12},{4,0},{8,4},{12,8},{1,13},{5,1},{9,5},{13,9},{2,14},{6,2},{... | collective-permute-start | bytes 1572872 | tf_op jit(solution)/shard_map/ppermute | solution.py:341
  66.5 0.0 collective-permute-start.7
  66.5 3.7 %collective-permute-start.8 = (bf16[2,512,256]{2,1,0:T(8,128)(2,1)S(1)}, bf16[2,512,256]{2,1,0:T(8,128)(2,1)}, u32[]{:S(2)}, u32[]{:S(2)}) collective-permute-start(bf16[2,512,256]{2,1,0:T(8,128)(2,1)S(1)} %coupling.1.c0), channel_id=1, source_target_pairs={{0,2},{1,3},{2,0},{3,1},{4,6},{5,7},{6,4},{7,5},{8,10},{9,11},{10,... | collective-permute-start | bytes 1572872 | tf_op jit(solution)/shard_map/ppermute | solution.py:339
  70.2 4.2 %collective-permute-done.10.l1 = bf16[2,512,256]{2,1,0:T(8,128)(2,1)S(1)} collective-permute-done((bf16[2,512,256]{2,1,0:T(8,128)(2,1)}, bf16[2,512,256]{2,1,0:T(8,128)(2,1)S(1)}, u32[]{:S(2)}, u32[]{:S(2)}) %collective-permute-start.10) | collective-permute-done | bytes 524320 | tf_op jit(solution)/shard_map/ppermute | solution.py:341
  74.4 0.0 collective-permute-start.9
  74.4 0.2 fusion
  74.6 0.4 select_reduce_fusion
  74.9 0.7 reshape.118.codes_ref
  75.6 2.4 %copy.25 = bf16[1,512,2,512]{3,1,2,0:T(8,128)(2,1)} copy(bf16[1,512,2,512]{3,2,1,0:T(2,128)(2,1)} %param.10) | data formatting | bytes 2097152 | tf_op args[2]
  78.0 0.0 copy-done.1
  78.0 0.0 copy-done.9
  78.6 0.6 fusion.2.mask_ref
  79.3 6.5 %collective-permute-done.11.l2 = bf16[2,512,256]{2,1,0:T(8,128)(2,1)S(1)} collective-permute-done((bf16[2,512,256]{2,1,0:T(8,128)(2,1)}, bf16[2,512,256]{2,1,0:T(8,128)(2,1)S(1)}, u32[]{:S(2)}, u32[]{:S(2)}) %collective-permute-start.11) | collective-permute-done | bytes 524320 | tf_op jit(solution)/shard_map/ppermute | solution.py:341
  85.7 1.8 %collective-permute-done.12.l3 = bf16[2,512,256]{2,1,0:T(8,128)(2,1)S(1)} collective-permute-done((bf16[2,512,256]{2,1,0:T(8,128)(2,1)}, bf16[2,512,256]{2,1,0:T(8,128)(2,1)S(1)}, u32[]{:S(2)}, u32[]{:S(2)}) %collective-permute-start.12) | collective-permute-done | bytes 524320 | tf_op jit(solution)/shard_map/ppermute | solution.py:341
  87.5 0.0 collective-permute-done.7.c1
  87.6 5.2 %collective-permute-done.8.c2 = bf16[2,512,256]{2,1,0:T(8,128)(2,1)} collective-permute-done((bf16[2,512,256]{2,1,0:T(8,128)(2,1)S(1)}, bf16[2,512,256]{2,1,0:T(8,128)(2,1)}, u32[]{:S(2)}, u32[]{:S(2)}) %collective-permute-start.8) | collective-permute-done | bytes 524320 | tf_op jit(solution)/shard_map/ppermute | solution.py:339
  92.7 0.0 collective-permute-done.9.c3
  92.7 0.0 copy-done.12
  92.8 0.0 copy-done.10
  92.8 0.0 copy-done.11
  92.8 0.0 copy-start.6
  92.8 0.0 copy-start
  92.8 13.3 %block_and_pairs.1 = (bf16[2,512,512]{2,1,0:T(8,128)(2,1)}, bf16[16,80,128]{2,1,0:T(8,128)(2,1)}) custom-call(s32[1]{0:T(128)} %bitcast.base_ref, s32[1]{0:T(128)S(6)} %copy.28.slot_ref, s32[1024]{0:T(1024)} %reshape.118.codes_ref, s32[16]{0:T(128)} %get-tuple-element.18.counts_ref, bf16[2,512,256]{2,1,0:T(8,128)(2,1)} %copy-done.1, ...), custom_call_target="tpu_custom_call" | custom-call | flops 2147483648 | bytes 12582912 | tf_op jit(solution)/shard_map/block_and_pairs/pallas_call | solution.py:188
  106.1 10.3 %all-to-all-start = ((bf16[16,80,128]{2,1,0:T(8,128)(2,1)}), bf16[16,80,128]{2,1,0:T(8,128)(2,1)S(1)}, u32[]{:S(2)}, u32[]{:S(2)}) async-start(bf16[16,80,128]{2,1,0:T(8,128)(2,1)} %get-tuple-element.13), calls=%async_computation | async-start | bytes 655360 | tf_op jit(solution)/shard_map/all_to_all | solution.py:348
  116.4 0.0 copy-done.6
  116.4 0.1 copy.19
  116.5 0.2 convert_reduce_fusion
  116.7 12.7 %all-to-all-done.parts_ref = bf16[16,80,128]{2,1,0:T(8,128)(2,1)S(1)} async-done(((bf16[16,80,128]{2,1,0:T(8,128)(2,1)}), bf16[16,80,128]{2,1,0:T(8,128)(2,1)S(1)}, u32[]{:S(2)}, u32[]{:S(2)}) %all-to-all-start) | async-done | bytes 327712 | tf_op jit(solution)/shard_map/all_to_all | solution.py:348
  129.4 0.0 copy-done
  129.4 0.9 pole_sum.1
  130.4 5.9 %all-to-all-start.1 = ((bf16[16,64,128]{2,1,0:T(8,128)(2,1)}), bf16[16,64,128]{2,1,0:T(8,128)(2,1)S(1)}, u32[]{:S(2)}, u32[]{:S(2)}) async-start(bf16[16,64,128]{2,1,0:T(8,128)(2,1)} %pole_sum.1), calls=%async_computation.1 | async-start | bytes 524288 | tf_op jit(solution)/shard_map/all_to_all | solution.py:351
  136.3 0.1 maximum_convert_fusion.projector_ref
  136.4 0.0 copy-done.4
  136.4 2.0 %copy.21 = bf16[1,512,2,512]{3,2,1,0:T(2,128)(2,1)} copy(bf16[1,512,2,512]{3,1,2,0:T(8,128)(2,1)S(1)} %bitcast.29) | data formatting | bytes 2097152
  138.5 6.9 %all-to-all-done.1 = bf16[16,64,128]{2,1,0:T(8,128)(2,1)S(1)} async-done(((bf16[16,64,128]{2,1,0:T(8,128)(2,1)}), bf16[16,64,128]{2,1,0:T(8,128)(2,1)S(1)}, u32[]{:S(2)}, u32[]{:S(2)}) %all-to-all-start.1) | async-done | bytes 262176 | tf_op jit(solution)/shard_map/all_to_all | solution.py:351
  145.4 1.8 %density.1 = f32[512,128]{1,0:T(8,128)} custom-call(s32[512]{0:T(512)S(1)} %multiply_add_fusion.index_ref, bf16[1024,128]{1,0:T(8,128)(2,1)S(1)} %bitcast.23, f32[512,128]{1,0:T(8,128)S(1)} %maximum_convert_fusion.projector_ref), custom_call_target="tpu_custom_call" | custom-call | tf_op jit(solution)/shard_map/density/pallas_call | solution.py:266
  (13 shorter events, 0.1 us)
Async XLA Ops:
  0.6 2.0 %copy-start.5 = (bf16[1,256,2,256]{3,2,1,0:T(2,128)(2,1)S(1)}, bf16[1,256,2,256]{3,2,1,0:T(2,128)(2,1)}, u32[]{:S(2)}) copy-start(bf16[1,256,2,256]{3,2,1,0:T(2,128)(2,1)} %param.8) | copy-start | bytes 786436
  2.6 11.7 %collective-permute-start.4 = (bf16[2,256,256]{2,1,0:T(8,128)(2,1)S(1)}, bf16[2,256,256]{2,1,0:T(8,128)(2,1)S(1)}, u32[]{:S(2)}, u32[]{:S(2)}) collective-permute-start(bf16[2,256,256]{2,1,0:T(8,128)(2,1)S(1)} %bitcast.24), channel_id=1, source_target_pairs={{0,4},{4,8},{8,12},{12,0},{1,5},{5,9},{9,13},{13,1},{2,6},{6,10},{... | collective-permute-start | bytes 786440 | tf_op jit(solution)/shard_map/ppermute | solution.py:325
  4.8 36.4 %collective-permute-start.5 = (bf16[2,256,256]{2,1,0:T(8,128)(2,1)S(1)}, bf16[2,256,256]{2,1,0:T(8,128)(2,1)S(1)}, u32[]{:S(2)}, u32[]{:S(2)}) collective-permute-start(bf16[2,256,256]{2,1,0:T(8,128)(2,1)S(1)} %bitcast.25), channel_id=1, source_target_pairs={{0,8},{4,12},{8,0},{12,4},{1,9},{5,13},{9,1},{13,5},{2,10},{6,14},... | collective-permute-start | bytes 786440 | tf_op jit(solution)/shard_map/ppermute | solution.py:325
  7.5 40.4 %collective-permute-start = (bf16[2,512,256]{2,1,0:T(8,128)(2,1)}, bf16[2,512,256]{2,1,0:T(8,128)(2,1)S(1)}, u32[]{:S(2)}, u32[]{:S(2)}) collective-permute-start(bf16[2,512,256]{2,1,0:T(8,128)(2,1)} %bitcast.21.l0), channel_id=1, source_target_pairs={{0,0},{1,4},{2,8},{3,12},{4,1},{5,5},{6,9},{7,13},{8,2},{9,6},{10,... | collective-permute-start | bytes 1572872 | tf_op jit(solution)/shard_map/ppermute | solution.py:326
  9.1 38.7 %collective-permute-start.1 = (bf16[2,512,256]{2,1,0:T(8,128)(2,1)}, bf16[2,512,256]{2,1,0:T(8,128)(2,1)S(1)}, u32[]{:S(2)}, u32[]{:S(2)}) collective-permute-start(bf16[2,512,256]{2,1,0:T(8,128)(2,1)} %bitcast.21.l0), channel_id=1, source_target_pairs={{0,1},{1,5},{2,9},{3,13},{4,2},{5,6},{6,10},{7,14},{8,3},{9,7},{10... | collective-permute-start | bytes 1572872 | tf_op jit(solution)/shard_map/ppermute | solution.py:326
  10.7 37.2 %collective-permute-start.2 = (bf16[2,512,256]{2,1,0:T(8,128)(2,1)}, bf16[2,512,256]{2,1,0:T(8,128)(2,1)S(1)}, u32[]{:S(2)}, u32[]{:S(2)}) collective-permute-start(bf16[2,512,256]{2,1,0:T(8,128)(2,1)} %bitcast.21.l0), channel_id=1, source_target_pairs={{0,2},{1,6},{2,10},{3,14},{4,3},{5,7},{6,11},{7,15},{8,0},{9,4},{1... | collective-permute-start | bytes 1572872 | tf_op jit(solution)/shard_map/ppermute | solution.py:326
  14.4 33.5 %collective-permute-start.3 = (bf16[2,512,256]{2,1,0:T(8,128)(2,1)}, bf16[2,512,256]{2,1,0:T(8,128)(2,1)S(1)}, u32[]{:S(2)}, u32[]{:S(2)}) collective-permute-start(bf16[2,512,256]{2,1,0:T(8,128)(2,1)} %bitcast.21.l0), channel_id=1, source_target_pairs={{0,3},{1,7},{2,11},{3,15},{4,0},{5,4},{6,8},{7,12},{8,1},{9,5},{10... | collective-permute-start | bytes 1572872 | tf_op jit(solution)/shard_map/ppermute | solution.py:326
  41.2 5.9 %collective-permute-start.6 = (bf16[2,256,256]{2,1,0:T(8,128)(2,1)S(1)}, bf16[2,256,256]{2,1,0:T(8,128)(2,1)S(1)}, u32[]{:S(2)}, u32[]{:S(2)}) collective-permute-start(bf16[2,256,256]{2,1,0:T(8,128)(2,1)S(1)} %bitcast.26), channel_id=1, source_target_pairs={{0,12},{4,0},{8,4},{12,8},{1,13},{5,1},{9,5},{13,9},{2,14},{6,2},{... | collective-permute-start | bytes 786440 | tf_op jit(solution)/shard_map/ppermute | solution.py:325
  47.1 0.7 copy-start.2
  47.8 1.0 copy-start.3
  48.8 14.5 %copy-start.7 = (s32[8192]{0:T(1024)S(1)}, s32[8192]{0:T(1024)}, u32[]{:S(2)}) copy-start(s32[8192]{0:T(1024)} %param.13) | copy-start | bytes 98308
  48.8 14.5 %copy-start.8 = (s32[8192]{0:T(1024)S(1)}, s32[8192]{0:T(1024)}, u32[]{:S(2)}) copy-start(s32[8192]{0:T(1024)} %param.14) | copy-start | bytes 98308
  50.5 27.5 %copy-start.1 = (bf16[2,512,256]{2,1,0:T(8,128)(2,1)}, bf16[2,512,256]{2,1,0:T(8,128)(2,1)S(1)}, u32[]{:S(2)}) copy-start(bf16[2,512,256]{2,1,0:T(8,128)(2,1)S(1)} %coupling.1.c0) | copy-start | bytes 1572868
  50.5 23.9 %collective-permute-start.10 = (bf16[2,512,256]{2,1,0:T(8,128)(2,1)}, bf16[2,512,256]{2,1,0:T(8,128)(2,1)S(1)}, u32[]{:S(2)}, u32[]{:S(2)}) collective-permute-start(bf16[2,512,256]{2,1,0:T(8,128)(2,1)} %bitcast.21.l0), channel_id=1, source_target_pairs={{0,4},{4,8},{8,12},{12,0},{1,5},{5,9},{9,13},{13,1},{2,6},{6,10},{... | collective-permute-start | bytes 1572872 | tf_op jit(solution)/shard_map/ppermute | solution.py:341
  64.1 21.7 %collective-permute-start.11 = (bf16[2,512,256]{2,1,0:T(8,128)(2,1)}, bf16[2,512,256]{2,1,0:T(8,128)(2,1)S(1)}, u32[]{:S(2)}, u32[]{:S(2)}) collective-permute-start(bf16[2,512,256]{2,1,0:T(8,128)(2,1)} %bitcast.21.l0), channel_id=1, source_target_pairs={{0,8},{4,12},{8,0},{12,4},{1,9},{5,13},{9,1},{13,5},{2,10},{6,14},... | collective-permute-start | bytes 1572872 | tf_op jit(solution)/shard_map/ppermute | solution.py:341
  64.1 23.5 %collective-permute-start.12 = (bf16[2,512,256]{2,1,0:T(8,128)(2,1)}, bf16[2,512,256]{2,1,0:T(8,128)(2,1)S(1)}, u32[]{:S(2)}, u32[]{:S(2)}) collective-permute-start(bf16[2,512,256]{2,1,0:T(8,128)(2,1)} %bitcast.21.l0), channel_id=1, source_target_pairs={{0,12},{4,0},{8,4},{12,8},{1,13},{5,1},{9,5},{13,9},{2,14},{6,2},{... | collective-permute-start | bytes 1572872 | tf_op jit(solution)/shard_map/ppermute | solution.py:341
  66.5 21.1 %collective-permute-start.7 = (bf16[2,512,256]{2,1,0:T(8,128)(2,1)S(1)}, bf16[2,512,256]{2,1,0:T(8,128)(2,1)S(1)}, u32[]{:S(2)}, u32[]{:S(2)}) collective-permute-start(bf16[2,512,256]{2,1,0:T(8,128)(2,1)S(1)} %coupling.1.c0), channel_id=1, source_target_pairs={{0,1},{1,2},{2,3},{3,0},{4,5},{5,6},{6,7},{7,4},{8,9},{9,10},{10,1... | collective-permute-start | bytes 1572872 | tf_op jit(solution)/shard_map/ppermute | solution.py:339
  66.5 26.2 %collective-permute-start.8 = (bf16[2,512,256]{2,1,0:T(8,128)(2,1)S(1)}, bf16[2,512,256]{2,1,0:T(8,128)(2,1)}, u32[]{:S(2)}, u32[]{:S(2)}) collective-permute-start(bf16[2,512,256]{2,1,0:T(8,128)(2,1)S(1)} %coupling.1.c0), channel_id=1, source_target_pairs={{0,2},{1,3},{2,0},{3,1},{4,6},{5,7},{6,4},{7,5},{8,10},{9,11},{10,... | collective-permute-start | bytes 1572872 | tf_op jit(solution)/shard_map/ppermute | solution.py:339
  74.4 3.6 %copy-start.9 = (bf16[2,512,256]{2,1,0:T(8,128)(2,1)}, bf16[2,512,256]{2,1,0:T(8,128)(2,1)S(1)}, u32[]{:S(2)}) copy-start(bf16[2,512,256]{2,1,0:T(8,128)(2,1)S(1)} %collective-permute-done.10.l1) | copy-start | bytes 1572868
  74.4 18.4 %collective-permute-start.9 = (bf16[2,512,256]{2,1,0:T(8,128)(2,1)S(1)}, bf16[2,512,256]{2,1,0:T(8,128)(2,1)}, u32[]{:S(2)}, u32[]{:S(2)}) collective-permute-start(bf16[2,512,256]{2,1,0:T(8,128)(2,1)S(1)} %coupling.1.c0), channel_id=1, source_target_pairs={{0,3},{1,0},{2,1},{3,2},{4,7},{5,4},{6,5},{7,6},{8,11},{9,8},{10,9... | collective-permute-start | bytes 1572872 | tf_op jit(solution)/shard_map/ppermute | solution.py:339
  85.7 7.0 %copy-start.10 = (bf16[2,512,256]{2,1,0:T(8,128)(2,1)}, bf16[2,512,256]{2,1,0:T(8,128)(2,1)S(1)}, u32[]{:S(2)}) copy-start(bf16[2,512,256]{2,1,0:T(8,128)(2,1)S(1)} %collective-permute-done.11.l2) | copy-start | bytes 1572868
  87.5 5.2 %copy-start.11 = (bf16[2,512,256]{2,1,0:T(8,128)(2,1)}, bf16[2,512,256]{2,1,0:T(8,128)(2,1)S(1)}, u32[]{:S(2)}) copy-start(bf16[2,512,256]{2,1,0:T(8,128)(2,1)S(1)} %collective-permute-done.12.l3) | copy-start | bytes 1572868
  87.6 5.2 %copy-start.12 = (bf16[2,512,256]{2,1,0:T(8,128)(2,1)}, bf16[2,512,256]{2,1,0:T(8,128)(2,1)S(1)}, u32[]{:S(2)}) copy-start(bf16[2,512,256]{2,1,0:T(8,128)(2,1)S(1)} %collective-permute-done.7.c1) | copy-start | bytes 1572868
  92.8 23.6 %copy-start.6 = (bf16[512,64]{0,1:T(8,128)(2,1)S(1)}, bf16[512,64]{0,1:T(8,128)(2,1)}, u32[]{:S(2)}) copy-start(bf16[512,64]{0,1:T(8,128)(2,1)} %param.15) | copy-start | bytes 196612
  92.8 36.7 %copy-start = (f32[256,2]{0,1:T(2,128)S(1)}, f32[256,2]{0,1:T(2,128)}, u32[]{:S(2)}) copy-start(f32[256,2]{0,1:T(2,128)} %param.11) | copy-start | bytes 6148
  106.1 30.3 %copy-start.4 = (bf16[2,512,512]{2,1,0:T(8,128)(2,1)S(1)}, bf16[2,512,512]{2,1,0:T(8,128)(2,1)}, u32[]{:S(2)}) copy-start(bf16[2,512,512]{2,1,0:T(8,128)(2,1)} %get-tuple-element.12) | copy-start | bytes 3145732
  106.1 23.3 %all-to-all-start = ((bf16[16,80,128]{2,1,0:T(8,128)(2,1)}), bf16[16,80,128]{2,1,0:T(8,128)(2,1)S(1)}, u32[]{:S(2)}, u32[]{:S(2)}) async-start(bf16[16,80,128]{2,1,0:T(8,128)(2,1)} %get-tuple-element.13), calls=%async_computation | async-start | bytes 655360 | tf_op jit(solution)/shard_map/all_to_all | solution.py:348
  130.4 15.0 %all-to-all-start.1 = ((bf16[16,64,128]{2,1,0:T(8,128)(2,1)}), bf16[16,64,128]{2,1,0:T(8,128)(2,1)S(1)}, u32[]{:S(2)}, u32[]{:S(2)}) async-start(bf16[16,64,128]{2,1,0:T(8,128)(2,1)} %pole_sum.1), calls=%async_computation.1 | async-start | bytes 524288 | tf_op jit(solution)/shard_map/all_to_all | solution.py:351

commit v6 on v5

--- a/solution.py
+++ b/solution.py
@@ -22,7 +22,9 @@
 
 def to_process_rows(shift):
     return [
-        (k * COLS + x, x * COLS + (k + shift) % COLS) for k in range(ROWS) for x in range(COLS)
+        (k * COLS + x, x * COLS + (x + k + shift) % COLS)
+        for k in range(ROWS)
+        for x in range(COLS)
     ]
 
 
@@ -72,20 +74,18 @@
 def coupling_call(base, lefts, trails):
     _, rows, inner = lefts[0].shape
     columns = trails[0].shape[2]
-    tile = 256
-    left_spec = pl.BlockSpec((2, tile, inner), lambda i, *_: (0, i, 0))
     return pl.pallas_call(
         coupling_kernel,
         out_shape=jax.ShapeDtypeStruct((2, rows, columns), jnp.bfloat16),
         grid_spec=pltpu.PrefetchScalarGridSpec(
             num_scalar_prefetch=1,
-            grid=(rows // tile,),
-            in_specs=[left_spec] * 4 + [whole(trails[0].shape)] * 4,
-            out_specs=pl.BlockSpec((2, tile, columns), lambda i, *_: (0, i, 0)),
+            grid=(1,),
+            in_specs=[whole(lefts[0].shape)] * 4 + [whole(trails[0].shape)] * 4,
+            out_specs=whole((2, rows, columns)),
         ),
         compiler_params=pltpu.CompilerParams(vmem_limit_bytes=14 * MIB),
         cost_estimate=pl.CostEstimate(
-            flops=2 * rows * inner * 16 * columns, bytes_accessed=6 << 20, transcendentals=0
+            flops=2 * rows * inner * 16 * columns, bytes_accessed=3 << 20, transcendentals=0
         ),
         name="coupling",
     )(base, *lefts, *trails)
@@ -126,14 +126,15 @@
 
 
 def block_kernel(
-    base_ref, slot_ref, codes_ref, counts_ref, c0, c1, c2, c3, l0, l1, l2, l3, diag_ref, mask_ref,
-    out_ref, pairs_ref, table, lanes, spread, keep, fold,
+    base_ref, slot_ref, codes_ref, counts_ref, *refs
 ):
+    first_half, second_half, lowers = refs[:4], refs[4:8], refs[8:12]
+    diag_ref, mask_ref, out_ref, pairs_ref, table, lanes, spread, keep, fold = refs[12:]
     step = pl.program_id(0)
     last = pl.num_programs(0) - 1
     tile = out_ref.shape[1]
     per_tile = table.shape[0] // 4
-    trail_rows = 2 * c0.shape[2]
+    trail_rows = 2 * refs[0].shape[2]
     super_rows = per_tile - trail_rows
 
     @pl.when(step == 0)
@@ -152,8 +153,8 @@
         for owner in range(pairs_ref.shape[0]):
             pairs_ref[owner, SLOTS:, :] = slot.astype(jnp.bfloat16)
 
-    def run(order):
-        re, im = complex_product((c0, c1, c2, c3), (l0, l1, l2, l3), 1, order)
+    def run(order, couplings):
+        re, im = complex_product(couplings, lowers, 1, order)
         re = diag_ref[0].astype(jnp.float32) - re
         im = diag_ref[1].astype(jnp.float32) - im
         out_ref[0] = re.astype(jnp.bfloat16)
@@ -162,17 +163,18 @@
         for t in range(4):
             first = pl.multiple_of(t * per_tile + step * 2 * tile, 2 * tile)
             table[pl.ds(first, 2 * tile), :] = rows[:, t * 128 : t * 128 + 128]
-        own = [c0[part].astype(jnp.float32).T for part in range(2)]
+        own = [couplings[0][part].astype(jnp.float32).T for part in range(2)]
         rows = by_atom(own[0], own[1])
         for t in range(tile // 128):
             first = pl.multiple_of((step * (tile // 128) + t) * per_tile + super_rows, trail_rows)
             table[pl.ds(first, trail_rows), :] = rows[:, t * 128 : t * 128 + 128]
 
     for base in range(ROWS):
-
-        @pl.when(base_ref[0] == base)
-        def _():
-            run([(base + d) % ROWS for d in range(ROWS)])
+        for half, couplings in enumerate((first_half, second_half)):
+
+            @pl.when((base_ref[0] == base) & (step == half))
+            def _():
+                run([(base + d) % ROWS for d in range(ROWS)], couplings)
 
     @pl.when(step == last)
     def _():
@@ -183,7 +185,7 @@
     _, rows, columns = diag.shape
     inner = couplings[0].shape[2]
     owners = codes.shape[0] // SLOTS
-    tile = 256
+    tile = couplings[0].shape[1]
     row_spec = lambda last: pl.BlockSpec((2, tile, last), lambda i, *_: (0, i, 0))
     return pl.pallas_call(
         block_kernel,
@@ -194,7 +196,7 @@
         grid_spec=pltpu.PrefetchScalarGridSpec(
             num_scalar_prefetch=4,
             grid=(rows // tile,),
-            in_specs=[row_spec(inner)] * 4
+            in_specs=[whole(couplings[0].shape)] * 8
             + [whole(lowers[0].shape)] * 4
             + [row_spec(columns), whole(masks.shape)],
             out_specs=(row_spec(columns), whole((owners, SLOTS + 16, 2 * B * B))),
@@ -320,10 +322,15 @@
 
     trail = parts_apart(inverse_trail[0])
     lower = parts_apart(lower_t[0])
-    lower, trail = lax.optimization_barrier((lower, trail))
+    half = lower.shape[1] // 2
+    halves = [parts_apart(lower_t[0, :half]), parts_apart(lower_t[0, half:])]
+    lower, trail, halves = lax.optimization_barrier((lower, trail, halves))
+    pair_axes = ("row", "col")
 
     trails = [trail] + [lax.ppermute(trail, "row", ring(e, ROWS)) for e in range(1, ROWS)]
-    lefts = [lax.ppermute(lower, ("row", "col"), to_process_rows(d)) for d in range(COLS)]
+    first = [lax.ppermute(halves[0], pair_axes, to_process_rows(e)) for e in range(COLS)]
+    second_half, _ = lax.optimization_barrier((halves[1], first[0]))
+    second = [lax.ppermute(second_half, pair_axes, to_process_rows(e)) for e in range(COLS)]
 
     codes, counts, index = pair_tables(pair_row, pair_col, row, col, pole, poles)
     diag = parts_apart(diag_inverse[0])
@@ -333,11 +340,15 @@
         == jnp.broadcast_to(jnp.arange(128, dtype=jnp.int32) // B, (16, 128))[None]
     ).astype(jnp.bfloat16)
 
-    coupling = coupling_call(base, lefts, trails)
-    lower_late, coupling = lax.optimization_barrier((lower, coupling))
-    couplings = [coupling] + [
-        lax.ppermute(coupling, "col", ring(d, COLS)) for d in range(1, COLS)
-    ]
+    trail_base = ((2 * row - col + COLS) % COLS).astype(jnp.int32).reshape(1)
+    couplings = []
+    for lefts in (first, second):
+        coupling = coupling_call(trail_base, lefts, trails)
+        if not couplings:
+            lower_late, coupling = lax.optimization_barrier((lower, coupling))
+        couplings += [coupling] + [
+            lax.ppermute(coupling, "col", ring(d, COLS)) for d in range(1, COLS)
+        ]
     lowers = [lower] + [lax.ppermute(lower_late, "row", ring(e, ROWS)) for e in range(1, ROWS)]
 
     block, pairs = block_call(

time: 148 us -> 144 us (0.973)
  waiting for transfers between devices: 66.6 us -> 41.4 us
  starting transfers between devices: 50.3 us -> 74.5 us
  local copies, waits for them, and re-layouts: 8.89 us -> 5.96 us
    ppermute x3, waiting for transfers between devices: 29.3 us -> 0.01 us  [local(): lax.ppermute(trail, 'row', ring(e, ROWS))]
    ppermute x4 -> x8, starting transfers between devices: 10.4 us -> 38.4 us  [the longest x4 25.9 us: local(): lax.ppermute(halves[0], pair_axes, to_process_rows(e))]
    ppermute x3 -> x6, waiting for transfers between devices: 5.19 us -> 21.1 us  [local(): lax.ppermute(coupling, 'col', ring(d, COLS))]
    ppermute x3, waiting for transfers between devices: 12.5 us -> 0.01 us  [local(): lax.ppermute(lower_late, 'row', ring(e, ROWS))]
    ppermute x3, starting transfers between devices: 15.2 us -> 6.27 us  [local(): lax.ppermute(lower_late, 'row', ring(e, ROWS))]
    ppermute x3, starting transfers between devices: 4.83 us -> 9.64 us  [local(): lax.ppermute(trail, 'row', ring(e, ROWS))]
    unnamed x31 -> x36, local copies, waits for them, and re-layouts: 8.2 us -> 5.22 us
    ppermute x3 -> x6, starting transfers between devices: 3.7 us -> 4.13 us  [local(): lax.ppermute(coupling, 'col', ring(d, COLS))]
  transfers between devices with their start and end apart: 15 -> 22, of which waited for: 8 -> 8; matrix products, arithmetic and copies ran while one was open for 5% -> 4% of each run, Pallas kernels for 0% -> 1%
where the time goes in v6:
time: 144 us
  starting transfers between devices  74.5 us (52%)
  waiting for transfers between devices  41.4 us (29%)
  Pallas kernels  17.9 us (12%)
  local copies, waits for them, and re-layouts  5.96 us (4%)
  other arithmetic  2.05 us (1%)
  between operations  1.67 us (1%)
    ppermute x4, starting transfers between devices, local(): lax.ppermute(halves[0], pair_axes, to_process_rows(e))  25.9 us
    ppermute x6, waiting for transfers between devices, local(): lax.ppermute(coupling, 'col', ring(d, COLS))  21.1 us
    pallas_call x1, Pallas kernels, block_call(): pl.pallas_call(block_kernel, out_shape=(jax.ShapeDtypeStruct((2, rows, co...  13.7 us
    all_to_all x1, waiting for transfers between devices, local(): parts = lax.all_to_all(pairs, POLE, 0, 0, tiled=True)  12.7 us
    ppermute x4, starting transfers between devices, local(): lax.ppermute(second_half, pair_axes, to_process_rows(e))  12.4 us
    all_to_all x1, starting transfers between devices, local(): parts = lax.all_to_all(pairs, POLE, 0, 0, tiled=True)  10.5 us
    ppermute x3, starting transfers between devices, local(): lax.ppermute(trail, 'row', ring(e, ROWS))  9.64 us
    all_to_all x1, waiting for transfers between devices, local(): everywhere = lax.all_to_all(summed, ('row', 'col'), 0, 0, tiled=True)  6.89 us
  transfers between devices with their start and end apart: 22, of which 8 were waited for; matrix products, arithmetic and copies ran while one was open for 4% of the time, Pallas kernels for 1%

profile of v6, /device:TPU:1, one launch (start us, length us, event | category | flops | bytes accessed | tf_op | source)
XLA Modules:
  0.0 143.7 jit_solution(15398628320490645032)
XLA Ops:
  0.6 1.2 copy.31
  1.8 0.0 copy-start.8
  1.8 0.0 copy-start.9
  1.8 0.1 slice_bitcast_fusion
  1.9 0.8 collective-permute-start
  2.7 4.5 %collective-permute-start.4 = (bf16[2,256,256]{2,1,0:T(8,128)(2,1)S(1)}, bf16[2,256,256]{2,1,0:T(8,128)(2,1)S(1)}, u32[]{:S(2)}, u32[]{:S(2)}) collective-permute-start(bf16[2,256,256]{2,1,0:T(8,128)(2,1)S(1)} %get-tuple-element.13.t0), channel_id=1, source_target_pairs={{0,4},{4,8},{8,12},{12,0},{1,5},{5,9},{9,13},{13,1},{2,6},{6,10},{... | collective-permute-start | bytes 786440 | tf_op jit(solution)/shard_map/ppermute | solution.py:330
  7.3 3.7 %collective-permute-start.5 = (bf16[2,256,256]{2,1,0:T(8,128)(2,1)S(1)}, bf16[2,256,256]{2,1,0:T(8,128)(2,1)S(1)}, u32[]{:S(2)}, u32[]{:S(2)}) collective-permute-start(bf16[2,256,256]{2,1,0:T(8,128)(2,1)S(1)} %get-tuple-element.13.t0), channel_id=1, source_target_pairs={{0,8},{4,12},{8,0},{12,4},{1,9},{5,13},{9,1},{13,5},{2,10},{6,14},... | collective-permute-start | bytes 786440 | tf_op jit(solution)/shard_map/ppermute | solution.py:330
  10.9 1.4 %collective-permute-start.6 = (bf16[2,256,256]{2,1,0:T(8,128)(2,1)S(1)}, bf16[2,256,256]{2,1,0:T(8,128)(2,1)S(1)}, u32[]{:S(2)}, u32[]{:S(2)}) collective-permute-start(bf16[2,256,256]{2,1,0:T(8,128)(2,1)S(1)} %get-tuple-element.13.t0), channel_id=1, source_target_pairs={{0,12},{4,0},{8,4},{12,8},{1,13},{5,1},{9,5},{13,9},{2,14},{6,2},{... | collective-permute-start | bytes 786440 | tf_op jit(solution)/shard_map/ppermute | solution.py:330
  12.4 2.3 %collective-permute-start.1 = (bf16[2,256,256]{2,1,0:T(8,128)(2,1)S(1)}, bf16[2,256,256]{2,1,0:T(8,128)(2,1)S(1)}, u32[]{:S(2)}, u32[]{:S(2)}) collective-permute-start(bf16[2,256,256]{2,1,0:T(8,128)(2,1)S(1)} %get-tuple-element.12), channel_id=1, source_target_pairs={{0,1},{1,6},{2,11},{3,12},{4,2},{5,7},{6,8},{7,13},{8,3},{9,4},{10... | collective-permute-start | bytes 786440 | tf_op jit(solution)/shard_map/ppermute | solution.py:331
  14.7 0.0 collective-permute-done.l0
  14.7 5.8 %collective-permute-start.2 = (bf16[2,256,256]{2,1,0:T(8,128)(2,1)S(1)}, bf16[2,256,256]{2,1,0:T(8,128)(2,1)S(1)}, u32[]{:S(2)}, u32[]{:S(2)}) collective-permute-start(bf16[2,256,256]{2,1,0:T(8,128)(2,1)S(1)} %get-tuple-element.12), channel_id=1, source_target_pairs={{0,2},{1,7},{2,8},{3,13},{4,3},{5,4},{6,9},{7,14},{8,0},{9,5},{10,... | collective-permute-start | bytes 786440 | tf_op jit(solution)/shard_map/ppermute | solution.py:331
  20.5 0.0 collective-permute-done.4.t1
  20.5 17.0 %collective-permute-start.3 = (bf16[2,256,256]{2,1,0:T(8,128)(2,1)S(1)}, bf16[2,256,256]{2,1,0:T(8,128)(2,1)S(1)}, u32[]{:S(2)}, u32[]{:S(2)}) collective-permute-start(bf16[2,256,256]{2,1,0:T(8,128)(2,1)S(1)} %get-tuple-element.12), channel_id=1, source_target_pairs={{0,3},{1,4},{2,9},{3,14},{4,0},{5,5},{6,10},{7,15},{8,1},{9,6},{10... | collective-permute-start | bytes 786440 | tf_op jit(solution)/shard_map/ppermute | solution.py:331
  37.5 0.0 collective-permute-done.5.t2
  37.6 0.7 collective-permute-start.10
  38.3 0.0 collective-permute-done.6.t3
  38.3 1.9 %collective-permute-start.11 = (bf16[2,256,256]{2,1,0:T(8,128)(2,1)S(1)}, bf16[2,256,256]{2,1,0:T(8,128)(2,1)S(1)}, u32[]{:S(2)}, u32[]{:S(2)}) collective-permute-start(bf16[2,256,256]{2,1,0:T(8,128)(2,1)S(1)} %get-tuple-element.16), channel_id=1, source_target_pairs={{0,1},{1,6},{2,11},{3,12},{4,2},{5,7},{6,8},{7,13},{8,3},{9,4},{10... | collective-permute-start | bytes 786440 | tf_op jit(solution)/shard_map/ppermute | solution.py:333
  40.3 0.0 collective-permute-done.1.l1
  40.3 4.4 %collective-permute-start.12 = (bf16[2,256,256]{2,1,0:T(8,128)(2,1)S(1)}, bf16[2,256,256]{2,1,0:T(8,128)(2,1)S(1)}, u32[]{:S(2)}, u32[]{:S(2)}) collective-permute-start(bf16[2,256,256]{2,1,0:T(8,128)(2,1)S(1)} %get-tuple-element.16), channel_id=1, source_target_pairs={{0,2},{1,7},{2,8},{3,13},{4,3},{5,4},{6,9},{7,14},{8,0},{9,5},{10,... | collective-permute-start | bytes 786440 | tf_op jit(solution)/shard_map/ppermute | solution.py:333
  44.6 0.0 collective-permute-done.2.l2
  44.7 5.5 %collective-permute-start.13 = (bf16[2,256,256]{2,1,0:T(8,128)(2,1)S(1)}, bf16[2,256,256]{2,1,0:T(8,128)(2,1)S(1)}, u32[]{:S(2)}, u32[]{:S(2)}) collective-permute-start(bf16[2,256,256]{2,1,0:T(8,128)(2,1)S(1)} %get-tuple-element.16), channel_id=1, source_target_pairs={{0,3},{1,4},{2,9},{3,14},{4,0},{5,5},{6,10},{7,15},{8,1},{9,6},{10... | collective-permute-start | bytes 786440 | tf_op jit(solution)/shard_map/ppermute | solution.py:333
  50.1 0.0 collective-permute-done.3.l3
  50.1 0.7 coupling.2.refs_0_
  50.9 0.0 copy-start
  50.9 2.4 %collective-permute-start.7 = (bf16[2,256,256]{2,1,0:T(8,128)(2,1)S(1)}, bf16[2,256,256]{2,1,0:T(8,128)(2,1)S(1)}, u32[]{:S(2)}, u32[]{:S(2)}) collective-permute-start(bf16[2,256,256]{2,1,0:T(8,128)(2,1)S(1)} %coupling.2.refs_0_), channel_id=1, source_target_pairs={{0,1},{1,2},{2,3},{3,0},{4,5},{5,6},{6,7},{7,4},{8,9},{9,10},{10,1... | collective-permute-start | bytes 786440 | tf_op jit(solution)/shard_map/ppermute | solution.py:350
  53.3 0.0 collective-permute-done.10.l0
  53.3 0.0 collective-permute-start.8
  53.3 0.8 convert_reduce_fusion.1
  54.1 0.7 collective-permute-done.11.l1
  54.8 0.0 collective-permute-start.17
  54.8 0.0 collective-permute-done.12.l2
  54.8 6.3 %collective-permute-start.18 = (bf16[2,512,256]{2,1,0:T(8,128)(2,1)S(1)}, bf16[2,512,256]{2,1,0:T(8,128)(2,1)}, u32[]{:S(2)}, u32[]{:S(2)}) collective-permute-start(bf16[2,512,256]{2,1,0:T(8,128)(2,1)S(1)} %bitcast.33), channel_id=1, source_target_pairs={{0,8},{4,12},{8,0},{12,4},{1,9},{5,13},{9,1},{13,5},{2,10},{6,14},... | collective-permute-start | bytes 1572872 | tf_op jit(solution)/shard_map/ppermute | solution.py:352
  61.0 0.0 collective-permute-done.13.l3
  61.0 0.0 collective-permute-start.19
  61.1 0.7 coupling.3.refs_4_
  61.8 7.0 %collective-permute-done.7.refs_1_ = bf16[2,256,256]{2,1,0:T(8,128)(2,1)S(1)} collective-permute-done((bf16[2,256,256]{2,1,0:T(8,128)(2,1)S(1)}, bf16[2,256,256]{2,1,0:T(8,128)(2,1)S(1)}, u32[]{:S(2)}, u32[]{:S(2)}) %collective-permute-start.7) | collective-permute-done | bytes 262176 | tf_op jit(solution)/shard_map/ppermute | solution.py:350
  68.8 0.0 collective-permute-start.9
  68.8 0.0 collective-permute-done.8.refs_2_
  68.8 1.4 %collective-permute-start.14 = (bf16[2,256,256]{2,1,0:T(8,128)(2,1)S(1)}, bf16[2,256,256]{2,1,0:T(8,128)(2,1)S(1)}, u32[]{:S(2)}, u32[]{:S(2)}) collective-permute-start(bf16[2,256,256]{2,1,0:T(8,128)(2,1)S(1)} %coupling.3.refs_4_), channel_id=1, source_target_pairs={{0,1},{1,2},{2,3},{3,0},{4,5},{5,6},{6,7},{7,4},{8,9},{9,10},{10,1... | collective-permute-start | bytes 786440 | tf_op jit(solution)/shard_map/ppermute | solution.py:350
  70.3 0.2 fusion
  70.5 0.4 select_reduce_fusion
  70.8 4.2 %collective-permute-done.9.refs_3_ = bf16[2,256,256]{2,1,0:T(8,128)(2,1)S(1)} collective-permute-done((bf16[2,256,256]{2,1,0:T(8,128)(2,1)S(1)}, bf16[2,256,256]{2,1,0:T(8,128)(2,1)S(1)}, u32[]{:S(2)}, u32[]{:S(2)}) %collective-permute-start.9) | collective-permute-done | bytes 262176 | tf_op jit(solution)/shard_map/ppermute | solution.py:350
  75.0 0.0 collective-permute-start.15
  75.1 1.5 %collective-permute-done.14.refs_5_ = bf16[2,256,256]{2,1,0:T(8,128)(2,1)S(1)} collective-permute-done((bf16[2,256,256]{2,1,0:T(8,128)(2,1)S(1)}, bf16[2,256,256]{2,1,0:T(8,128)(2,1)S(1)}, u32[]{:S(2)}, u32[]{:S(2)}) %collective-permute-start.14) | collective-permute-done | bytes 262176 | tf_op jit(solution)/shard_map/ppermute | solution.py:350
  76.5 0.2 collective-permute-start.16
  76.8 0.7 reshape.121.codes_ref
  77.5 1.1 copy.30
  79.3 0.6 fusion.2.refs_13_
  79.9 2.3 %collective-permute-done.15.refs_6_ = bf16[2,256,256]{2,1,0:T(8,128)(2,1)S(1)} collective-permute-done((bf16[2,256,256]{2,1,0:T(8,128)(2,1)S(1)}, bf16[2,256,256]{2,1,0:T(8,128)(2,1)S(1)}, u32[]{:S(2)}, u32[]{:S(2)}) %collective-permute-start.15) | collective-permute-done | bytes 262176 | tf_op jit(solution)/shard_map/ppermute | solution.py:350
  82.2 6.1 %collective-permute-done.16.refs_7_ = bf16[2,256,256]{2,1,0:T(8,128)(2,1)S(1)} collective-permute-done((bf16[2,256,256]{2,1,0:T(8,128)(2,1)S(1)}, bf16[2,256,256]{2,1,0:T(8,128)(2,1)S(1)}, u32[]{:S(2)}, u32[]{:S(2)}) %collective-permute-start.16) | collective-permute-done | bytes 262176 | tf_op jit(solution)/shard_map/ppermute | solution.py:350
  88.3 0.0 collective-permute-done.18.refs_10_
  88.3 0.0 collective-permute-done.19.refs_11_
  88.3 0.7 copy-done.15
  89.0 13.7 %block_and_pairs.1 = (bf16[2,512,512]{2,1,0:T(8,128)(2,1)}, bf16[16,80,128]{2,1,0:T(8,128)(2,1)}) custom-call(s32[1]{0:T(128)} %bitcast.base_ref, s32[1]{0:T(128)S(6)} %copy.32.slot_ref, s32[1024]{0:T(1024)} %reshape.121.codes_ref, s32[16]{0:T(128)} %get-tuple-element.24.counts_ref, bf16[2,256,256]{2,1,0:T(8,128)(2,1)} %copy-done, ...), custom_call_target="tpu_custom_call" | custom-call | flops 2147483648 | bytes 12582912 | tf_op jit(solution)/shard_map/block_and_pairs/pallas_call | solution.py:190
  102.7 10.5 %all-to-all-start = ((bf16[16,80,128]{2,1,0:T(8,128)(2,1)}), bf16[16,80,128]{2,1,0:T(8,128)(2,1)S(1)}, u32[]{:S(2)}, u32[]{:S(2)}) async-start(bf16[16,80,128]{2,1,0:T(8,128)(2,1)} %get-tuple-element.19), calls=%async_computation | async-start | bytes 655360 | tf_op jit(solution)/shard_map/all_to_all | solution.py:359
  113.2 0.1 copy.23
  113.4 0.2 convert_reduce_fusion
  113.5 12.7 %all-to-all-done.parts_ref = bf16[16,80,128]{2,1,0:T(8,128)(2,1)S(1)} async-done(((bf16[16,80,128]{2,1,0:T(8,128)(2,1)}), bf16[16,80,128]{2,1,0:T(8,128)(2,1)S(1)}, u32[]{:S(2)}, u32[]{:S(2)}) %all-to-all-start) | async-done | bytes 327712 | tf_op jit(solution)/shard_map/all_to_all | solution.py:359
  126.3 0.9 pole_sum.1
  127.2 5.6 %all-to-all-start.1 = ((bf16[16,64,128]{2,1,0:T(8,128)(2,1)}), bf16[16,64,128]{2,1,0:T(8,128)(2,1)S(1)}, u32[]{:S(2)}, u32[]{:S(2)}) async-start(bf16[16,64,128]{2,1,0:T(8,128)(2,1)} %pole_sum.1), calls=%async_computation.1 | async-start | bytes 524288 | tf_op jit(solution)/shard_map/all_to_all | solution.py:362
  132.8 0.1 maximum_convert_fusion.projector_ref
  133.0 2.0 %copy.25 = bf16[1,512,2,512]{3,2,1,0:T(2,128)(2,1)} copy(bf16[1,512,2,512]{3,1,2,0:T(8,128)(2,1)S(1)} %bitcast.36) | data formatting | bytes 2097152
  135.0 6.9 %all-to-all-done.1 = bf16[16,64,128]{2,1,0:T(8,128)(2,1)S(1)} async-done(((bf16[16,64,128]{2,1,0:T(8,128)(2,1)}), bf16[16,64,128]{2,1,0:T(8,128)(2,1)S(1)}, u32[]{:S(2)}, u32[]{:S(2)}) %all-to-all-start.1) | async-done | bytes 262176 | tf_op jit(solution)/shard_map/all_to_all | solution.py:362
  141.9 1.8 %density.1 = f32[512,128]{1,0:T(8,128)} custom-call(s32[512]{0:T(512)S(1)} %multiply_add_fusion.index_ref, bf16[1024,128]{1,0:T(8,128)(2,1)S(1)} %bitcast.30, f32[512,128]{1,0:T(8,128)S(1)} %maximum_convert_fusion.projector_ref), custom_call_target="tpu_custom_call" | custom-call | tf_op jit(solution)/shard_map/density/pallas_call | solution.py:268
  (34 shorter events, 0.1 us)
Async XLA Ops:
  0.6 1.2 copy-start.6
  1.8 59.2 %copy-start.3 = (bf16[1,512,2,256]{3,1,2,0:T(8,128)(2,1)}, bf16[1,512,2,256]{3,1,2,0:T(8,128)(2,1)S(1)}, u32[]{:S(2)}) copy-start(bf16[1,512,2,256]{3,1,2,0:T(8,128)(2,1)S(1)} %copy.31) | copy-start | bytes 1572868
  1.8 36.4 %copy-start.8 = (s32[8192]{0:T(1024)S(1)}, s32[8192]{0:T(1024)}, u32[]{:S(2)}) copy-start(s32[8192]{0:T(1024)} %param.13) | copy-start | bytes 98308
  1.8 36.5 %copy-start.9 = (s32[8192]{0:T(1024)S(1)}, s32[8192]{0:T(1024)}, u32[]{:S(2)}) copy-start(s32[8192]{0:T(1024)} %param.14) | copy-start | bytes 98308
  1.9 12.8 %collective-permute-start = (bf16[2,256,256]{2,1,0:T(8,128)(2,1)S(1)}, bf16[2,256,256]{2,1,0:T(8,128)(2,1)S(1)}, u32[]{:S(2)}, u32[]{:S(2)}) collective-permute-start(bf16[2,256,256]{2,1,0:T(8,128)(2,1)S(1)} %get-tuple-element.12), channel_id=1, source_target_pairs={{0,0},{1,5},{2,10},{3,15},{4,1},{5,6},{6,11},{7,12},{8,2},{9,7},{1... | collective-permute-start | bytes 786440 | tf_op jit(solution)/shard_map/ppermute | solution.py:331
  2.7 17.8 %collective-permute-start.4 = (bf16[2,256,256]{2,1,0:T(8,128)(2,1)S(1)}, bf16[2,256,256]{2,1,0:T(8,128)(2,1)S(1)}, u32[]{:S(2)}, u32[]{:S(2)}) collective-permute-start(bf16[2,256,256]{2,1,0:T(8,128)(2,1)S(1)} %get-tuple-element.13.t0), channel_id=1, source_target_pairs={{0,4},{4,8},{8,12},{12,0},{1,5},{5,9},{9,13},{13,1},{2,6},{6,10},{... | collective-permute-start | bytes 786440 | tf_op jit(solution)/shard_map/ppermute | solution.py:330
  7.3 30.3 %collective-permute-start.5 = (bf16[2,256,256]{2,1,0:T(8,128)(2,1)S(1)}, bf16[2,256,256]{2,1,0:T(8,128)(2,1)S(1)}, u32[]{:S(2)}, u32[]{:S(2)}) collective-permute-start(bf16[2,256,256]{2,1,0:T(8,128)(2,1)S(1)} %get-tuple-element.13.t0), channel_id=1, source_target_pairs={{0,8},{4,12},{8,0},{12,4},{1,9},{5,13},{9,1},{13,5},{2,10},{6,14},... | collective-permute-start | bytes 786440 | tf_op jit(solution)/shard_map/ppermute | solution.py:330
  10.9 27.4 %collective-permute-start.6 = (bf16[2,256,256]{2,1,0:T(8,128)(2,1)S(1)}, bf16[2,256,256]{2,1,0:T(8,128)(2,1)S(1)}, u32[]{:S(2)}, u32[]{:S(2)}) collective-permute-start(bf16[2,256,256]{2,1,0:T(8,128)(2,1)S(1)} %get-tuple-element.13.t0), channel_id=1, source_target_pairs={{0,12},{4,0},{8,4},{12,8},{1,13},{5,1},{9,5},{13,9},{2,14},{6,2},{... | collective-permute-start | bytes 786440 | tf_op jit(solution)/shard_map/ppermute | solution.py:330
  12.4 27.9 %collective-permute-start.1 = (bf16[2,256,256]{2,1,0:T(8,128)(2,1)S(1)}, bf16[2,256,256]{2,1,0:T(8,128)(2,1)S(1)}, u32[]{:S(2)}, u32[]{:S(2)}) collective-permute-start(bf16[2,256,256]{2,1,0:T(8,128)(2,1)S(1)} %get-tuple-element.12), channel_id=1, source_target_pairs={{0,1},{1,6},{2,11},{3,12},{4,2},{5,7},{6,8},{7,13},{8,3},{9,4},{10... | collective-permute-start | bytes 786440 | tf_op jit(solution)/shard_map/ppermute | solution.py:331
  14.7 29.9 %collective-permute-start.2 = (bf16[2,256,256]{2,1,0:T(8,128)(2,1)S(1)}, bf16[2,256,256]{2,1,0:T(8,128)(2,1)S(1)}, u32[]{:S(2)}, u32[]{:S(2)}) collective-permute-start(bf16[2,256,256]{2,1,0:T(8,128)(2,1)S(1)} %get-tuple-element.12), channel_id=1, source_target_pairs={{0,2},{1,7},{2,8},{3,13},{4,3},{5,4},{6,9},{7,14},{8,0},{9,5},{10,... | collective-permute-start | bytes 786440 | tf_op jit(solution)/shard_map/ppermute | solution.py:331
  20.5 29.6 %collective-permute-start.3 = (bf16[2,256,256]{2,1,0:T(8,128)(2,1)S(1)}, bf16[2,256,256]{2,1,0:T(8,128)(2,1)S(1)}, u32[]{:S(2)}, u32[]{:S(2)}) collective-permute-start(bf16[2,256,256]{2,1,0:T(8,128)(2,1)S(1)} %get-tuple-element.12), channel_id=1, source_target_pairs={{0,3},{1,4},{2,9},{3,14},{4,0},{5,5},{6,10},{7,15},{8,1},{9,6},{10... | collective-permute-start | bytes 786440 | tf_op jit(solution)/shard_map/ppermute | solution.py:331
  37.6 15.8 %collective-permute-start.10 = (bf16[2,256,256]{2,1,0:T(8,128)(2,1)S(1)}, bf16[2,256,256]{2,1,0:T(8,128)(2,1)S(1)}, u32[]{:S(2)}, u32[]{:S(2)}) collective-permute-start(bf16[2,256,256]{2,1,0:T(8,128)(2,1)S(1)} %get-tuple-element.16), channel_id=1, source_target_pairs={{0,0},{1,5},{2,10},{3,15},{4,1},{5,6},{6,11},{7,12},{8,2},{9,7},{1... | collective-permute-start | bytes 786440 | tf_op jit(solution)/shard_map/ppermute | solution.py:333
  38.3 16.4 %collective-permute-start.11 = (bf16[2,256,256]{2,1,0:T(8,128)(2,1)S(1)}, bf16[2,256,256]{2,1,0:T(8,128)(2,1)S(1)}, u32[]{:S(2)}, u32[]{:S(2)}) collective-permute-start(bf16[2,256,256]{2,1,0:T(8,128)(2,1)S(1)} %get-tuple-element.16), channel_id=1, source_target_pairs={{0,1},{1,6},{2,11},{3,12},{4,2},{5,7},{6,8},{7,13},{8,3},{9,4},{10... | collective-permute-start | bytes 786440 | tf_op jit(solution)/shard_map/ppermute | solution.py:333
  40.3 14.5 %collective-permute-start.12 = (bf16[2,256,256]{2,1,0:T(8,128)(2,1)S(1)}, bf16[2,256,256]{2,1,0:T(8,128)(2,1)S(1)}, u32[]{:S(2)}, u32[]{:S(2)}) collective-permute-start(bf16[2,256,256]{2,1,0:T(8,128)(2,1)S(1)} %get-tuple-element.16), channel_id=1, source_target_pairs={{0,2},{1,7},{2,8},{3,13},{4,3},{5,4},{6,9},{7,14},{8,0},{9,5},{10,... | collective-permute-start | bytes 786440 | tf_op jit(solution)/shard_map/ppermute | solution.py:333
  44.7 16.4 %collective-permute-start.13 = (bf16[2,256,256]{2,1,0:T(8,128)(2,1)S(1)}, bf16[2,256,256]{2,1,0:T(8,128)(2,1)S(1)}, u32[]{:S(2)}, u32[]{:S(2)}) collective-permute-start(bf16[2,256,256]{2,1,0:T(8,128)(2,1)S(1)} %get-tuple-element.16), channel_id=1, source_target_pairs={{0,3},{1,4},{2,9},{3,14},{4,0},{5,5},{6,10},{7,15},{8,1},{9,6},{10... | collective-permute-start | bytes 786440 | tf_op jit(solution)/shard_map/ppermute | solution.py:333
  50.9 17.9 %copy-start = (bf16[2,256,256]{2,1,0:T(8,128)(2,1)}, bf16[2,256,256]{2,1,0:T(8,128)(2,1)S(1)}, u32[]{:S(2)}) copy-start(bf16[2,256,256]{2,1,0:T(8,128)(2,1)S(1)} %coupling.2.refs_0_) | copy-start | bytes 786436
  50.9 17.9 %collective-permute-start.7 = (bf16[2,256,256]{2,1,0:T(8,128)(2,1)S(1)}, bf16[2,256,256]{2,1,0:T(8,128)(2,1)S(1)}, u32[]{:S(2)}, u32[]{:S(2)}) collective-permute-start(bf16[2,256,256]{2,1,0:T(8,128)(2,1)S(1)} %coupling.2.refs_0_), channel_id=1, source_target_pairs={{0,1},{1,2},{2,3},{3,0},{4,5},{5,6},{6,7},{7,4},{8,9},{9,10},{10,1... | collective-permute-start | bytes 786440 | tf_op jit(solution)/shard_map/ppermute | solution.py:350
  53.3 15.5 %collective-permute-start.8 = (bf16[2,256,256]{2,1,0:T(8,128)(2,1)S(1)}, bf16[2,256,256]{2,1,0:T(8,128)(2,1)S(1)}, u32[]{:S(2)}, u32[]{:S(2)}) collective-permute-start(bf16[2,256,256]{2,1,0:T(8,128)(2,1)S(1)} %coupling.2.refs_0_), channel_id=1, source_target_pairs={{0,2},{1,3},{2,0},{3,1},{4,6},{5,7},{6,4},{7,5},{8,10},{9,11},{10,... | collective-permute-start | bytes 786440 | tf_op jit(solution)/shard_map/ppermute | solution.py:350
  54.1 23.4 %copy-start.4 = (bf16[1,512,2,512]{3,2,1,0:T(2,128)(2,1)S(1)}, bf16[1,512,2,512]{3,2,1,0:T(2,128)(2,1)}, u32[]{:S(2)}) copy-start(bf16[1,512,2,512]{3,2,1,0:T(2,128)(2,1)} %param.10) | copy-start | bytes 3145732
  54.8 33.5 %collective-permute-start.17 = (bf16[2,512,256]{2,1,0:T(8,128)(2,1)S(1)}, bf16[2,512,256]{2,1,0:T(8,128)(2,1)}, u32[]{:S(2)}, u32[]{:S(2)}) collective-permute-start(bf16[2,512,256]{2,1,0:T(8,128)(2,1)S(1)} %bitcast.32), channel_id=1, source_target_pairs={{0,4},{4,8},{8,12},{12,0},{1,5},{5,9},{9,13},{13,1},{2,6},{6,10},{... | collective-permute-start | bytes 1572872 | tf_op jit(solution)/shard_map/ppermute | solution.py:352
  54.8 33.5 %collective-permute-start.18 = (bf16[2,512,256]{2,1,0:T(8,128)(2,1)S(1)}, bf16[2,512,256]{2,1,0:T(8,128)(2,1)}, u32[]{:S(2)}, u32[]{:S(2)}) collective-permute-start(bf16[2,512,256]{2,1,0:T(8,128)(2,1)S(1)} %bitcast.33), channel_id=1, source_target_pairs={{0,8},{4,12},{8,0},{12,4},{1,9},{5,13},{9,1},{13,5},{2,10},{6,14},... | collective-permute-start | bytes 1572872 | tf_op jit(solution)/shard_map/ppermute | solution.py:352
  61.0 27.2 %collective-permute-start.19 = (bf16[2,512,256]{2,1,0:T(8,128)(2,1)S(1)}, bf16[2,512,256]{2,1,0:T(8,128)(2,1)}, u32[]{:S(2)}, u32[]{:S(2)}) collective-permute-start(bf16[2,512,256]{2,1,0:T(8,128)(2,1)S(1)} %bitcast.34), channel_id=1, source_target_pairs={{0,12},{4,0},{8,4},{12,8},{1,13},{5,1},{9,5},{13,9},{2,14},{6,2},{... | collective-permute-start | bytes 1572872 | tf_op jit(solution)/shard_map/ppermute | solution.py:352
  61.8 16.8 %copy-start.1 = (bf16[2,256,256]{2,1,0:T(8,128)(2,1)}, bf16[2,256,256]{2,1,0:T(8,128)(2,1)S(1)}, u32[]{:S(2)}) copy-start(bf16[2,256,256]{2,1,0:T(8,128)(2,1)S(1)} %coupling.3.refs_4_) | copy-start | bytes 786436
  68.8 7.7 %copy-start.10 = (bf16[2,256,256]{2,1,0:T(8,128)(2,1)}, bf16[2,256,256]{2,1,0:T(8,128)(2,1)S(1)}, u32[]{:S(2)}) copy-start(bf16[2,256,256]{2,1,0:T(8,128)(2,1)S(1)} %collective-permute-done.7.refs_1_) | copy-start | bytes 786436
  68.8 6.2 %collective-permute-start.9 = (bf16[2,256,256]{2,1,0:T(8,128)(2,1)S(1)}, bf16[2,256,256]{2,1,0:T(8,128)(2,1)S(1)}, u32[]{:S(2)}, u32[]{:S(2)}) collective-permute-start(bf16[2,256,256]{2,1,0:T(8,128)(2,1)S(1)} %coupling.2.refs_0_), channel_id=1, source_target_pairs={{0,3},{1,0},{2,1},{3,2},{4,7},{5,4},{6,5},{7,6},{8,11},{9,8},{10,9... | collective-permute-start | bytes 786440 | tf_op jit(solution)/shard_map/ppermute | solution.py:350
  68.8 8.0 %copy-start.11 = (bf16[2,256,256]{2,1,0:T(8,128)(2,1)}, bf16[2,256,256]{2,1,0:T(8,128)(2,1)S(1)}, u32[]{:S(2)}) copy-start(bf16[2,256,256]{2,1,0:T(8,128)(2,1)S(1)} %collective-permute-done.8.refs_2_) | copy-start | bytes 786436
  68.8 7.7 %collective-permute-start.14 = (bf16[2,256,256]{2,1,0:T(8,128)(2,1)S(1)}, bf16[2,256,256]{2,1,0:T(8,128)(2,1)S(1)}, u32[]{:S(2)}, u32[]{:S(2)}) collective-permute-start(bf16[2,256,256]{2,1,0:T(8,128)(2,1)S(1)} %coupling.3.refs_4_), channel_id=1, source_target_pairs={{0,1},{1,2},{2,3},{3,0},{4,5},{5,6},{6,7},{7,4},{8,9},{9,10},{10,1... | collective-permute-start | bytes 786440 | tf_op jit(solution)/shard_map/ppermute | solution.py:350
  75.0 3.6 %copy-start.12 = (bf16[2,256,256]{2,1,0:T(8,128)(2,1)}, bf16[2,256,256]{2,1,0:T(8,128)(2,1)S(1)}, u32[]{:S(2)}) copy-start(bf16[2,256,256]{2,1,0:T(8,128)(2,1)S(1)} %collective-permute-done.9.refs_3_) | copy-start | bytes 786436
  75.0 7.1 %collective-permute-start.15 = (bf16[2,256,256]{2,1,0:T(8,128)(2,1)S(1)}, bf16[2,256,256]{2,1,0:T(8,128)(2,1)S(1)}, u32[]{:S(2)}, u32[]{:S(2)}) collective-permute-start(bf16[2,256,256]{2,1,0:T(8,128)(2,1)S(1)} %coupling.3.refs_4_), channel_id=1, source_target_pairs={{0,2},{1,3},{2,0},{3,1},{4,6},{5,7},{6,4},{7,5},{8,10},{9,11},{10,... | collective-permute-start | bytes 786440 | tf_op jit(solution)/shard_map/ppermute | solution.py:350
  76.5 2.1 %copy-start.13 = (bf16[2,256,256]{2,1,0:T(8,128)(2,1)}, bf16[2,256,256]{2,1,0:T(8,128)(2,1)S(1)}, u32[]{:S(2)}) copy-start(bf16[2,256,256]{2,1,0:T(8,128)(2,1)S(1)} %collective-permute-done.14.refs_5_) | copy-start | bytes 786436
  76.5 11.7 %collective-permute-start.16 = (bf16[2,256,256]{2,1,0:T(8,128)(2,1)S(1)}, bf16[2,256,256]{2,1,0:T(8,128)(2,1)S(1)}, u32[]{:S(2)}, u32[]{:S(2)}) collective-permute-start(bf16[2,256,256]{2,1,0:T(8,128)(2,1)S(1)} %coupling.3.refs_4_), channel_id=1, source_target_pairs={{0,3},{1,0},{2,1},{3,2},{4,7},{5,4},{6,5},{7,6},{8,11},{9,8},{10,9... | collective-permute-start | bytes 786440 | tf_op jit(solution)/shard_map/ppermute | solution.py:350
  82.2 6.1 %copy-start.14 = (bf16[2,256,256]{2,1,0:T(8,128)(2,1)}, bf16[2,256,256]{2,1,0:T(8,128)(2,1)S(1)}, u32[]{:S(2)}) copy-start(bf16[2,256,256]{2,1,0:T(8,128)(2,1)S(1)} %collective-permute-done.15.refs_6_) | copy-start | bytes 786436
  88.3 0.7 copy-start.15
  89.0 24.2 %copy-start.7 = (bf16[512,64]{0,1:T(8,128)(2,1)S(1)}, bf16[512,64]{0,1:T(8,128)(2,1)}, u32[]{:S(2)}) copy-start(bf16[512,64]{0,1:T(8,128)(2,1)} %param.15) | copy-start | bytes 196612
  89.0 37.3 %copy-start.2 = (f32[256,2]{0,1:T(2,128)S(1)}, f32[256,2]{0,1:T(2,128)}, u32[]{:S(2)}) copy-start(f32[256,2]{0,1:T(2,128)} %param.11) | copy-start | bytes 6148
  102.7 30.2 %copy-start.5 = (bf16[2,512,512]{2,1,0:T(8,128)(2,1)S(1)}, bf16[2,512,512]{2,1,0:T(8,128)(2,1)}, u32[]{:S(2)}) copy-start(bf16[2,512,512]{2,1,0:T(8,128)(2,1)} %get-tuple-element.18) | copy-start | bytes 3145732
  102.7 23.6 %all-to-all-start = ((bf16[16,80,128]{2,1,0:T(8,128)(2,1)}), bf16[16,80,128]{2,1,0:T(8,128)(2,1)S(1)}, u32[]{:S(2)}, u32[]{:S(2)}) async-start(bf16[16,80,128]{2,1,0:T(8,128)(2,1)} %get-tuple-element.19), calls=%async_computation | async-start | bytes 655360 | tf_op jit(solution)/shard_map/all_to_all | solution.py:359
  127.2 14.7 %all-to-all-start.1 = ((bf16[16,64,128]{2,1,0:T(8,128)(2,1)}), bf16[16,64,128]{2,1,0:T(8,128)(2,1)S(1)}, u32[]{:S(2)}, u32[]{:S(2)}) async-start(bf16[16,64,128]{2,1,0:T(8,128)(2,1)} %pole_sum.1), calls=%async_computation.1 | async-start | bytes 524288 | tf_op jit(solution)/shard_map/all_to_all | solution.py:362

commit v7 on v6

--- a/solution.py
+++ b/solution.py
@@ -208,7 +208,7 @@
                 pltpu.VMEM((SLOTS, SLOTS * 8), jnp.bfloat16),
             ],
         ),
-        compiler_params=pltpu.CompilerParams(vmem_limit_bytes=60 * MIB),
+        compiler_params=pltpu.CompilerParams(vmem_limit_bytes=52 * MIB),
         cost_estimate=pl.CostEstimate(
             flops=2 * rows * inner * 16 * columns, bytes_accessed=12 << 20, transcendentals=0
         ),

time: 144 us -> 144 us (level)
    unnamed x36 -> x22, local copies, waits for them, and re-layouts: 5.22 us -> 6.57 us
where the time goes in v7:
time: 144 us; the launch traced here: 143 us
  starting transfers between devices  74.4 us (52%)
  waiting for transfers between devices  41.6 us (29%)
  Pallas kernels  17.2 us (12%)
  local copies, waits for them, and re-layouts  6.72 us (5%)
  between operations  1.63 us (1%)
    ppermute x4, starting transfers between devices, local(): lax.ppermute(halves[0], pair_axes, to_process_rows(e))  25.9 us
    ppermute x6, waiting for transfers between devices, local(): lax.ppermute(coupling, 'col', ring(d, COLS))  20.7 us
    pallas_call x1, Pallas kernels, block_call(): pl.pallas_call(block_kernel, out_shape=(jax.ShapeDtypeStruct((2, rows, co...  13 us
    all_to_all x1, waiting for transfers between devices, local(): parts = lax.all_to_all(pairs, POLE, 0, 0, tiled=True)  12.7 us
    ppermute x4, starting transfers between devices, local(): lax.ppermute(second_half, pair_axes, to_process_rows(e))  12.4 us
    all_to_all x1, starting transfers between devices, local(): parts = lax.all_to_all(pairs, POLE, 0, 0, tiled=True)  10.6 us
    ppermute x3, starting transfers between devices, local(): lax.ppermute(trail, 'row', ring(e, ROWS))  9.64 us
    all_to_all x1, waiting for transfers between devices, local(): everywhere = lax.all_to_all(summed, ('row', 'col'), 0, 0, tiled=True)  6.89 us
  transfers between devices with their start and end apart: 22, of which 8 were waited for; matrix products, arithmetic and copies ran while one was open for 4% of the time, Pallas kernels for 1%

profile of v7, /device:TPU:1, one launch (start us, length us, event | category | flops | bytes accessed | tf_op | source)
XLA Modules:
  0.0 142.7 jit_solution(10001192153502229684)
XLA Ops:
  0.6 1.2 copy.31
  1.8 0.0 copy-start.5
  1.8 0.0 copy-start.6
  1.8 0.1 slice_bitcast_fusion
  1.9 0.8 collective-permute-start
  2.7 4.5 %collective-permute-start.4 = (bf16[2,256,256]{2,1,0:T(8,128)(2,1)S(1)}, bf16[2,256,256]{2,1,0:T(8,128)(2,1)S(1)}, u32[]{:S(2)}, u32[]{:S(2)}) collective-permute-start(bf16[2,256,256]{2,1,0:T(8,128)(2,1)S(1)} %get-tuple-element.13.t0), channel_id=1, source_target_pairs={{0,4},{4,8},{8,12},{12,0},{1,5},{5,9},{9,13},{13,1},{2,6},{6,10},{... | collective-permute-start | bytes 786440 | tf_op jit(solution)/shard_map/ppermute | solution.py:330
  7.3 3.7 %collective-permute-start.5 = (bf16[2,256,256]{2,1,0:T(8,128)(2,1)S(1)}, bf16[2,256,256]{2,1,0:T(8,128)(2,1)S(1)}, u32[]{:S(2)}, u32[]{:S(2)}) collective-permute-start(bf16[2,256,256]{2,1,0:T(8,128)(2,1)S(1)} %get-tuple-element.13.t0), channel_id=1, source_target_pairs={{0,8},{4,12},{8,0},{12,4},{1,9},{5,13},{9,1},{13,5},{2,10},{6,14},... | collective-permute-start | bytes 786440 | tf_op jit(solution)/shard_map/ppermute | solution.py:330
  10.9 1.4 %collective-permute-start.6 = (bf16[2,256,256]{2,1,0:T(8,128)(2,1)S(1)}, bf16[2,256,256]{2,1,0:T(8,128)(2,1)S(1)}, u32[]{:S(2)}, u32[]{:S(2)}) collective-permute-start(bf16[2,256,256]{2,1,0:T(8,128)(2,1)S(1)} %get-tuple-element.13.t0), channel_id=1, source_target_pairs={{0,12},{4,0},{8,4},{12,8},{1,13},{5,1},{9,5},{13,9},{2,14},{6,2},{... | collective-permute-start | bytes 786440 | tf_op jit(solution)/shard_map/ppermute | solution.py:330
  12.4 2.3 %collective-permute-start.1 = (bf16[2,256,256]{2,1,0:T(8,128)(2,1)S(1)}, bf16[2,256,256]{2,1,0:T(8,128)(2,1)S(1)}, u32[]{:S(2)}, u32[]{:S(2)}) collective-permute-start(bf16[2,256,256]{2,1,0:T(8,128)(2,1)S(1)} %get-tuple-element.12), channel_id=1, source_target_pairs={{0,1},{1,6},{2,11},{3,12},{4,2},{5,7},{6,8},{7,13},{8,3},{9,4},{10... | collective-permute-start | bytes 786440 | tf_op jit(solution)/shard_map/ppermute | solution.py:331
  14.7 0.0 collective-permute-done.l0
  14.7 5.8 %collective-permute-start.2 = (bf16[2,256,256]{2,1,0:T(8,128)(2,1)S(1)}, bf16[2,256,256]{2,1,0:T(8,128)(2,1)S(1)}, u32[]{:S(2)}, u32[]{:S(2)}) collective-permute-start(bf16[2,256,256]{2,1,0:T(8,128)(2,1)S(1)} %get-tuple-element.12), channel_id=1, source_target_pairs={{0,2},{1,7},{2,8},{3,13},{4,3},{5,4},{6,9},{7,14},{8,0},{9,5},{10,... | collective-permute-start | bytes 786440 | tf_op jit(solution)/shard_map/ppermute | solution.py:331
  20.5 0.0 collective-permute-done.4.t1
  20.5 17.0 %collective-permute-start.3 = (bf16[2,256,256]{2,1,0:T(8,128)(2,1)S(1)}, bf16[2,256,256]{2,1,0:T(8,128)(2,1)S(1)}, u32[]{:S(2)}, u32[]{:S(2)}) collective-permute-start(bf16[2,256,256]{2,1,0:T(8,128)(2,1)S(1)} %get-tuple-element.12), channel_id=1, source_target_pairs={{0,3},{1,4},{2,9},{3,14},{4,0},{5,5},{6,10},{7,15},{8,1},{9,6},{10... | collective-permute-start | bytes 786440 | tf_op jit(solution)/shard_map/ppermute | solution.py:331
  37.5 0.0 collective-permute-done.5.t2
  37.6 0.7 collective-permute-start.10
  38.3 0.0 collective-permute-done.6.t3
  38.3 1.9 %collective-permute-start.11 = (bf16[2,256,256]{2,1,0:T(8,128)(2,1)S(1)}, bf16[2,256,256]{2,1,0:T(8,128)(2,1)S(1)}, u32[]{:S(2)}, u32[]{:S(2)}) collective-permute-start(bf16[2,256,256]{2,1,0:T(8,128)(2,1)S(1)} %get-tuple-element.16), channel_id=1, source_target_pairs={{0,1},{1,6},{2,11},{3,12},{4,2},{5,7},{6,8},{7,13},{8,3},{9,4},{10... | collective-permute-start | bytes 786440 | tf_op jit(solution)/shard_map/ppermute | solution.py:333
  40.3 0.0 collective-permute-done.1.l1
  40.3 4.4 %collective-permute-start.12 = (bf16[2,256,256]{2,1,0:T(8,128)(2,1)S(1)}, bf16[2,256,256]{2,1,0:T(8,128)(2,1)S(1)}, u32[]{:S(2)}, u32[]{:S(2)}) collective-permute-start(bf16[2,256,256]{2,1,0:T(8,128)(2,1)S(1)} %get-tuple-element.16), channel_id=1, source_target_pairs={{0,2},{1,7},{2,8},{3,13},{4,3},{5,4},{6,9},{7,14},{8,0},{9,5},{10,... | collective-permute-start | bytes 786440 | tf_op jit(solution)/shard_map/ppermute | solution.py:333
  44.6 0.0 collective-permute-done.2.l2
  44.7 5.5 %collective-permute-start.13 = (bf16[2,256,256]{2,1,0:T(8,128)(2,1)S(1)}, bf16[2,256,256]{2,1,0:T(8,128)(2,1)S(1)}, u32[]{:S(2)}, u32[]{:S(2)}) collective-permute-start(bf16[2,256,256]{2,1,0:T(8,128)(2,1)S(1)} %get-tuple-element.16), channel_id=1, source_target_pairs={{0,3},{1,4},{2,9},{3,14},{4,0},{5,5},{6,10},{7,15},{8,1},{9,6},{10... | collective-permute-start | bytes 786440 | tf_op jit(solution)/shard_map/ppermute | solution.py:333
  50.1 0.0 collective-permute-done.3.l3
  50.1 0.7 coupling.2.refs_0_
  50.9 2.4 %collective-permute-start.7 = (bf16[2,256,256]{2,1,0:T(8,128)(2,1)S(1)}, bf16[2,256,256]{2,1,0:T(8,128)(2,1)S(1)}, u32[]{:S(2)}, u32[]{:S(2)}) collective-permute-start(bf16[2,256,256]{2,1,0:T(8,128)(2,1)S(1)} %coupling.2.refs_0_), channel_id=1, source_target_pairs={{0,1},{1,2},{2,3},{3,0},{4,5},{5,6},{6,7},{7,4},{8,9},{9,10},{10,1... | collective-permute-start | bytes 786440 | tf_op jit(solution)/shard_map/ppermute | solution.py:350
  53.3 0.0 collective-permute-done.10.l0
  53.3 0.0 collective-permute-start.8
  53.3 0.2 convert_reduce_fusion.1
  53.6 1.2 collective-permute-done.11.l1
  54.8 0.0 collective-permute-start.17
  54.8 0.0 collective-permute-done.12.l2
  54.8 6.3 %collective-permute-start.18 = (bf16[2,512,256]{2,1,0:T(8,128)(2,1)S(1)}, bf16[2,512,256]{2,1,0:T(8,128)(2,1)}, u32[]{:S(2)}, u32[]{:S(2)}) collective-permute-start(bf16[2,512,256]{2,1,0:T(8,128)(2,1)S(1)} %bitcast.33), channel_id=1, source_target_pairs={{0,8},{4,12},{8,0},{12,4},{1,9},{5,13},{9,1},{13,5},{2,10},{6,14},... | collective-permute-start | bytes 1572872 | tf_op jit(solution)/shard_map/ppermute | solution.py:352
  61.0 0.0 collective-permute-done.13.l3
  61.0 0.0 collective-permute-start.19
  61.1 0.7 coupling.3.refs_4_
  61.8 7.0 %collective-permute-done.7.refs_1_ = bf16[2,256,256]{2,1,0:T(8,128)(2,1)S(1)} collective-permute-done((bf16[2,256,256]{2,1,0:T(8,128)(2,1)S(1)}, bf16[2,256,256]{2,1,0:T(8,128)(2,1)S(1)}, u32[]{:S(2)}, u32[]{:S(2)}) %collective-permute-start.7) | collective-permute-done | bytes 262176 | tf_op jit(solution)/shard_map/ppermute | solution.py:350
  68.8 0.0 collective-permute-start.9
  68.8 0.0 collective-permute-done.8.refs_2_
  68.8 1.5 %collective-permute-start.14 = (bf16[2,256,256]{2,1,0:T(8,128)(2,1)S(1)}, bf16[2,256,256]{2,1,0:T(8,128)(2,1)S(1)}, u32[]{:S(2)}, u32[]{:S(2)}) collective-permute-start(bf16[2,256,256]{2,1,0:T(8,128)(2,1)S(1)} %coupling.3.refs_4_), channel_id=1, source_target_pairs={{0,1},{1,2},{2,3},{3,0},{4,5},{5,6},{6,7},{7,4},{8,9},{9,10},{10,1... | collective-permute-start | bytes 786440 | tf_op jit(solution)/shard_map/ppermute | solution.py:350
  70.3 0.2 fusion
  70.5 0.4 select_reduce_fusion
  70.8 4.2 %collective-permute-done.9.refs_3_ = bf16[2,256,256]{2,1,0:T(8,128)(2,1)S(1)} collective-permute-done((bf16[2,256,256]{2,1,0:T(8,128)(2,1)S(1)}, bf16[2,256,256]{2,1,0:T(8,128)(2,1)S(1)}, u32[]{:S(2)}, u32[]{:S(2)}) %collective-permute-start.9) | collective-permute-done | bytes 262176 | tf_op jit(solution)/shard_map/ppermute | solution.py:350
  75.0 0.0 collective-permute-start.15
  75.0 1.2 collective-permute-done.14.refs_5_
  76.3 0.4 collective-permute-start.16
  76.7 0.1 reshape.121.codes_ref
  76.8 2.4 %copy.30 = bf16[1,512,2,512]{3,1,2,0:T(8,128)(2,1)} copy(bf16[1,512,2,512]{3,2,1,0:T(2,128)(2,1)} %param.10) | data formatting | bytes 2097152 | tf_op args[2]
  79.8 2.3 %collective-permute-done.15.refs_6_ = bf16[2,256,256]{2,1,0:T(8,128)(2,1)S(1)} collective-permute-done((bf16[2,256,256]{2,1,0:T(8,128)(2,1)S(1)}, bf16[2,256,256]{2,1,0:T(8,128)(2,1)S(1)}, u32[]{:S(2)}, u32[]{:S(2)}) %collective-permute-start.15) | collective-permute-done | bytes 262176 | tf_op jit(solution)/shard_map/ppermute | solution.py:350
  82.2 6.0 %collective-permute-done.16.refs_7_ = bf16[2,256,256]{2,1,0:T(8,128)(2,1)S(1)} collective-permute-done((bf16[2,256,256]{2,1,0:T(8,128)(2,1)S(1)}, bf16[2,256,256]{2,1,0:T(8,128)(2,1)S(1)}, u32[]{:S(2)}, u32[]{:S(2)}) %collective-permute-start.16) | collective-permute-done | bytes 262176 | tf_op jit(solution)/shard_map/ppermute | solution.py:350
  88.1 0.0 collective-permute-done.17.refs_9_
  88.1 0.0 collective-permute-done.18.refs_10_
  88.1 0.0 collective-permute-done.19.refs_11_
  88.1 0.7 copy-done.8
  88.8 0.2 copy-done.7
  89.0 13.0 %block_and_pairs.1 = (bf16[2,512,512]{2,1,0:T(8,128)(2,1)}, bf16[16,80,128]{2,1,0:T(8,128)(2,1)}) custom-call(s32[1]{0:T(128)} %bitcast.base_ref, s32[1]{0:T(128)S(6)} %copy.32.slot_ref, s32[1024]{0:T(1024)S(1)} %reshape.121.codes_ref, s32[16]{0:T(128)S(1)} %get-tuple-element.24.counts_ref, bf16[2,256,256]{2,1,0:T(8,128)(2,1)S(1)} %coupling.2.refs_0_, ...), custom_call_target="tpu_custom_call" | custom-call | flops 2147483648 | bytes 12582912 | tf_op jit(solution)/shard_map/block_and_pairs/pallas_call | solution.py:190
  102.0 10.6 %all-to-all-start = ((bf16[16,80,128]{2,1,0:T(8,128)(2,1)}), bf16[16,80,128]{2,1,0:T(8,128)(2,1)S(1)}, u32[]{:S(2)}, u32[]{:S(2)}) async-start(bf16[16,80,128]{2,1,0:T(8,128)(2,1)} %get-tuple-element.19), calls=%async_computation | async-start | bytes 655360 | tf_op jit(solution)/shard_map/all_to_all | solution.py:359
  112.7 0.1 copy.23
  112.8 0.2 convert_reduce_fusion
  113.0 12.7 %all-to-all-done.parts_ref = bf16[16,80,128]{2,1,0:T(8,128)(2,1)S(1)} async-done(((bf16[16,80,128]{2,1,0:T(8,128)(2,1)}), bf16[16,80,128]{2,1,0:T(8,128)(2,1)S(1)}, u32[]{:S(2)}, u32[]{:S(2)}) %all-to-all-start) | async-done | bytes 327712 | tf_op jit(solution)/shard_map/all_to_all | solution.py:359
  125.7 0.9 pole_sum.1
  126.7 5.1 %all-to-all-start.1 = ((bf16[16,64,128]{2,1,0:T(8,128)(2,1)}), bf16[16,64,128]{2,1,0:T(8,128)(2,1)S(1)}, u32[]{:S(2)}, u32[]{:S(2)}) async-start(bf16[16,64,128]{2,1,0:T(8,128)(2,1)} %pole_sum.1), calls=%async_computation.1 | async-start | bytes 524288 | tf_op jit(solution)/shard_map/all_to_all | solution.py:362
  131.8 0.1 maximum_convert_fusion.projector_ref
  131.9 2.0 %copy.25 = bf16[1,512,2,512]{3,2,1,0:T(2,128)(2,1)} copy(bf16[1,512,2,512]{3,1,2,0:T(8,128)(2,1)S(1)} %bitcast.36) | data formatting | bytes 2097152
  134.0 6.9 %all-to-all-done.1 = bf16[16,64,128]{2,1,0:T(8,128)(2,1)S(1)} async-done(((bf16[16,64,128]{2,1,0:T(8,128)(2,1)}), bf16[16,64,128]{2,1,0:T(8,128)(2,1)S(1)}, u32[]{:S(2)}, u32[]{:S(2)}) %all-to-all-start.1) | async-done | bytes 262176 | tf_op jit(solution)/shard_map/all_to_all | solution.py:362
  140.9 1.8 %density.1 = f32[512,128]{1,0:T(8,128)} custom-call(s32[512]{0:T(512)S(1)} %multiply_add_fusion.index_ref, bf16[1024,128]{1,0:T(8,128)(2,1)S(1)} %bitcast.30, f32[512,128]{1,0:T(8,128)S(1)} %maximum_convert_fusion.projector_ref), custom_call_target="tpu_custom_call" | custom-call | tf_op jit(solution)/shard_map/density/pallas_call | solution.py:268
  (20 shorter events, 0.1 us)
Async XLA Ops:
  0.6 1.2 copy-start.3
  1.8 59.2 %copy-start.1 = (bf16[1,512,2,256]{3,1,2,0:T(8,128)(2,1)}, bf16[1,512,2,256]{3,1,2,0:T(8,128)(2,1)S(1)}, u32[]{:S(2)}) copy-start(bf16[1,512,2,256]{3,1,2,0:T(8,128)(2,1)S(1)} %copy.31) | copy-start | bytes 1572868
  1.8 36.4 %copy-start.5 = (s32[8192]{0:T(1024)S(1)}, s32[8192]{0:T(1024)}, u32[]{:S(2)}) copy-start(s32[8192]{0:T(1024)} %param.13) | copy-start | bytes 98308
  1.8 36.5 %copy-start.6 = (s32[8192]{0:T(1024)S(1)}, s32[8192]{0:T(1024)}, u32[]{:S(2)}) copy-start(s32[8192]{0:T(1024)} %param.14) | copy-start | bytes 98308
  1.9 12.8 %collective-permute-start = (bf16[2,256,256]{2,1,0:T(8,128)(2,1)S(1)}, bf16[2,256,256]{2,1,0:T(8,128)(2,1)S(1)}, u32[]{:S(2)}, u32[]{:S(2)}) collective-permute-start(bf16[2,256,256]{2,1,0:T(8,128)(2,1)S(1)} %get-tuple-element.12), channel_id=1, source_target_pairs={{0,0},{1,5},{2,10},{3,15},{4,1},{5,6},{6,11},{7,12},{8,2},{9,7},{1... | collective-permute-start | bytes 786440 | tf_op jit(solution)/shard_map/ppermute | solution.py:331
  2.7 17.8 %collective-permute-start.4 = (bf16[2,256,256]{2,1,0:T(8,128)(2,1)S(1)}, bf16[2,256,256]{2,1,0:T(8,128)(2,1)S(1)}, u32[]{:S(2)}, u32[]{:S(2)}) collective-permute-start(bf16[2,256,256]{2,1,0:T(8,128)(2,1)S(1)} %get-tuple-element.13.t0), channel_id=1, source_target_pairs={{0,4},{4,8},{8,12},{12,0},{1,5},{5,9},{9,13},{13,1},{2,6},{6,10},{... | collective-permute-start | bytes 786440 | tf_op jit(solution)/shard_map/ppermute | solution.py:330
  7.3 30.3 %collective-permute-start.5 = (bf16[2,256,256]{2,1,0:T(8,128)(2,1)S(1)}, bf16[2,256,256]{2,1,0:T(8,128)(2,1)S(1)}, u32[]{:S(2)}, u32[]{:S(2)}) collective-permute-start(bf16[2,256,256]{2,1,0:T(8,128)(2,1)S(1)} %get-tuple-element.13.t0), channel_id=1, source_target_pairs={{0,8},{4,12},{8,0},{12,4},{1,9},{5,13},{9,1},{13,5},{2,10},{6,14},... | collective-permute-start | bytes 786440 | tf_op jit(solution)/shard_map/ppermute | solution.py:330
  10.9 27.4 %collective-permute-start.6 = (bf16[2,256,256]{2,1,0:T(8,128)(2,1)S(1)}, bf16[2,256,256]{2,1,0:T(8,128)(2,1)S(1)}, u32[]{:S(2)}, u32[]{:S(2)}) collective-permute-start(bf16[2,256,256]{2,1,0:T(8,128)(2,1)S(1)} %get-tuple-element.13.t0), channel_id=1, source_target_pairs={{0,12},{4,0},{8,4},{12,8},{1,13},{5,1},{9,5},{13,9},{2,14},{6,2},{... | collective-permute-start | bytes 786440 | tf_op jit(solution)/shard_map/ppermute | solution.py:330
  12.4 27.9 %collective-permute-start.1 = (bf16[2,256,256]{2,1,0:T(8,128)(2,1)S(1)}, bf16[2,256,256]{2,1,0:T(8,128)(2,1)S(1)}, u32[]{:S(2)}, u32[]{:S(2)}) collective-permute-start(bf16[2,256,256]{2,1,0:T(8,128)(2,1)S(1)} %get-tuple-element.12), channel_id=1, source_target_pairs={{0,1},{1,6},{2,11},{3,12},{4,2},{5,7},{6,8},{7,13},{8,3},{9,4},{10... | collective-permute-start | bytes 786440 | tf_op jit(solution)/shard_map/ppermute | solution.py:331
  14.7 29.9 %collective-permute-start.2 = (bf16[2,256,256]{2,1,0:T(8,128)(2,1)S(1)}, bf16[2,256,256]{2,1,0:T(8,128)(2,1)S(1)}, u32[]{:S(2)}, u32[]{:S(2)}) collective-permute-start(bf16[2,256,256]{2,1,0:T(8,128)(2,1)S(1)} %get-tuple-element.12), channel_id=1, source_target_pairs={{0,2},{1,7},{2,8},{3,13},{4,3},{5,4},{6,9},{7,14},{8,0},{9,5},{10,... | collective-permute-start | bytes 786440 | tf_op jit(solution)/shard_map/ppermute | solution.py:331
  20.5 29.6 %collective-permute-start.3 = (bf16[2,256,256]{2,1,0:T(8,128)(2,1)S(1)}, bf16[2,256,256]{2,1,0:T(8,128)(2,1)S(1)}, u32[]{:S(2)}, u32[]{:S(2)}) collective-permute-start(bf16[2,256,256]{2,1,0:T(8,128)(2,1)S(1)} %get-tuple-element.12), channel_id=1, source_target_pairs={{0,3},{1,4},{2,9},{3,14},{4,0},{5,5},{6,10},{7,15},{8,1},{9,6},{10... | collective-permute-start | bytes 786440 | tf_op jit(solution)/shard_map/ppermute | solution.py:331
  37.6 15.8 %collective-permute-start.10 = (bf16[2,256,256]{2,1,0:T(8,128)(2,1)S(1)}, bf16[2,256,256]{2,1,0:T(8,128)(2,1)S(1)}, u32[]{:S(2)}, u32[]{:S(2)}) collective-permute-start(bf16[2,256,256]{2,1,0:T(8,128)(2,1)S(1)} %get-tuple-element.16), channel_id=1, source_target_pairs={{0,0},{1,5},{2,10},{3,15},{4,1},{5,6},{6,11},{7,12},{8,2},{9,7},{1... | collective-permute-start | bytes 786440 | tf_op jit(solution)/shard_map/ppermute | solution.py:333
  38.3 16.4 %collective-permute-start.11 = (bf16[2,256,256]{2,1,0:T(8,128)(2,1)S(1)}, bf16[2,256,256]{2,1,0:T(8,128)(2,1)S(1)}, u32[]{:S(2)}, u32[]{:S(2)}) collective-permute-start(bf16[2,256,256]{2,1,0:T(8,128)(2,1)S(1)} %get-tuple-element.16), channel_id=1, source_target_pairs={{0,1},{1,6},{2,11},{3,12},{4,2},{5,7},{6,8},{7,13},{8,3},{9,4},{10... | collective-permute-start | bytes 786440 | tf_op jit(solution)/shard_map/ppermute | solution.py:333
  40.3 14.5 %collective-permute-start.12 = (bf16[2,256,256]{2,1,0:T(8,128)(2,1)S(1)}, bf16[2,256,256]{2,1,0:T(8,128)(2,1)S(1)}, u32[]{:S(2)}, u32[]{:S(2)}) collective-permute-start(bf16[2,256,256]{2,1,0:T(8,128)(2,1)S(1)} %get-tuple-element.16), channel_id=1, source_target_pairs={{0,2},{1,7},{2,8},{3,13},{4,3},{5,4},{6,9},{7,14},{8,0},{9,5},{10,... | collective-permute-start | bytes 786440 | tf_op jit(solution)/shard_map/ppermute | solution.py:333
  44.7 16.4 %collective-permute-start.13 = (bf16[2,256,256]{2,1,0:T(8,128)(2,1)S(1)}, bf16[2,256,256]{2,1,0:T(8,128)(2,1)S(1)}, u32[]{:S(2)}, u32[]{:S(2)}) collective-permute-start(bf16[2,256,256]{2,1,0:T(8,128)(2,1)S(1)} %get-tuple-element.16), channel_id=1, source_target_pairs={{0,3},{1,4},{2,9},{3,14},{4,0},{5,5},{6,10},{7,15},{8,1},{9,6},{10... | collective-permute-start | bytes 786440 | tf_op jit(solution)/shard_map/ppermute | solution.py:333
  50.9 17.9 %collective-permute-start.7 = (bf16[2,256,256]{2,1,0:T(8,128)(2,1)S(1)}, bf16[2,256,256]{2,1,0:T(8,128)(2,1)S(1)}, u32[]{:S(2)}, u32[]{:S(2)}) collective-permute-start(bf16[2,256,256]{2,1,0:T(8,128)(2,1)S(1)} %coupling.2.refs_0_), channel_id=1, source_target_pairs={{0,1},{1,2},{2,3},{3,0},{4,5},{5,6},{6,7},{7,4},{8,9},{9,10},{10,1... | collective-permute-start | bytes 786440 | tf_op jit(solution)/shard_map/ppermute | solution.py:350
  53.3 15.5 %collective-permute-start.8 = (bf16[2,256,256]{2,1,0:T(8,128)(2,1)S(1)}, bf16[2,256,256]{2,1,0:T(8,128)(2,1)S(1)}, u32[]{:S(2)}, u32[]{:S(2)}) collective-permute-start(bf16[2,256,256]{2,1,0:T(8,128)(2,1)S(1)} %coupling.2.refs_0_), channel_id=1, source_target_pairs={{0,2},{1,3},{2,0},{3,1},{4,6},{5,7},{6,4},{7,5},{8,10},{9,11},{10,... | collective-permute-start | bytes 786440 | tf_op jit(solution)/shard_map/ppermute | solution.py:350
  54.8 33.4 %collective-permute-start.17 = (bf16[2,512,256]{2,1,0:T(8,128)(2,1)S(1)}, bf16[2,512,256]{2,1,0:T(8,128)(2,1)}, u32[]{:S(2)}, u32[]{:S(2)}) collective-permute-start(bf16[2,512,256]{2,1,0:T(8,128)(2,1)S(1)} %bitcast.32), channel_id=1, source_target_pairs={{0,4},{4,8},{8,12},{12,0},{1,5},{5,9},{9,13},{13,1},{2,6},{6,10},{... | collective-permute-start | bytes 1572872 | tf_op jit(solution)/shard_map/ppermute | solution.py:352
  54.8 33.4 %collective-permute-start.18 = (bf16[2,512,256]{2,1,0:T(8,128)(2,1)S(1)}, bf16[2,512,256]{2,1,0:T(8,128)(2,1)}, u32[]{:S(2)}, u32[]{:S(2)}) collective-permute-start(bf16[2,512,256]{2,1,0:T(8,128)(2,1)S(1)} %bitcast.33), channel_id=1, source_target_pairs={{0,8},{4,12},{8,0},{12,4},{1,9},{5,13},{9,1},{13,5},{2,10},{6,14},... | collective-permute-start | bytes 1572872 | tf_op jit(solution)/shard_map/ppermute | solution.py:352
  61.0 27.1 %collective-permute-start.19 = (bf16[2,512,256]{2,1,0:T(8,128)(2,1)S(1)}, bf16[2,512,256]{2,1,0:T(8,128)(2,1)S(1)}, u32[]{:S(2)}, u32[]{:S(2)}) collective-permute-start(bf16[2,512,256]{2,1,0:T(8,128)(2,1)S(1)} %bitcast.34), channel_id=1, source_target_pairs={{0,12},{4,0},{8,4},{12,8},{1,13},{5,1},{9,5},{13,9},{2,14},{6,2},{... | collective-permute-start | bytes 1572872 | tf_op jit(solution)/shard_map/ppermute | solution.py:352
  68.8 6.2 %collective-permute-start.9 = (bf16[2,256,256]{2,1,0:T(8,128)(2,1)S(1)}, bf16[2,256,256]{2,1,0:T(8,128)(2,1)S(1)}, u32[]{:S(2)}, u32[]{:S(2)}) collective-permute-start(bf16[2,256,256]{2,1,0:T(8,128)(2,1)S(1)} %coupling.2.refs_0_), channel_id=1, source_target_pairs={{0,3},{1,0},{2,1},{3,2},{4,7},{5,4},{6,5},{7,6},{8,11},{9,8},{10,9... | collective-permute-start | bytes 786440 | tf_op jit(solution)/shard_map/ppermute | solution.py:350
  68.8 7.5 %collective-permute-start.14 = (bf16[2,256,256]{2,1,0:T(8,128)(2,1)S(1)}, bf16[2,256,256]{2,1,0:T(8,128)(2,1)S(1)}, u32[]{:S(2)}, u32[]{:S(2)}) collective-permute-start(bf16[2,256,256]{2,1,0:T(8,128)(2,1)S(1)} %coupling.3.refs_4_), channel_id=1, source_target_pairs={{0,1},{1,2},{2,3},{3,0},{4,5},{5,6},{6,7},{7,4},{8,9},{9,10},{10,1... | collective-permute-start | bytes 786440 | tf_op jit(solution)/shard_map/ppermute | solution.py:350
  75.0 7.1 %collective-permute-start.15 = (bf16[2,256,256]{2,1,0:T(8,128)(2,1)S(1)}, bf16[2,256,256]{2,1,0:T(8,128)(2,1)S(1)}, u32[]{:S(2)}, u32[]{:S(2)}) collective-permute-start(bf16[2,256,256]{2,1,0:T(8,128)(2,1)S(1)} %coupling.3.refs_4_), channel_id=1, source_target_pairs={{0,2},{1,3},{2,0},{3,1},{4,6},{5,7},{6,4},{7,5},{8,10},{9,11},{10,... | collective-permute-start | bytes 786440 | tf_op jit(solution)/shard_map/ppermute | solution.py:350
  76.3 11.9 %collective-permute-start.16 = (bf16[2,256,256]{2,1,0:T(8,128)(2,1)S(1)}, bf16[2,256,256]{2,1,0:T(8,128)(2,1)S(1)}, u32[]{:S(2)}, u32[]{:S(2)}) collective-permute-start(bf16[2,256,256]{2,1,0:T(8,128)(2,1)S(1)} %coupling.3.refs_4_), channel_id=1, source_target_pairs={{0,3},{1,0},{2,1},{3,2},{4,7},{5,4},{6,5},{7,6},{8,11},{9,8},{10,9... | collective-permute-start | bytes 786440 | tf_op jit(solution)/shard_map/ppermute | solution.py:350
  88.1 0.7 copy-start.8
  88.1 0.9 copy-start.7
  89.0 23.7 %copy-start.4 = (bf16[512,64]{0,1:T(8,128)(2,1)S(1)}, bf16[512,64]{0,1:T(8,128)(2,1)}, u32[]{:S(2)}) copy-start(bf16[512,64]{0,1:T(8,128)(2,1)} %param.15) | copy-start | bytes 196612
  89.0 36.7 %copy-start = (f32[256,2]{0,1:T(2,128)S(1)}, f32[256,2]{0,1:T(2,128)}, u32[]{:S(2)}) copy-start(f32[256,2]{0,1:T(2,128)} %param.11) | copy-start | bytes 6148
  102.0 29.9 %copy-start.2 = (bf16[2,512,512]{2,1,0:T(8,128)(2,1)S(1)}, bf16[2,512,512]{2,1,0:T(8,128)(2,1)}, u32[]{:S(2)}) copy-start(bf16[2,512,512]{2,1,0:T(8,128)(2,1)} %get-tuple-element.18) | copy-start | bytes 3145732
  102.0 23.7 %all-to-all-start = ((bf16[16,80,128]{2,1,0:T(8,128)(2,1)}), bf16[16,80,128]{2,1,0:T(8,128)(2,1)S(1)}, u32[]{:S(2)}, u32[]{:S(2)}) async-start(bf16[16,80,128]{2,1,0:T(8,128)(2,1)} %get-tuple-element.19), calls=%async_computation | async-start | bytes 655360 | tf_op jit(solution)/shard_map/all_to_all | solution.py:359
  126.7 14.2 %all-to-all-start.1 = ((bf16[16,64,128]{2,1,0:T(8,128)(2,1)}), bf16[16,64,128]{2,1,0:T(8,128)(2,1)S(1)}, u32[]{:S(2)}, u32[]{:S(2)}) async-start(bf16[16,64,128]{2,1,0:T(8,128)(2,1)} %pole_sum.1), calls=%async_computation.1 | async-start | bytes 524288 | tf_op jit(solution)/shard_map/all_to_all | solution.py:362

commit v8 on v7

--- a/solution.py
+++ b/solution.py
@@ -149,7 +149,7 @@
         row = lax.broadcasted_iota(jnp.int32, fold.shape, 0)
         lane = lax.broadcasted_iota(jnp.int32, fold.shape, 1)
         fold[...] = jnp.where(lane // 8 == row, 1.0, 0.0).astype(jnp.bfloat16)
-        slot = jnp.full((16, 128), slot_ref[0], jnp.int32).astype(jnp.float32)
+        slot = jnp.full((8, 128), slot_ref[0], jnp.int32).astype(jnp.float32)
         for owner in range(pairs_ref.shape[0]):
             pairs_ref[owner, SLOTS:, :] = slot.astype(jnp.bfloat16)
 
@@ -191,7 +191,7 @@
         block_kernel,
         out_shape=(
             jax.ShapeDtypeStruct((2, rows, columns), jnp.bfloat16),
-            jax.ShapeDtypeStruct((owners, SLOTS + 16, 2 * B * B), jnp.bfloat16),
+            jax.ShapeDtypeStruct((owners, SLOTS + 8, 2 * B * B), jnp.bfloat16),
         ),
         grid_spec=pltpu.PrefetchScalarGridSpec(
             num_scalar_prefetch=4,
@@ -199,7 +199,7 @@
             in_specs=[whole(couplings[0].shape)] * 8
             + [whole(lowers[0].shape)] * 4
             + [row_spec(columns), whole(masks.shape)],
-            out_specs=(row_spec(columns), whole((owners, SLOTS + 16, 2 * B * B))),
+            out_specs=(row_spec(columns), whole((owners, SLOTS + 8, 2 * B * B))),
             scratch_shapes=[
                 pltpu.VMEM((4 * (2 * rows + 2 * inner), 128), jnp.bfloat16),
                 pltpu.VMEM((owners * SLOTS * 16, 128), jnp.bfloat16),
@@ -349,7 +349,11 @@
         couplings += [coupling] + [
             lax.ppermute(coupling, "col", ring(d, COLS)) for d in range(1, COLS)
         ]
-    lowers = [lower] + [lax.ppermute(lower_late, "row", ring(e, ROWS)) for e in range(1, ROWS)]
+    lower_early, _ = lax.optimization_barrier((lower, second[1]))
+    lowers = [lower] + [
+        lax.ppermute(lower_early if e == 2 else lower_late, "row", ring(e, ROWS))
+        for e in range(1, ROWS)
+    ]
 
     block, pairs = block_call(
         base, pole_slot, codes, counts, couplings, lowers, diag, masks

time: 144 us -> 142 us (0.986)
  waiting for transfers between devices: 41.6 us -> 34.6 us
  starting transfers between devices: 74.4 us -> 80.5 us
    ppermute x6, waiting for transfers between devices: 20.7 us -> 12.3 us  [local(): lax.ppermute(coupling, 'col', ring(d, COLS))]
    ppermute x6, starting transfers between devices: 4.35 us -> 8.38 us  [local(): lax.ppermute(coupling, 'col', ring(d, COLS))]
    ppermute x4, waiting for transfers between devices: 1.2 us -> 3.75 us  [local(): lax.ppermute(second_half, pair_axes, to_process_rows(e))]
    ppermute x3, starting transfers between devices: 6.27 us -> 8.61 us  [local(): lax.ppermute(lower_early if e == 2 else lower_late, 'row', ring(e, ROWS))]
where the time goes in v8:
time: 142 us
  starting transfers between devices  80.5 us (57%)
  waiting for transfers between devices  34.6 us (24%)
  Pallas kernels  16.9 us (12%)
  local copies, waits for them, and re-layouts  6.73 us (5%)
  between operations  1.68 us (1%)
    ppermute x4, starting transfers between devices, local(): lax.ppermute(halves[0], pair_axes, to_process_rows(e))  25.9 us
    pallas_call x1, Pallas kernels, block_call(): pl.pallas_call(block_kernel, out_shape=(jax.ShapeDtypeStruct((2, rows, co...  12.7 us
    ppermute x6, waiting for transfers between devices, local(): lax.ppermute(coupling, 'col', ring(d, COLS))  12.3 us
    all_to_all x1, waiting for transfers between devices, local(): parts = lax.all_to_all(pairs, POLE, 0, 0, tiled=True)  12 us
    ppermute x4, starting transfers between devices, local(): lax.ppermute(second_half, pair_axes, to_process_rows(e))  11.5 us
    all_to_all x1, starting transfers between devices, local(): parts = lax.all_to_all(pairs, POLE, 0, 0, tiled=True)  10.3 us
    ppermute x3, starting transfers between devices, local(): lax.ppermute(trail, 'row', ring(e, ROWS))  9.64 us
    ppermute x3, starting transfers between devices, local(): lax.ppermute(lower_early if e == 2 else lower_late, 'row', ring(e, ROWS))  8.61 us
  transfers between devices with their start and end apart: 22, of which 8 were waited for; matrix products, arithmetic and copies ran while one was open for 4% of the time, Pallas kernels for 1%

profile of v8, /device:TPU:1, one launch (start us, length us, event | category | flops | bytes accessed | tf_op | source)
XLA Modules:
  0.0 141.5 jit_solution(16110591059025393103)
XLA Ops:
  0.6 1.2 copy.31
  1.8 0.0 copy-start.5
  1.8 0.0 copy-start.6
  1.8 0.1 slice_bitcast_fusion
  1.9 0.8 collective-permute-start
  2.7 4.5 %collective-permute-start.4 = (bf16[2,256,256]{2,1,0:T(8,128)(2,1)S(1)}, bf16[2,256,256]{2,1,0:T(8,128)(2,1)S(1)}, u32[]{:S(2)}, u32[]{:S(2)}) collective-permute-start(bf16[2,256,256]{2,1,0:T(8,128)(2,1)S(1)} %get-tuple-element.14.t0), channel_id=1, source_target_pairs={{0,4},{4,8},{8,12},{12,0},{1,5},{5,9},{9,13},{13,1},{2,6},{6,10},{... | collective-permute-start | bytes 786440 | tf_op jit(solution)/shard_map/ppermute | solution.py:330
  7.3 3.7 %collective-permute-start.5 = (bf16[2,256,256]{2,1,0:T(8,128)(2,1)S(1)}, bf16[2,256,256]{2,1,0:T(8,128)(2,1)S(1)}, u32[]{:S(2)}, u32[]{:S(2)}) collective-permute-start(bf16[2,256,256]{2,1,0:T(8,128)(2,1)S(1)} %get-tuple-element.14.t0), channel_id=1, source_target_pairs={{0,8},{4,12},{8,0},{12,4},{1,9},{5,13},{9,1},{13,5},{2,10},{6,14},... | collective-permute-start | bytes 786440 | tf_op jit(solution)/shard_map/ppermute | solution.py:330
  10.9 1.4 %collective-permute-start.6 = (bf16[2,256,256]{2,1,0:T(8,128)(2,1)S(1)}, bf16[2,256,256]{2,1,0:T(8,128)(2,1)S(1)}, u32[]{:S(2)}, u32[]{:S(2)}) collective-permute-start(bf16[2,256,256]{2,1,0:T(8,128)(2,1)S(1)} %get-tuple-element.14.t0), channel_id=1, source_target_pairs={{0,12},{4,0},{8,4},{12,8},{1,13},{5,1},{9,5},{13,9},{2,14},{6,2},{... | collective-permute-start | bytes 786440 | tf_op jit(solution)/shard_map/ppermute | solution.py:330
  12.4 2.3 %collective-permute-start.1 = (bf16[2,256,256]{2,1,0:T(8,128)(2,1)S(1)}, bf16[2,256,256]{2,1,0:T(8,128)(2,1)S(1)}, u32[]{:S(2)}, u32[]{:S(2)}) collective-permute-start(bf16[2,256,256]{2,1,0:T(8,128)(2,1)S(1)} %get-tuple-element.13), channel_id=1, source_target_pairs={{0,1},{1,6},{2,11},{3,12},{4,2},{5,7},{6,8},{7,13},{8,3},{9,4},{10... | collective-permute-start | bytes 786440 | tf_op jit(solution)/shard_map/ppermute | solution.py:331
  14.7 0.0 collective-permute-done.l0
  14.7 5.8 %collective-permute-start.2 = (bf16[2,256,256]{2,1,0:T(8,128)(2,1)S(1)}, bf16[2,256,256]{2,1,0:T(8,128)(2,1)S(1)}, u32[]{:S(2)}, u32[]{:S(2)}) collective-permute-start(bf16[2,256,256]{2,1,0:T(8,128)(2,1)S(1)} %get-tuple-element.13), channel_id=1, source_target_pairs={{0,2},{1,7},{2,8},{3,13},{4,3},{5,4},{6,9},{7,14},{8,0},{9,5},{10,... | collective-permute-start | bytes 786440 | tf_op jit(solution)/shard_map/ppermute | solution.py:331
  20.5 0.0 collective-permute-done.4.t1
  20.5 17.0 %collective-permute-start.3 = (bf16[2,256,256]{2,1,0:T(8,128)(2,1)S(1)}, bf16[2,256,256]{2,1,0:T(8,128)(2,1)S(1)}, u32[]{:S(2)}, u32[]{:S(2)}) collective-permute-start(bf16[2,256,256]{2,1,0:T(8,128)(2,1)S(1)} %get-tuple-element.13), channel_id=1, source_target_pairs={{0,3},{1,4},{2,9},{3,14},{4,0},{5,5},{6,10},{7,15},{8,1},{9,6},{10... | collective-permute-start | bytes 786440 | tf_op jit(solution)/shard_map/ppermute | solution.py:331
  37.5 0.0 collective-permute-done.5.t2
  37.6 1.9 %collective-permute-start.11 = (bf16[2,256,256]{2,1,0:T(8,128)(2,1)S(1)}, bf16[2,256,256]{2,1,0:T(8,128)(2,1)S(1)}, u32[]{:S(2)}, u32[]{:S(2)}) collective-permute-start(bf16[2,256,256]{2,1,0:T(8,128)(2,1)S(1)} %get-tuple-element.17), channel_id=1, source_target_pairs={{0,1},{1,6},{2,11},{3,12},{4,2},{5,7},{6,8},{7,13},{8,3},{9,4},{10... | collective-permute-start | bytes 786440 | tf_op jit(solution)/shard_map/ppermute | solution.py:333
  39.6 0.0 collective-permute-done.6.t3
  39.6 0.7 collective-permute-start.10
  40.3 0.0 collective-permute-done.1.l1
  40.3 2.3 %collective-permute-start.12 = (bf16[2,256,256]{2,1,0:T(8,128)(2,1)S(1)}, bf16[2,256,256]{2,1,0:T(8,128)(2,1)S(1)}, u32[]{:S(2)}, u32[]{:S(2)}) collective-permute-start(bf16[2,256,256]{2,1,0:T(8,128)(2,1)S(1)} %get-tuple-element.17), channel_id=1, source_target_pairs={{0,2},{1,7},{2,8},{3,13},{4,3},{5,4},{6,9},{7,14},{8,0},{9,5},{10,... | collective-permute-start | bytes 786440 | tf_op jit(solution)/shard_map/ppermute | solution.py:333
  42.5 0.0 collective-permute-done.2.l2
  42.5 6.7 %collective-permute-start.13 = (bf16[2,256,256]{2,1,0:T(8,128)(2,1)S(1)}, bf16[2,256,256]{2,1,0:T(8,128)(2,1)S(1)}, u32[]{:S(2)}, u32[]{:S(2)}) collective-permute-start(bf16[2,256,256]{2,1,0:T(8,128)(2,1)S(1)} %get-tuple-element.17), channel_id=1, source_target_pairs={{0,3},{1,4},{2,9},{3,14},{4,0},{5,5},{6,10},{7,15},{8,1},{9,6},{10... | collective-permute-start | bytes 786440 | tf_op jit(solution)/shard_map/ppermute | solution.py:333
  49.2 0.0 collective-permute-done.3.l3
  49.2 0.7 coupling.2.refs_0_
  50.0 2.1 %collective-permute-start.7 = (bf16[2,256,256]{2,1,0:T(8,128)(2,1)S(1)}, bf16[2,256,256]{2,1,0:T(8,128)(2,1)S(1)}, u32[]{:S(2)}, u32[]{:S(2)}) collective-permute-start(bf16[2,256,256]{2,1,0:T(8,128)(2,1)S(1)} %coupling.2.refs_0_), channel_id=1, source_target_pairs={{0,1},{1,2},{2,3},{3,0},{4,5},{5,6},{6,7},{7,4},{8,9},{9,10},{10,1... | collective-permute-start | bytes 786440 | tf_op jit(solution)/shard_map/ppermute | solution.py:350
  52.1 1.2 collective-permute-done.11.l1
  53.3 0.0 collective-permute-start.8
  53.3 0.2 convert_reduce_fusion.1
  53.5 0.0 collective-permute-done.10.l0
  53.6 0.1 collective-permute-start.17
  53.6 0.0 collective-permute-done.12.l2
  53.7 5.7 %collective-permute-start.19 = (bf16[2,512,256]{2,1,0:T(8,128)(2,1)S(1)}, bf16[2,512,256]{2,1,0:T(8,128)(2,1)}, u32[]{:S(2)}, u32[]{:S(2)}) collective-permute-start(bf16[2,512,256]{2,1,0:T(8,128)(2,1)S(1)} %bitcast.33), channel_id=1, source_target_pairs={{0,12},{4,0},{8,4},{12,8},{1,13},{5,1},{9,5},{13,9},{2,14},{6,2},{... | collective-permute-start | bytes 1572872 | tf_op jit(solution)/shard_map/ppermute | solution.py:354
  59.3 2.6 %collective-permute-done.13.l3 = bf16[2,256,256]{2,1,0:T(8,128)(2,1)S(1)} collective-permute-done((bf16[2,256,256]{2,1,0:T(8,128)(2,1)S(1)}, bf16[2,256,256]{2,1,0:T(8,128)(2,1)S(1)}, u32[]{:S(2)}, u32[]{:S(2)}) %collective-permute-start.13) | collective-permute-done | bytes 262176 | tf_op jit(solution)/shard_map/ppermute | solution.py:333
  61.9 4.0 %collective-permute-start.9 = (bf16[2,256,256]{2,1,0:T(8,128)(2,1)S(1)}, bf16[2,256,256]{2,1,0:T(8,128)(2,1)S(1)}, u32[]{:S(2)}, u32[]{:S(2)}) collective-permute-start(bf16[2,256,256]{2,1,0:T(8,128)(2,1)S(1)} %coupling.2.refs_0_), channel_id=1, source_target_pairs={{0,3},{1,0},{2,1},{3,2},{4,7},{5,4},{6,5},{7,6},{8,11},{9,8},{10,9... | collective-permute-start | bytes 786440 | tf_op jit(solution)/shard_map/ppermute | solution.py:350
  65.9 0.7 coupling.3.refs_4_
  66.6 0.0 collective-permute-done.7.refs_1_
  66.6 0.1 collective-permute-start.14
  66.7 0.0 collective-permute-done.8.refs_2_
  66.8 2.9 %collective-permute-start.18 = (bf16[2,512,256]{2,1,0:T(8,128)(2,1)S(1)}, bf16[2,512,256]{2,1,0:T(8,128)(2,1)S(1)}, u32[]{:S(2)}, u32[]{:S(2)}) collective-permute-start(bf16[2,512,256]{2,1,0:T(8,128)(2,1)S(1)} %bitcast.34), channel_id=1, source_target_pairs={{0,8},{4,12},{8,0},{12,4},{1,9},{5,13},{9,1},{13,5},{2,10},{6,14},... | collective-permute-start | bytes 1572872 | tf_op jit(solution)/shard_map/ppermute | solution.py:354
  69.6 0.2 fusion
  69.8 0.4 select_reduce_fusion
  70.2 2.3 %collective-permute-done.9.refs_3_ = bf16[2,256,256]{2,1,0:T(8,128)(2,1)S(1)} collective-permute-done((bf16[2,256,256]{2,1,0:T(8,128)(2,1)S(1)}, bf16[2,256,256]{2,1,0:T(8,128)(2,1)S(1)}, u32[]{:S(2)}, u32[]{:S(2)}) %collective-permute-start.9) | collective-permute-done | bytes 262176 | tf_op jit(solution)/shard_map/ppermute | solution.py:350
  72.5 1.2 collective-permute-start.15
  73.7 1.3 collective-permute-done.14.refs_5_
  75.0 0.9 collective-permute-start.16
  75.9 0.1 reshape.121.codes_ref
  76.0 2.4 %copy.30 = bf16[1,512,2,512]{3,1,2,0:T(8,128)(2,1)} copy(bf16[1,512,2,512]{3,2,1,0:T(2,128)(2,1)} %param.10) | data formatting | bytes 2097152 | tf_op args[2]
  79.0 0.5 collective-permute-done.15.refs_6_
  79.5 8.2 %collective-permute-done.16.refs_7_ = bf16[2,256,256]{2,1,0:T(8,128)(2,1)S(1)} collective-permute-done((bf16[2,256,256]{2,1,0:T(8,128)(2,1)S(1)}, bf16[2,256,256]{2,1,0:T(8,128)(2,1)S(1)}, u32[]{:S(2)}, u32[]{:S(2)}) %collective-permute-start.16) | collective-permute-done | bytes 262176 | tf_op jit(solution)/shard_map/ppermute | solution.py:350
  87.7 0.0 collective-permute-done.17.refs_9_
  87.7 0.0 collective-permute-done.19.refs_11_
  87.7 0.0 collective-permute-done.18.refs_10_
  87.7 0.7 copy-done.8
  88.4 0.2 copy-done.7
  88.6 12.7 %block_and_pairs.1 = (bf16[2,512,512]{2,1,0:T(8,128)(2,1)}, bf16[16,72,128]{2,1,0:T(8,128)(2,1)}) custom-call(s32[1]{0:T(128)} %bitcast.base_ref, s32[1]{0:T(128)S(6)} %copy.32.slot_ref, s32[1024]{0:T(1024)S(1)} %reshape.121.codes_ref, s32[16]{0:T(128)S(1)} %get-tuple-element.26.counts_ref, bf16[2,256,256]{2,1,0:T(8,128)(2,1)S(1)} %coupling.2.refs_0_, ...), custom_call_target="tpu_custom_call" | custom-call | flops 2147483648 | bytes 12582912 | tf_op jit(solution)/shard_map/block_and_pairs/pallas_call | solution.py:190
  101.3 10.3 %all-to-all-start = ((bf16[16,72,128]{2,1,0:T(8,128)(2,1)}), bf16[16,72,128]{2,1,0:T(8,128)(2,1)S(1)}, u32[]{:S(2)}, u32[]{:S(2)}) async-start(bf16[16,72,128]{2,1,0:T(8,128)(2,1)} %get-tuple-element.21), calls=%async_computation | async-start | bytes 589824 | tf_op jit(solution)/shard_map/all_to_all | solution.py:363
  111.6 0.1 copy.23
  111.8 0.2 convert_reduce_fusion
  112.0 12.0 %all-to-all-done.parts_ref = bf16[16,72,128]{2,1,0:T(8,128)(2,1)S(1)} async-done(((bf16[16,72,128]{2,1,0:T(8,128)(2,1)}), bf16[16,72,128]{2,1,0:T(8,128)(2,1)S(1)}, u32[]{:S(2)}, u32[]{:S(2)}) %all-to-all-start) | async-done | bytes 294944 | tf_op jit(solution)/shard_map/all_to_all | solution.py:363
  124.0 0.9 pole_sum.1
  124.9 6.1 %all-to-all-start.1 = ((bf16[16,64,128]{2,1,0:T(8,128)(2,1)}), bf16[16,64,128]{2,1,0:T(8,128)(2,1)S(1)}, u32[]{:S(2)}, u32[]{:S(2)}) async-start(bf16[16,64,128]{2,1,0:T(8,128)(2,1)} %pole_sum.1), calls=%async_computation.1 | async-start | bytes 524288 | tf_op jit(solution)/shard_map/all_to_all | solution.py:366
  131.0 0.1 maximum_convert_fusion.projector_ref
  131.2 2.0 %copy.25 = bf16[1,512,2,512]{3,2,1,0:T(2,128)(2,1)} copy(bf16[1,512,2,512]{3,1,2,0:T(8,128)(2,1)S(1)} %bitcast.36) | data formatting | bytes 2097152
  133.2 6.5 %all-to-all-done.1 = bf16[16,64,128]{2,1,0:T(8,128)(2,1)S(1)} async-done(((bf16[16,64,128]{2,1,0:T(8,128)(2,1)}), bf16[16,64,128]{2,1,0:T(8,128)(2,1)S(1)}, u32[]{:S(2)}, u32[]{:S(2)}) %all-to-all-start.1) | async-done | bytes 262176 | tf_op jit(solution)/shard_map/all_to_all | solution.py:366
  139.7 1.8 %density.1 = f32[512,128]{1,0:T(8,128)} custom-call(s32[512]{0:T(512)S(1)} %multiply_add_fusion.index_ref, bf16[1024,128]{1,0:T(8,128)(2,1)S(1)} %bitcast.30, f32[512,128]{1,0:T(8,128)S(1)} %maximum_convert_fusion.projector_ref), custom_call_target="tpu_custom_call" | custom-call | tf_op jit(solution)/shard_map/density/pallas_call | solution.py:268
  (20 shorter events, 0.1 us)
Async XLA Ops:
  0.6 1.2 copy-start.3
  1.8 64.9 %copy-start.1 = (bf16[1,512,2,256]{3,1,2,0:T(8,128)(2,1)}, bf16[1,512,2,256]{3,1,2,0:T(8,128)(2,1)S(1)}, u32[]{:S(2)}) copy-start(bf16[1,512,2,256]{3,1,2,0:T(8,128)(2,1)S(1)} %copy.31) | copy-start | bytes 1572868
  1.8 37.7 %copy-start.5 = (s32[8192]{0:T(1024)S(1)}, s32[8192]{0:T(1024)}, u32[]{:S(2)}) copy-start(s32[8192]{0:T(1024)} %param.13) | copy-start | bytes 98308
  1.8 37.7 %copy-start.6 = (s32[8192]{0:T(1024)S(1)}, s32[8192]{0:T(1024)}, u32[]{:S(2)}) copy-start(s32[8192]{0:T(1024)} %param.14) | copy-start | bytes 98308
  1.9 12.8 %collective-permute-start = (bf16[2,256,256]{2,1,0:T(8,128)(2,1)S(1)}, bf16[2,256,256]{2,1,0:T(8,128)(2,1)S(1)}, u32[]{:S(2)}, u32[]{:S(2)}) collective-permute-start(bf16[2,256,256]{2,1,0:T(8,128)(2,1)S(1)} %get-tuple-element.13), channel_id=1, source_target_pairs={{0,0},{1,5},{2,10},{3,15},{4,1},{5,6},{6,11},{7,12},{8,2},{9,7},{1... | collective-permute-start | bytes 786440 | tf_op jit(solution)/shard_map/ppermute | solution.py:331
  2.7 17.8 %collective-permute-start.4 = (bf16[2,256,256]{2,1,0:T(8,128)(2,1)S(1)}, bf16[2,256,256]{2,1,0:T(8,128)(2,1)S(1)}, u32[]{:S(2)}, u32[]{:S(2)}) collective-permute-start(bf16[2,256,256]{2,1,0:T(8,128)(2,1)S(1)} %get-tuple-element.14.t0), channel_id=1, source_target_pairs={{0,4},{4,8},{8,12},{12,0},{1,5},{5,9},{9,13},{13,1},{2,6},{6,10},{... | collective-permute-start | bytes 786440 | tf_op jit(solution)/shard_map/ppermute | solution.py:330
  7.3 30.3 %collective-permute-start.5 = (bf16[2,256,256]{2,1,0:T(8,128)(2,1)S(1)}, bf16[2,256,256]{2,1,0:T(8,128)(2,1)S(1)}, u32[]{:S(2)}, u32[]{:S(2)}) collective-permute-start(bf16[2,256,256]{2,1,0:T(8,128)(2,1)S(1)} %get-tuple-element.14.t0), channel_id=1, source_target_pairs={{0,8},{4,12},{8,0},{12,4},{1,9},{5,13},{9,1},{13,5},{2,10},{6,14},... | collective-permute-start | bytes 786440 | tf_op jit(solution)/shard_map/ppermute | solution.py:330
  10.9 28.6 %collective-permute-start.6 = (bf16[2,256,256]{2,1,0:T(8,128)(2,1)S(1)}, bf16[2,256,256]{2,1,0:T(8,128)(2,1)S(1)}, u32[]{:S(2)}, u32[]{:S(2)}) collective-permute-start(bf16[2,256,256]{2,1,0:T(8,128)(2,1)S(1)} %get-tuple-element.14.t0), channel_id=1, source_target_pairs={{0,12},{4,0},{8,4},{12,8},{1,13},{5,1},{9,5},{13,9},{2,14},{6,2},{... | collective-permute-start | bytes 786440 | tf_op jit(solution)/shard_map/ppermute | solution.py:330
  12.4 27.9 %collective-permute-start.1 = (bf16[2,256,256]{2,1,0:T(8,128)(2,1)S(1)}, bf16[2,256,256]{2,1,0:T(8,128)(2,1)S(1)}, u32[]{:S(2)}, u32[]{:S(2)}) collective-permute-start(bf16[2,256,256]{2,1,0:T(8,128)(2,1)S(1)} %get-tuple-element.13), channel_id=1, source_target_pairs={{0,1},{1,6},{2,11},{3,12},{4,2},{5,7},{6,8},{7,13},{8,3},{9,4},{10... | collective-permute-start | bytes 786440 | tf_op jit(solution)/shard_map/ppermute | solution.py:331
  14.7 27.8 %collective-permute-start.2 = (bf16[2,256,256]{2,1,0:T(8,128)(2,1)S(1)}, bf16[2,256,256]{2,1,0:T(8,128)(2,1)S(1)}, u32[]{:S(2)}, u32[]{:S(2)}) collective-permute-start(bf16[2,256,256]{2,1,0:T(8,128)(2,1)S(1)} %get-tuple-element.13), channel_id=1, source_target_pairs={{0,2},{1,7},{2,8},{3,13},{4,3},{5,4},{6,9},{7,14},{8,0},{9,5},{10,... | collective-permute-start | bytes 786440 | tf_op jit(solution)/shard_map/ppermute | solution.py:331
  20.5 28.7 %collective-permute-start.3 = (bf16[2,256,256]{2,1,0:T(8,128)(2,1)S(1)}, bf16[2,256,256]{2,1,0:T(8,128)(2,1)S(1)}, u32[]{:S(2)}, u32[]{:S(2)}) collective-permute-start(bf16[2,256,256]{2,1,0:T(8,128)(2,1)S(1)} %get-tuple-element.13), channel_id=1, source_target_pairs={{0,3},{1,4},{2,9},{3,14},{4,0},{5,5},{6,10},{7,15},{8,1},{9,6},{10... | collective-permute-start | bytes 786440 | tf_op jit(solution)/shard_map/ppermute | solution.py:331
  37.6 15.8 %collective-permute-start.11 = (bf16[2,256,256]{2,1,0:T(8,128)(2,1)S(1)}, bf16[2,256,256]{2,1,0:T(8,128)(2,1)S(1)}, u32[]{:S(2)}, u32[]{:S(2)}) collective-permute-start(bf16[2,256,256]{2,1,0:T(8,128)(2,1)S(1)} %get-tuple-element.17), channel_id=1, source_target_pairs={{0,1},{1,6},{2,11},{3,12},{4,2},{5,7},{6,8},{7,13},{8,3},{9,4},{10... | collective-permute-start | bytes 786440 | tf_op jit(solution)/shard_map/ppermute | solution.py:333
  39.6 14.0 %collective-permute-start.10 = (bf16[2,256,256]{2,1,0:T(8,128)(2,1)S(1)}, bf16[2,256,256]{2,1,0:T(8,128)(2,1)S(1)}, u32[]{:S(2)}, u32[]{:S(2)}) collective-permute-start(bf16[2,256,256]{2,1,0:T(8,128)(2,1)S(1)} %get-tuple-element.17), channel_id=1, source_target_pairs={{0,0},{1,5},{2,10},{3,15},{4,1},{5,6},{6,11},{7,12},{8,2},{9,7},{1... | collective-permute-start | bytes 786440 | tf_op jit(solution)/shard_map/ppermute | solution.py:333
  40.3 13.4 %collective-permute-start.12 = (bf16[2,256,256]{2,1,0:T(8,128)(2,1)S(1)}, bf16[2,256,256]{2,1,0:T(8,128)(2,1)S(1)}, u32[]{:S(2)}, u32[]{:S(2)}) collective-permute-start(bf16[2,256,256]{2,1,0:T(8,128)(2,1)S(1)} %get-tuple-element.17), channel_id=1, source_target_pairs={{0,2},{1,7},{2,8},{3,13},{4,3},{5,4},{6,9},{7,14},{8,0},{9,5},{10,... | collective-permute-start | bytes 786440 | tf_op jit(solution)/shard_map/ppermute | solution.py:333
  42.5 19.4 %collective-permute-start.13 = (bf16[2,256,256]{2,1,0:T(8,128)(2,1)S(1)}, bf16[2,256,256]{2,1,0:T(8,128)(2,1)S(1)}, u32[]{:S(2)}, u32[]{:S(2)}) collective-permute-start(bf16[2,256,256]{2,1,0:T(8,128)(2,1)S(1)} %get-tuple-element.17), channel_id=1, source_target_pairs={{0,3},{1,4},{2,9},{3,14},{4,0},{5,5},{6,10},{7,15},{8,1},{9,6},{10... | collective-permute-start | bytes 786440 | tf_op jit(solution)/shard_map/ppermute | solution.py:333
  50.0 16.7 %collective-permute-start.7 = (bf16[2,256,256]{2,1,0:T(8,128)(2,1)S(1)}, bf16[2,256,256]{2,1,0:T(8,128)(2,1)S(1)}, u32[]{:S(2)}, u32[]{:S(2)}) collective-permute-start(bf16[2,256,256]{2,1,0:T(8,128)(2,1)S(1)} %coupling.2.refs_0_), channel_id=1, source_target_pairs={{0,1},{1,2},{2,3},{3,0},{4,5},{5,6},{6,7},{7,4},{8,9},{9,10},{10,1... | collective-permute-start | bytes 786440 | tf_op jit(solution)/shard_map/ppermute | solution.py:350
  53.3 13.4 %collective-permute-start.8 = (bf16[2,256,256]{2,1,0:T(8,128)(2,1)S(1)}, bf16[2,256,256]{2,1,0:T(8,128)(2,1)S(1)}, u32[]{:S(2)}, u32[]{:S(2)}) collective-permute-start(bf16[2,256,256]{2,1,0:T(8,128)(2,1)S(1)} %coupling.2.refs_0_), channel_id=1, source_target_pairs={{0,2},{1,3},{2,0},{3,1},{4,6},{5,7},{6,4},{7,5},{8,10},{9,11},{10,... | collective-permute-start | bytes 786440 | tf_op jit(solution)/shard_map/ppermute | solution.py:350
  53.6 34.1 %collective-permute-start.17 = (bf16[2,512,256]{2,1,0:T(8,128)(2,1)S(1)}, bf16[2,512,256]{2,1,0:T(8,128)(2,1)}, u32[]{:S(2)}, u32[]{:S(2)}) collective-permute-start(bf16[2,512,256]{2,1,0:T(8,128)(2,1)S(1)} %bitcast.32), channel_id=1, source_target_pairs={{0,4},{4,8},{8,12},{12,0},{1,5},{5,9},{9,13},{13,1},{2,6},{6,10},{... | collective-permute-start | bytes 1572872 | tf_op jit(solution)/shard_map/ppermute | solution.py:354
  53.7 34.0 %collective-permute-start.19 = (bf16[2,512,256]{2,1,0:T(8,128)(2,1)S(1)}, bf16[2,512,256]{2,1,0:T(8,128)(2,1)}, u32[]{:S(2)}, u32[]{:S(2)}) collective-permute-start(bf16[2,512,256]{2,1,0:T(8,128)(2,1)S(1)} %bitcast.33), channel_id=1, source_target_pairs={{0,12},{4,0},{8,4},{12,8},{1,13},{5,1},{9,5},{13,9},{2,14},{6,2},{... | collective-permute-start | bytes 1572872 | tf_op jit(solution)/shard_map/ppermute | solution.py:354
  61.9 10.6 %collective-permute-start.9 = (bf16[2,256,256]{2,1,0:T(8,128)(2,1)S(1)}, bf16[2,256,256]{2,1,0:T(8,128)(2,1)S(1)}, u32[]{:S(2)}, u32[]{:S(2)}) collective-permute-start(bf16[2,256,256]{2,1,0:T(8,128)(2,1)S(1)} %coupling.2.refs_0_), channel_id=1, source_target_pairs={{0,3},{1,0},{2,1},{3,2},{4,7},{5,4},{6,5},{7,6},{8,11},{9,8},{10,9... | collective-permute-start | bytes 786440 | tf_op jit(solution)/shard_map/ppermute | solution.py:350
  66.6 8.4 %collective-permute-start.14 = (bf16[2,256,256]{2,1,0:T(8,128)(2,1)S(1)}, bf16[2,256,256]{2,1,0:T(8,128)(2,1)S(1)}, u32[]{:S(2)}, u32[]{:S(2)}) collective-permute-start(bf16[2,256,256]{2,1,0:T(8,128)(2,1)S(1)} %coupling.3.refs_4_), channel_id=1, source_target_pairs={{0,1},{1,2},{2,3},{3,0},{4,5},{5,6},{6,7},{7,4},{8,9},{9,10},{10,1... | collective-permute-start | bytes 786440 | tf_op jit(solution)/shard_map/ppermute | solution.py:350
  66.8 20.9 %collective-permute-start.18 = (bf16[2,512,256]{2,1,0:T(8,128)(2,1)S(1)}, bf16[2,512,256]{2,1,0:T(8,128)(2,1)S(1)}, u32[]{:S(2)}, u32[]{:S(2)}) collective-permute-start(bf16[2,512,256]{2,1,0:T(8,128)(2,1)S(1)} %bitcast.34), channel_id=1, source_target_pairs={{0,8},{4,12},{8,0},{12,4},{1,9},{5,13},{9,1},{13,5},{2,10},{6,14},... | collective-permute-start | bytes 1572872 | tf_op jit(solution)/shard_map/ppermute | solution.py:354
  72.5 7.0 %collective-permute-start.15 = (bf16[2,256,256]{2,1,0:T(8,128)(2,1)S(1)}, bf16[2,256,256]{2,1,0:T(8,128)(2,1)S(1)}, u32[]{:S(2)}, u32[]{:S(2)}) collective-permute-start(bf16[2,256,256]{2,1,0:T(8,128)(2,1)S(1)} %coupling.3.refs_4_), channel_id=1, source_target_pairs={{0,2},{1,3},{2,0},{3,1},{4,6},{5,7},{6,4},{7,5},{8,10},{9,11},{10,... | collective-permute-start | bytes 786440 | tf_op jit(solution)/shard_map/ppermute | solution.py:350
  75.0 12.7 %collective-permute-start.16 = (bf16[2,256,256]{2,1,0:T(8,128)(2,1)S(1)}, bf16[2,256,256]{2,1,0:T(8,128)(2,1)S(1)}, u32[]{:S(2)}, u32[]{:S(2)}) collective-permute-start(bf16[2,256,256]{2,1,0:T(8,128)(2,1)S(1)} %coupling.3.refs_4_), channel_id=1, source_target_pairs={{0,3},{1,0},{2,1},{3,2},{4,7},{5,4},{6,5},{7,6},{8,11},{9,8},{10,9... | collective-permute-start | bytes 786440 | tf_op jit(solution)/shard_map/ppermute | solution.py:350
  87.7 0.7 copy-start.8
  87.7 0.9 copy-start.7
  88.6 23.1 %copy-start.4 = (bf16[512,64]{0,1:T(8,128)(2,1)S(1)}, bf16[512,64]{0,1:T(8,128)(2,1)}, u32[]{:S(2)}) copy-start(bf16[512,64]{0,1:T(8,128)(2,1)} %param.15) | copy-start | bytes 196612
  88.6 35.4 %copy-start = (f32[256,2]{0,1:T(2,128)S(1)}, f32[256,2]{0,1:T(2,128)}, u32[]{:S(2)}) copy-start(f32[256,2]{0,1:T(2,128)} %param.11) | copy-start | bytes 6148
  101.3 29.9 %copy-start.2 = (bf16[2,512,512]{2,1,0:T(8,128)(2,1)S(1)}, bf16[2,512,512]{2,1,0:T(8,128)(2,1)}, u32[]{:S(2)}) copy-start(bf16[2,512,512]{2,1,0:T(8,128)(2,1)} %get-tuple-element.20) | copy-start | bytes 3145732
  101.3 22.7 %all-to-all-start = ((bf16[16,72,128]{2,1,0:T(8,128)(2,1)}), bf16[16,72,128]{2,1,0:T(8,128)(2,1)S(1)}, u32[]{:S(2)}, u32[]{:S(2)}) async-start(bf16[16,72,128]{2,1,0:T(8,128)(2,1)} %get-tuple-element.21), calls=%async_computation | async-start | bytes 589824 | tf_op jit(solution)/shard_map/all_to_all | solution.py:363
  124.9 14.8 %all-to-all-start.1 = ((bf16[16,64,128]{2,1,0:T(8,128)(2,1)}), bf16[16,64,128]{2,1,0:T(8,128)(2,1)S(1)}, u32[]{:S(2)}, u32[]{:S(2)}) async-start(bf16[16,64,128]{2,1,0:T(8,128)(2,1)} %pole_sum.1), calls=%async_computation.1 | async-start | bytes 524288 | tf_op jit(solution)/shard_map/all_to_all | solution.py:366

commit v9 on v8

--- a/solution.py
+++ b/solution.py
@@ -351,7 +351,7 @@
         ]
     lower_early, _ = lax.optimization_barrier((lower, second[1]))
     lowers = [lower] + [
-        lax.ppermute(lower_early if e == 2 else lower_late, "row", ring(e, ROWS))
+        lax.ppermute(lower_early if e == 1 else lower_late, "row", ring(e, ROWS))
         for e in range(1, ROWS)
     ]
 

time: 142 us -> 142 us (level)
  starting transfers between devices: 80.5 us -> 76.9 us
  waiting for transfers between devices: 34.6 us -> 38.1 us
    ppermute x6, waiting for transfers between devices: 12.3 us -> 15.8 us  [local(): lax.ppermute(coupling, 'col', ring(d, COLS))]
    ppermute x3, starting transfers between devices: 8.61 us -> 5.86 us  [local(): lax.ppermute(lower_early if e == 1 else lower_late, 'row', ring(e, ROWS))]
where the time goes in v9:
time: 142 us; the launch traced here: 141 us
  starting transfers between devices  76.9 us (54%)
  waiting for transfers between devices  38.1 us (27%)
  Pallas kernels  16.9 us (12%)
  local copies, waits for them, and re-layouts  6.72 us (5%)
  between operations  1.67 us (1%)
    ppermute x4, starting transfers between devices, local(): lax.ppermute(halves[0], pair_axes, to_process_rows(e))  25.9 us
    ppermute x6, waiting for transfers between devices, local(): lax.ppermute(coupling, 'col', ring(d, COLS))  15.8 us
    pallas_call x1, Pallas kernels, block_call(): pl.pallas_call(block_kernel, out_shape=(jax.ShapeDtypeStruct((2, rows, co...  12.7 us
    all_to_all x1, waiting for transfers between devices, local(): parts = lax.all_to_all(pairs, POLE, 0, 0, tiled=True)  12 us
    ppermute x4, starting transfers between devices, local(): lax.ppermute(second_half, pair_axes, to_process_rows(e))  11.5 us
    all_to_all x1, starting transfers between devices, local(): parts = lax.all_to_all(pairs, POLE, 0, 0, tiled=True)  10.4 us
    ppermute x3, starting transfers between devices, local(): lax.ppermute(trail, 'row', ring(e, ROWS))  9.64 us
    ppermute x6, starting transfers between devices, local(): lax.ppermute(coupling, 'col', ring(d, COLS))  7.59 us
  transfers between devices with their start and end apart: 22, of which 8 were waited for; matrix products, arithmetic and copies ran while one was open for 4% of the time, Pallas kernels for 1%

profile of v9, /device:TPU:1, one launch (start us, length us, event | category | flops | bytes accessed | tf_op | source)
XLA Modules:
  0.0 141.4 jit_solution(12407835240438101002)
XLA Ops:
  0.6 1.2 copy.31
  1.8 0.0 copy-start.5
  1.8 0.0 copy-start.6
  1.8 0.1 slice_bitcast_fusion
  1.9 0.8 collective-permute-start
  2.7 4.5 %collective-permute-start.4 = (bf16[2,256,256]{2,1,0:T(8,128)(2,1)S(1)}, bf16[2,256,256]{2,1,0:T(8,128)(2,1)S(1)}, u32[]{:S(2)}, u32[]{:S(2)}) collective-permute-start(bf16[2,256,256]{2,1,0:T(8,128)(2,1)S(1)} %get-tuple-element.14.t0), channel_id=1, source_target_pairs={{0,4},{4,8},{8,12},{12,0},{1,5},{5,9},{9,13},{13,1},{2,6},{6,10},{... | collective-permute-start | bytes 786440 | tf_op jit(solution)/shard_map/ppermute | solution.py:330
  7.3 3.7 %collective-permute-start.5 = (bf16[2,256,256]{2,1,0:T(8,128)(2,1)S(1)}, bf16[2,256,256]{2,1,0:T(8,128)(2,1)S(1)}, u32[]{:S(2)}, u32[]{:S(2)}) collective-permute-start(bf16[2,256,256]{2,1,0:T(8,128)(2,1)S(1)} %get-tuple-element.14.t0), channel_id=1, source_target_pairs={{0,8},{4,12},{8,0},{12,4},{1,9},{5,13},{9,1},{13,5},{2,10},{6,14},... | collective-permute-start | bytes 786440 | tf_op jit(solution)/shard_map/ppermute | solution.py:330
  10.9 1.4 %collective-permute-start.6 = (bf16[2,256,256]{2,1,0:T(8,128)(2,1)S(1)}, bf16[2,256,256]{2,1,0:T(8,128)(2,1)S(1)}, u32[]{:S(2)}, u32[]{:S(2)}) collective-permute-start(bf16[2,256,256]{2,1,0:T(8,128)(2,1)S(1)} %get-tuple-element.14.t0), channel_id=1, source_target_pairs={{0,12},{4,0},{8,4},{12,8},{1,13},{5,1},{9,5},{13,9},{2,14},{6,2},{... | collective-permute-start | bytes 786440 | tf_op jit(solution)/shard_map/ppermute | solution.py:330
  12.4 2.3 %collective-permute-start.1 = (bf16[2,256,256]{2,1,0:T(8,128)(2,1)S(1)}, bf16[2,256,256]{2,1,0:T(8,128)(2,1)S(1)}, u32[]{:S(2)}, u32[]{:S(2)}) collective-permute-start(bf16[2,256,256]{2,1,0:T(8,128)(2,1)S(1)} %get-tuple-element.13), channel_id=1, source_target_pairs={{0,1},{1,6},{2,11},{3,12},{4,2},{5,7},{6,8},{7,13},{8,3},{9,4},{10... | collective-permute-start | bytes 786440 | tf_op jit(solution)/shard_map/ppermute | solution.py:331
  14.7 0.0 collective-permute-done.l0
  14.7 5.8 %collective-permute-start.2 = (bf16[2,256,256]{2,1,0:T(8,128)(2,1)S(1)}, bf16[2,256,256]{2,1,0:T(8,128)(2,1)S(1)}, u32[]{:S(2)}, u32[]{:S(2)}) collective-permute-start(bf16[2,256,256]{2,1,0:T(8,128)(2,1)S(1)} %get-tuple-element.13), channel_id=1, source_target_pairs={{0,2},{1,7},{2,8},{3,13},{4,3},{5,4},{6,9},{7,14},{8,0},{9,5},{10,... | collective-permute-start | bytes 786440 | tf_op jit(solution)/shard_map/ppermute | solution.py:331
  20.5 0.0 collective-permute-done.4.t1
  20.5 17.0 %collective-permute-start.3 = (bf16[2,256,256]{2,1,0:T(8,128)(2,1)S(1)}, bf16[2,256,256]{2,1,0:T(8,128)(2,1)S(1)}, u32[]{:S(2)}, u32[]{:S(2)}) collective-permute-start(bf16[2,256,256]{2,1,0:T(8,128)(2,1)S(1)} %get-tuple-element.13), channel_id=1, source_target_pairs={{0,3},{1,4},{2,9},{3,14},{4,0},{5,5},{6,10},{7,15},{8,1},{9,6},{10... | collective-permute-start | bytes 786440 | tf_op jit(solution)/shard_map/ppermute | solution.py:331
  37.5 0.0 collective-permute-done.5.t2
  37.6 1.9 %collective-permute-start.11 = (bf16[2,256,256]{2,1,0:T(8,128)(2,1)S(1)}, bf16[2,256,256]{2,1,0:T(8,128)(2,1)S(1)}, u32[]{:S(2)}, u32[]{:S(2)}) collective-permute-start(bf16[2,256,256]{2,1,0:T(8,128)(2,1)S(1)} %get-tuple-element.17), channel_id=1, source_target_pairs={{0,1},{1,6},{2,11},{3,12},{4,2},{5,7},{6,8},{7,13},{8,3},{9,4},{10... | collective-permute-start | bytes 786440 | tf_op jit(solution)/shard_map/ppermute | solution.py:333
  39.6 0.0 collective-permute-done.6.t3
  39.6 0.7 collective-permute-start.10
  40.3 0.0 collective-permute-done.1.l1
  40.3 2.3 %collective-permute-start.12 = (bf16[2,256,256]{2,1,0:T(8,128)(2,1)S(1)}, bf16[2,256,256]{2,1,0:T(8,128)(2,1)S(1)}, u32[]{:S(2)}, u32[]{:S(2)}) collective-permute-start(bf16[2,256,256]{2,1,0:T(8,128)(2,1)S(1)} %get-tuple-element.17), channel_id=1, source_target_pairs={{0,2},{1,7},{2,8},{3,13},{4,3},{5,4},{6,9},{7,14},{8,0},{9,5},{10,... | collective-permute-start | bytes 786440 | tf_op jit(solution)/shard_map/ppermute | solution.py:333
  42.5 0.0 collective-permute-done.2.l2
  42.5 6.7 %collective-permute-start.13 = (bf16[2,256,256]{2,1,0:T(8,128)(2,1)S(1)}, bf16[2,256,256]{2,1,0:T(8,128)(2,1)S(1)}, u32[]{:S(2)}, u32[]{:S(2)}) collective-permute-start(bf16[2,256,256]{2,1,0:T(8,128)(2,1)S(1)} %get-tuple-element.17), channel_id=1, source_target_pairs={{0,3},{1,4},{2,9},{3,14},{4,0},{5,5},{6,10},{7,15},{8,1},{9,6},{10... | collective-permute-start | bytes 786440 | tf_op jit(solution)/shard_map/ppermute | solution.py:333
  49.2 0.0 collective-permute-done.3.l3
  49.2 0.7 coupling.2.refs_0_
  50.0 2.1 %collective-permute-start.7 = (bf16[2,256,256]{2,1,0:T(8,128)(2,1)S(1)}, bf16[2,256,256]{2,1,0:T(8,128)(2,1)S(1)}, u32[]{:S(2)}, u32[]{:S(2)}) collective-permute-start(bf16[2,256,256]{2,1,0:T(8,128)(2,1)S(1)} %coupling.2.refs_0_), channel_id=1, source_target_pairs={{0,1},{1,2},{2,3},{3,0},{4,5},{5,6},{6,7},{7,4},{8,9},{9,10},{10,1... | collective-permute-start | bytes 786440 | tf_op jit(solution)/shard_map/ppermute | solution.py:350
  52.1 1.2 collective-permute-done.11.l1
  53.3 0.0 collective-permute-start.8
  53.3 0.2 convert_reduce_fusion.1
  53.5 0.0 collective-permute-done.10.l0
  53.6 1.7 %collective-permute-start.18 = (bf16[2,512,256]{2,1,0:T(8,128)(2,1)S(1)}, bf16[2,512,256]{2,1,0:T(8,128)(2,1)}, u32[]{:S(2)}, u32[]{:S(2)}) collective-permute-start(bf16[2,512,256]{2,1,0:T(8,128)(2,1)S(1)} %bitcast.32), channel_id=1, source_target_pairs={{0,8},{4,12},{8,0},{12,4},{1,9},{5,13},{9,1},{13,5},{2,10},{6,14},... | collective-permute-start | bytes 1572872 | tf_op jit(solution)/shard_map/ppermute | solution.py:354
  55.2 0.0 collective-permute-done.12.l2
  55.2 4.1 %collective-permute-start.19 = (bf16[2,512,256]{2,1,0:T(8,128)(2,1)S(1)}, bf16[2,512,256]{2,1,0:T(8,128)(2,1)}, u32[]{:S(2)}, u32[]{:S(2)}) collective-permute-start(bf16[2,512,256]{2,1,0:T(8,128)(2,1)S(1)} %bitcast.33), channel_id=1, source_target_pairs={{0,12},{4,0},{8,4},{12,8},{1,13},{5,1},{9,5},{13,9},{2,14},{6,2},{... | collective-permute-start | bytes 1572872 | tf_op jit(solution)/shard_map/ppermute | solution.py:354
  59.3 2.6 %collective-permute-done.13.l3 = bf16[2,256,256]{2,1,0:T(8,128)(2,1)S(1)} collective-permute-done((bf16[2,256,256]{2,1,0:T(8,128)(2,1)S(1)}, bf16[2,256,256]{2,1,0:T(8,128)(2,1)S(1)}, u32[]{:S(2)}, u32[]{:S(2)}) %collective-permute-start.13) | collective-permute-done | bytes 262176 | tf_op jit(solution)/shard_map/ppermute | solution.py:333
  61.9 4.0 %collective-permute-start.9 = (bf16[2,256,256]{2,1,0:T(8,128)(2,1)S(1)}, bf16[2,256,256]{2,1,0:T(8,128)(2,1)S(1)}, u32[]{:S(2)}, u32[]{:S(2)}) collective-permute-start(bf16[2,256,256]{2,1,0:T(8,128)(2,1)S(1)} %coupling.2.refs_0_), channel_id=1, source_target_pairs={{0,3},{1,0},{2,1},{3,2},{4,7},{5,4},{6,5},{7,6},{8,11},{9,8},{10,9... | collective-permute-start | bytes 786440 | tf_op jit(solution)/shard_map/ppermute | solution.py:350
  65.9 0.7 coupling.3.refs_4_
  66.6 0.0 collective-permute-done.7.refs_1_
  66.6 0.1 collective-permute-start.14
  66.7 0.0 collective-permute-done.8.refs_2_
  66.8 0.1 collective-permute-start.17
  66.9 0.2 fusion
  67.0 0.4 select_reduce_fusion
  67.4 5.1 %collective-permute-done.9.refs_3_ = bf16[2,256,256]{2,1,0:T(8,128)(2,1)S(1)} collective-permute-done((bf16[2,256,256]{2,1,0:T(8,128)(2,1)S(1)}, bf16[2,256,256]{2,1,0:T(8,128)(2,1)S(1)}, u32[]{:S(2)}, u32[]{:S(2)}) %collective-permute-start.9) | collective-permute-done | bytes 262176 | tf_op jit(solution)/shard_map/ppermute | solution.py:350
  72.5 0.5 collective-permute-start.15
  73.0 2.1 %collective-permute-done.14.refs_5_ = bf16[2,256,256]{2,1,0:T(8,128)(2,1)S(1)} collective-permute-done((bf16[2,256,256]{2,1,0:T(8,128)(2,1)S(1)}, bf16[2,256,256]{2,1,0:T(8,128)(2,1)S(1)}, u32[]{:S(2)}, u32[]{:S(2)}) %collective-permute-start.14) | collective-permute-done | bytes 262176 | tf_op jit(solution)/shard_map/ppermute | solution.py:350
  75.0 0.9 collective-permute-start.16
  75.9 0.1 reshape.121.codes_ref
  76.0 2.4 %copy.30 = bf16[1,512,2,512]{3,1,2,0:T(8,128)(2,1)} copy(bf16[1,512,2,512]{3,2,1,0:T(2,128)(2,1)} %param.10) | data formatting | bytes 2097152 | tf_op args[2]
  79.0 1.8 %collective-permute-done.15.refs_6_ = bf16[2,256,256]{2,1,0:T(8,128)(2,1)S(1)} collective-permute-done((bf16[2,256,256]{2,1,0:T(8,128)(2,1)S(1)}, bf16[2,256,256]{2,1,0:T(8,128)(2,1)S(1)}, u32[]{:S(2)}, u32[]{:S(2)}) %collective-permute-start.15) | collective-permute-done | bytes 262176 | tf_op jit(solution)/shard_map/ppermute | solution.py:350
  80.8 6.9 %collective-permute-done.16.refs_7_ = bf16[2,256,256]{2,1,0:T(8,128)(2,1)S(1)} collective-permute-done((bf16[2,256,256]{2,1,0:T(8,128)(2,1)S(1)}, bf16[2,256,256]{2,1,0:T(8,128)(2,1)S(1)}, u32[]{:S(2)}, u32[]{:S(2)}) %collective-permute-start.16) | collective-permute-done | bytes 262176 | tf_op jit(solution)/shard_map/ppermute | solution.py:350
  87.7 0.0 collective-permute-done.18.refs_10_
  87.7 0.0 collective-permute-done.19.refs_11_
  87.7 0.0 collective-permute-done.17.refs_9_
  87.7 0.7 copy-done.8
  88.4 0.2 copy-done.7
  88.6 12.7 %block_and_pairs.1 = (bf16[2,512,512]{2,1,0:T(8,128)(2,1)}, bf16[16,72,128]{2,1,0:T(8,128)(2,1)}) custom-call(s32[1]{0:T(128)} %bitcast.base_ref, s32[1]{0:T(128)S(6)} %copy.32.slot_ref, s32[1024]{0:T(1024)S(1)} %reshape.121.codes_ref, s32[16]{0:T(128)S(1)} %get-tuple-element.26.counts_ref, bf16[2,256,256]{2,1,0:T(8,128)(2,1)S(1)} %coupling.2.refs_0_, ...), custom_call_target="tpu_custom_call" | custom-call | flops 2147483648 | bytes 12582912 | tf_op jit(solution)/shard_map/block_and_pairs/pallas_call | solution.py:190
  101.3 10.4 %all-to-all-start = ((bf16[16,72,128]{2,1,0:T(8,128)(2,1)}), bf16[16,72,128]{2,1,0:T(8,128)(2,1)S(1)}, u32[]{:S(2)}, u32[]{:S(2)}) async-start(bf16[16,72,128]{2,1,0:T(8,128)(2,1)} %get-tuple-element.21), calls=%async_computation | async-start | bytes 589824 | tf_op jit(solution)/shard_map/all_to_all | solution.py:363
  111.6 0.1 copy.23
  111.8 0.2 convert_reduce_fusion
  112.0 12.0 %all-to-all-done.parts_ref = bf16[16,72,128]{2,1,0:T(8,128)(2,1)S(1)} async-done(((bf16[16,72,128]{2,1,0:T(8,128)(2,1)}), bf16[16,72,128]{2,1,0:T(8,128)(2,1)S(1)}, u32[]{:S(2)}, u32[]{:S(2)}) %all-to-all-start) | async-done | bytes 294944 | tf_op jit(solution)/shard_map/all_to_all | solution.py:363
  124.0 0.9 pole_sum.1
  124.9 6.0 %all-to-all-start.1 = ((bf16[16,64,128]{2,1,0:T(8,128)(2,1)}), bf16[16,64,128]{2,1,0:T(8,128)(2,1)S(1)}, u32[]{:S(2)}, u32[]{:S(2)}) async-start(bf16[16,64,128]{2,1,0:T(8,128)(2,1)} %pole_sum.1), calls=%async_computation.1 | async-start | bytes 524288 | tf_op jit(solution)/shard_map/all_to_all | solution.py:366
  130.9 0.1 maximum_convert_fusion.projector_ref
  131.1 2.0 %copy.25 = bf16[1,512,2,512]{3,2,1,0:T(2,128)(2,1)} copy(bf16[1,512,2,512]{3,1,2,0:T(8,128)(2,1)S(1)} %bitcast.36) | data formatting | bytes 2097152
  133.1 6.5 %all-to-all-done.1 = bf16[16,64,128]{2,1,0:T(8,128)(2,1)S(1)} async-done(((bf16[16,64,128]{2,1,0:T(8,128)(2,1)}), bf16[16,64,128]{2,1,0:T(8,128)(2,1)S(1)}, u32[]{:S(2)}, u32[]{:S(2)}) %all-to-all-start.1) | async-done | bytes 262176 | tf_op jit(solution)/shard_map/all_to_all | solution.py:366
  139.6 1.8 %density.1 = f32[512,128]{1,0:T(8,128)} custom-call(s32[512]{0:T(512)S(1)} %multiply_add_fusion.index_ref, bf16[1024,128]{1,0:T(8,128)(2,1)S(1)} %bitcast.30, f32[512,128]{1,0:T(8,128)S(1)} %maximum_convert_fusion.projector_ref), custom_call_target="tpu_custom_call" | custom-call | tf_op jit(solution)/shard_map/density/pallas_call | solution.py:268
  (20 shorter events, 0.1 us)
Async XLA Ops:
  0.6 1.2 copy-start.3
  1.8 64.9 %copy-start.1 = (bf16[1,512,2,256]{3,1,2,0:T(8,128)(2,1)}, bf16[1,512,2,256]{3,1,2,0:T(8,128)(2,1)S(1)}, u32[]{:S(2)}) copy-start(bf16[1,512,2,256]{3,1,2,0:T(8,128)(2,1)S(1)} %copy.31) | copy-start | bytes 1572868
  1.8 37.7 %copy-start.5 = (s32[8192]{0:T(1024)S(1)}, s32[8192]{0:T(1024)}, u32[]{:S(2)}) copy-start(s32[8192]{0:T(1024)} %param.13) | copy-start | bytes 98308
  1.8 37.7 %copy-start.6 = (s32[8192]{0:T(1024)S(1)}, s32[8192]{0:T(1024)}, u32[]{:S(2)}) copy-start(s32[8192]{0:T(1024)} %param.14) | copy-start | bytes 98308
  1.9 12.8 %collective-permute-start = (bf16[2,256,256]{2,1,0:T(8,128)(2,1)S(1)}, bf16[2,256,256]{2,1,0:T(8,128)(2,1)S(1)}, u32[]{:S(2)}, u32[]{:S(2)}) collective-permute-start(bf16[2,256,256]{2,1,0:T(8,128)(2,1)S(1)} %get-tuple-element.13), channel_id=1, source_target_pairs={{0,0},{1,5},{2,10},{3,15},{4,1},{5,6},{6,11},{7,12},{8,2},{9,7},{1... | collective-permute-start | bytes 786440 | tf_op jit(solution)/shard_map/ppermute | solution.py:331
  2.7 17.8 %collective-permute-start.4 = (bf16[2,256,256]{2,1,0:T(8,128)(2,1)S(1)}, bf16[2,256,256]{2,1,0:T(8,128)(2,1)S(1)}, u32[]{:S(2)}, u32[]{:S(2)}) collective-permute-start(bf16[2,256,256]{2,1,0:T(8,128)(2,1)S(1)} %get-tuple-element.14.t0), channel_id=1, source_target_pairs={{0,4},{4,8},{8,12},{12,0},{1,5},{5,9},{9,13},{13,1},{2,6},{6,10},{... | collective-permute-start | bytes 786440 | tf_op jit(solution)/shard_map/ppermute | solution.py:330
  7.3 30.3 %collective-permute-start.5 = (bf16[2,256,256]{2,1,0:T(8,128)(2,1)S(1)}, bf16[2,256,256]{2,1,0:T(8,128)(2,1)S(1)}, u32[]{:S(2)}, u32[]{:S(2)}) collective-permute-start(bf16[2,256,256]{2,1,0:T(8,128)(2,1)S(1)} %get-tuple-element.14.t0), channel_id=1, source_target_pairs={{0,8},{4,12},{8,0},{12,4},{1,9},{5,13},{9,1},{13,5},{2,10},{6,14},... | collective-permute-start | bytes 786440 | tf_op jit(solution)/shard_map/ppermute | solution.py:330
  10.9 28.6 %collective-permute-start.6 = (bf16[2,256,256]{2,1,0:T(8,128)(2,1)S(1)}, bf16[2,256,256]{2,1,0:T(8,128)(2,1)S(1)}, u32[]{:S(2)}, u32[]{:S(2)}) collective-permute-start(bf16[2,256,256]{2,1,0:T(8,128)(2,1)S(1)} %get-tuple-element.14.t0), channel_id=1, source_target_pairs={{0,12},{4,0},{8,4},{12,8},{1,13},{5,1},{9,5},{13,9},{2,14},{6,2},{... | collective-permute-start | bytes 786440 | tf_op jit(solution)/shard_map/ppermute | solution.py:330
  12.4 27.9 %collective-permute-start.1 = (bf16[2,256,256]{2,1,0:T(8,128)(2,1)S(1)}, bf16[2,256,256]{2,1,0:T(8,128)(2,1)S(1)}, u32[]{:S(2)}, u32[]{:S(2)}) collective-permute-start(bf16[2,256,256]{2,1,0:T(8,128)(2,1)S(1)} %get-tuple-element.13), channel_id=1, source_target_pairs={{0,1},{1,6},{2,11},{3,12},{4,2},{5,7},{6,8},{7,13},{8,3},{9,4},{10... | collective-permute-start | bytes 786440 | tf_op jit(solution)/shard_map/ppermute | solution.py:331
  14.7 27.8 %collective-permute-start.2 = (bf16[2,256,256]{2,1,0:T(8,128)(2,1)S(1)}, bf16[2,256,256]{2,1,0:T(8,128)(2,1)S(1)}, u32[]{:S(2)}, u32[]{:S(2)}) collective-permute-start(bf16[2,256,256]{2,1,0:T(8,128)(2,1)S(1)} %get-tuple-element.13), channel_id=1, source_target_pairs={{0,2},{1,7},{2,8},{3,13},{4,3},{5,4},{6,9},{7,14},{8,0},{9,5},{10,... | collective-permute-start | bytes 786440 | tf_op jit(solution)/shard_map/ppermute | solution.py:331
  20.5 28.7 %collective-permute-start.3 = (bf16[2,256,256]{2,1,0:T(8,128)(2,1)S(1)}, bf16[2,256,256]{2,1,0:T(8,128)(2,1)S(1)}, u32[]{:S(2)}, u32[]{:S(2)}) collective-permute-start(bf16[2,256,256]{2,1,0:T(8,128)(2,1)S(1)} %get-tuple-element.13), channel_id=1, source_target_pairs={{0,3},{1,4},{2,9},{3,14},{4,0},{5,5},{6,10},{7,15},{8,1},{9,6},{10... | collective-permute-start | bytes 786440 | tf_op jit(solution)/shard_map/ppermute | solution.py:331
  37.6 15.8 %collective-permute-start.11 = (bf16[2,256,256]{2,1,0:T(8,128)(2,1)S(1)}, bf16[2,256,256]{2,1,0:T(8,128)(2,1)S(1)}, u32[]{:S(2)}, u32[]{:S(2)}) collective-permute-start(bf16[2,256,256]{2,1,0:T(8,128)(2,1)S(1)} %get-tuple-element.17), channel_id=1, source_target_pairs={{0,1},{1,6},{2,11},{3,12},{4,2},{5,7},{6,8},{7,13},{8,3},{9,4},{10... | collective-permute-start | bytes 786440 | tf_op jit(solution)/shard_map/ppermute | solution.py:333
  39.6 14.0 %collective-permute-start.10 = (bf16[2,256,256]{2,1,0:T(8,128)(2,1)S(1)}, bf16[2,256,256]{2,1,0:T(8,128)(2,1)S(1)}, u32[]{:S(2)}, u32[]{:S(2)}) collective-permute-start(bf16[2,256,256]{2,1,0:T(8,128)(2,1)S(1)} %get-tuple-element.17), channel_id=1, source_target_pairs={{0,0},{1,5},{2,10},{3,15},{4,1},{5,6},{6,11},{7,12},{8,2},{9,7},{1... | collective-permute-start | bytes 786440 | tf_op jit(solution)/shard_map/ppermute | solution.py:333
  40.3 15.0 %collective-permute-start.12 = (bf16[2,256,256]{2,1,0:T(8,128)(2,1)S(1)}, bf16[2,256,256]{2,1,0:T(8,128)(2,1)S(1)}, u32[]{:S(2)}, u32[]{:S(2)}) collective-permute-start(bf16[2,256,256]{2,1,0:T(8,128)(2,1)S(1)} %get-tuple-element.17), channel_id=1, source_target_pairs={{0,2},{1,7},{2,8},{3,13},{4,3},{5,4},{6,9},{7,14},{8,0},{9,5},{10,... | collective-permute-start | bytes 786440 | tf_op jit(solution)/shard_map/ppermute | solution.py:333
  42.5 19.4 %collective-permute-start.13 = (bf16[2,256,256]{2,1,0:T(8,128)(2,1)S(1)}, bf16[2,256,256]{2,1,0:T(8,128)(2,1)S(1)}, u32[]{:S(2)}, u32[]{:S(2)}) collective-permute-start(bf16[2,256,256]{2,1,0:T(8,128)(2,1)S(1)} %get-tuple-element.17), channel_id=1, source_target_pairs={{0,3},{1,4},{2,9},{3,14},{4,0},{5,5},{6,10},{7,15},{8,1},{9,6},{10... | collective-permute-start | bytes 786440 | tf_op jit(solution)/shard_map/ppermute | solution.py:333
  50.0 16.7 %collective-permute-start.7 = (bf16[2,256,256]{2,1,0:T(8,128)(2,1)S(1)}, bf16[2,256,256]{2,1,0:T(8,128)(2,1)S(1)}, u32[]{:S(2)}, u32[]{:S(2)}) collective-permute-start(bf16[2,256,256]{2,1,0:T(8,128)(2,1)S(1)} %coupling.2.refs_0_), channel_id=1, source_target_pairs={{0,1},{1,2},{2,3},{3,0},{4,5},{5,6},{6,7},{7,4},{8,9},{9,10},{10,1... | collective-permute-start | bytes 786440 | tf_op jit(solution)/shard_map/ppermute | solution.py:350
  53.3 13.4 %collective-permute-start.8 = (bf16[2,256,256]{2,1,0:T(8,128)(2,1)S(1)}, bf16[2,256,256]{2,1,0:T(8,128)(2,1)S(1)}, u32[]{:S(2)}, u32[]{:S(2)}) collective-permute-start(bf16[2,256,256]{2,1,0:T(8,128)(2,1)S(1)} %coupling.2.refs_0_), channel_id=1, source_target_pairs={{0,2},{1,3},{2,0},{3,1},{4,6},{5,7},{6,4},{7,5},{8,10},{9,11},{10,... | collective-permute-start | bytes 786440 | tf_op jit(solution)/shard_map/ppermute | solution.py:350
  53.6 34.1 %collective-permute-start.18 = (bf16[2,512,256]{2,1,0:T(8,128)(2,1)S(1)}, bf16[2,512,256]{2,1,0:T(8,128)(2,1)}, u32[]{:S(2)}, u32[]{:S(2)}) collective-permute-start(bf16[2,512,256]{2,1,0:T(8,128)(2,1)S(1)} %bitcast.32), channel_id=1, source_target_pairs={{0,8},{4,12},{8,0},{12,4},{1,9},{5,13},{9,1},{13,5},{2,10},{6,14},... | collective-permute-start | bytes 1572872 | tf_op jit(solution)/shard_map/ppermute | solution.py:354
  55.2 32.4 %collective-permute-start.19 = (bf16[2,512,256]{2,1,0:T(8,128)(2,1)S(1)}, bf16[2,512,256]{2,1,0:T(8,128)(2,1)}, u32[]{:S(2)}, u32[]{:S(2)}) collective-permute-start(bf16[2,512,256]{2,1,0:T(8,128)(2,1)S(1)} %bitcast.33), channel_id=1, source_target_pairs={{0,12},{4,0},{8,4},{12,8},{1,13},{5,1},{9,5},{13,9},{2,14},{6,2},{... | collective-permute-start | bytes 1572872 | tf_op jit(solution)/shard_map/ppermute | solution.py:354
  61.9 10.6 %collective-permute-start.9 = (bf16[2,256,256]{2,1,0:T(8,128)(2,1)S(1)}, bf16[2,256,256]{2,1,0:T(8,128)(2,1)S(1)}, u32[]{:S(2)}, u32[]{:S(2)}) collective-permute-start(bf16[2,256,256]{2,1,0:T(8,128)(2,1)S(1)} %coupling.2.refs_0_), channel_id=1, source_target_pairs={{0,3},{1,0},{2,1},{3,2},{4,7},{5,4},{6,5},{7,6},{8,11},{9,8},{10,9... | collective-permute-start | bytes 786440 | tf_op jit(solution)/shard_map/ppermute | solution.py:350
  66.6 8.4 %collective-permute-start.14 = (bf16[2,256,256]{2,1,0:T(8,128)(2,1)S(1)}, bf16[2,256,256]{2,1,0:T(8,128)(2,1)S(1)}, u32[]{:S(2)}, u32[]{:S(2)}) collective-permute-start(bf16[2,256,256]{2,1,0:T(8,128)(2,1)S(1)} %coupling.3.refs_4_), channel_id=1, source_target_pairs={{0,1},{1,2},{2,3},{3,0},{4,5},{5,6},{6,7},{7,4},{8,9},{9,10},{10,1... | collective-permute-start | bytes 786440 | tf_op jit(solution)/shard_map/ppermute | solution.py:350
  66.8 20.9 %collective-permute-start.17 = (bf16[2,512,256]{2,1,0:T(8,128)(2,1)S(1)}, bf16[2,512,256]{2,1,0:T(8,128)(2,1)S(1)}, u32[]{:S(2)}, u32[]{:S(2)}) collective-permute-start(bf16[2,512,256]{2,1,0:T(8,128)(2,1)S(1)} %bitcast.34), channel_id=1, source_target_pairs={{0,4},{4,8},{8,12},{12,0},{1,5},{5,9},{9,13},{13,1},{2,6},{6,10},{... | collective-permute-start | bytes 1572872 | tf_op jit(solution)/shard_map/ppermute | solution.py:354
  72.5 8.3 %collective-permute-start.15 = (bf16[2,256,256]{2,1,0:T(8,128)(2,1)S(1)}, bf16[2,256,256]{2,1,0:T(8,128)(2,1)S(1)}, u32[]{:S(2)}, u32[]{:S(2)}) collective-permute-start(bf16[2,256,256]{2,1,0:T(8,128)(2,1)S(1)} %coupling.3.refs_4_), channel_id=1, source_target_pairs={{0,2},{1,3},{2,0},{3,1},{4,6},{5,7},{6,4},{7,5},{8,10},{9,11},{10,... | collective-permute-start | bytes 786440 | tf_op jit(solution)/shard_map/ppermute | solution.py:350
  75.0 12.7 %collective-permute-start.16 = (bf16[2,256,256]{2,1,0:T(8,128)(2,1)S(1)}, bf16[2,256,256]{2,1,0:T(8,128)(2,1)S(1)}, u32[]{:S(2)}, u32[]{:S(2)}) collective-permute-start(bf16[2,256,256]{2,1,0:T(8,128)(2,1)S(1)} %coupling.3.refs_4_), channel_id=1, source_target_pairs={{0,3},{1,0},{2,1},{3,2},{4,7},{5,4},{6,5},{7,6},{8,11},{9,8},{10,9... | collective-permute-start | bytes 786440 | tf_op jit(solution)/shard_map/ppermute | solution.py:350
  87.7 0.7 copy-start.8
  87.7 0.9 copy-start.7
  88.6 23.1 %copy-start.4 = (bf16[512,64]{0,1:T(8,128)(2,1)S(1)}, bf16[512,64]{0,1:T(8,128)(2,1)}, u32[]{:S(2)}) copy-start(bf16[512,64]{0,1:T(8,128)(2,1)} %param.15) | copy-start | bytes 196612
  88.6 35.4 %copy-start = (f32[256,2]{0,1:T(2,128)S(1)}, f32[256,2]{0,1:T(2,128)}, u32[]{:S(2)}) copy-start(f32[256,2]{0,1:T(2,128)} %param.11) | copy-start | bytes 6148
  101.3 29.8 %copy-start.2 = (bf16[2,512,512]{2,1,0:T(8,128)(2,1)S(1)}, bf16[2,512,512]{2,1,0:T(8,128)(2,1)}, u32[]{:S(2)}) copy-start(bf16[2,512,512]{2,1,0:T(8,128)(2,1)} %get-tuple-element.20) | copy-start | bytes 3145732
  101.3 22.7 %all-to-all-start = ((bf16[16,72,128]{2,1,0:T(8,128)(2,1)}), bf16[16,72,128]{2,1,0:T(8,128)(2,1)S(1)}, u32[]{:S(2)}, u32[]{:S(2)}) async-start(bf16[16,72,128]{2,1,0:T(8,128)(2,1)} %get-tuple-element.21), calls=%async_computation | async-start | bytes 589824 | tf_op jit(solution)/shard_map/all_to_all | solution.py:363
  124.9 14.7 %all-to-all-start.1 = ((bf16[16,64,128]{2,1,0:T(8,128)(2,1)}), bf16[16,64,128]{2,1,0:T(8,128)(2,1)S(1)}, u32[]{:S(2)}, u32[]{:S(2)}) async-start(bf16[16,64,128]{2,1,0:T(8,128)(2,1)} %pole_sum.1), calls=%async_computation.1 | async-start | bytes 524288 | tf_op jit(solution)/shard_map/all_to_all | solution.py:366
